TPU v7x, 32 devices: a whole 2x2x4 slice. The times are simulated.
32 devices in a mesh: shard: 4 (over x, core), seq: 8 (over z, y).
Axes of the slice: x: 2, y: 2, z: 4, core: 2. Of those that a mesh axis runs over, the one named last changes fastest.
Arguments:
- hidden: bfloat16 [16384, 1536], P(('shard', 'seq')), may hold values from -6 to 6
- cotangent: bfloat16 [16384, 1536], P(('shard', 'seq')), may hold values from -6 to 6
- seg_ids: int32 [16384], replicated, may hold values from 0 to 7, never falling along the last dimension, each value on 1 to 4096 neighbouring positions
- norm_gain: bfloat16 [1536], P('shard'), may hold values from 0.5 to 1.5
- in_weight: bfloat16 [1536, 6448], P('shard'), may hold values from -0.15625 to 0.15625
- conv_weight: bfloat16 [4, 3328], P(None, 'shard'), may hold values from -3 to 3
- conv_bias: bfloat16 [3328], P('shard'), may hold values from -3 to 3
- dt_bias: bfloat16 [48], replicated, may hold values from -8 to -2
- a_log: bfloat16 [48], replicated, may hold values from 0 to 2.6875
- d_skip: bfloat16 [48], replicated, may hold values from 0.5 to 1.5
- out_gain: bfloat16 [3072], P('shard'), may hold values from 0.5 to 1.5
- out_weight: bfloat16 [3072, 1536], P('shard'), may hold values from -0.109375 to 0.109375
Outputs:
- block_out: bfloat16 [16384, 1536], P(('shard', 'seq'))
- grad_hidden: float32 [16384, 1536], P(('shard', 'seq'))
- grad_norm_gain: float32 [1536], P(('shard', 'seq'))
- grad_in_weight: float32 [1536, 6448], P(('shard', 'seq'))
- grad_conv_weight: float32 [4, 3328], P(None, ('shard', 'seq'))
- grad_conv_bias: float32 [3328], P(('shard', 'seq'))
- grad_dt_bias: float32 [48], replicated
- grad_a_log: float32 [48], replicated
- grad_d_skip: float32 [48], replicated
- grad_out_gain: float32 [3072], P(('shard', 'seq'))
- grad_out_weight: float32 [3072, 1536], P(('shard', 'seq'))
Inputs may be any that keep to these rules, and one draw needn't show every extreme that they name: seg_ids never falls along the tokens; every value occurs; each document holds 1 to 4096 tokens and one holds exactly 4096.
All inputs are finite; a program needn't handle non-finite values.
Results may differ from a plain program's by a relative error of at most 0.02.
Values may be sent and summed in bfloat16 or wider, within the bound.
No kernel may reach another device: no remote copies, remote signals or barrier semaphores. Data moves between devices by JAX's collectives and lax.ppermute only.
A program may use at most 384 MiB of HBM per device.

v0:
```python
import jax
import jax.numpy as jnp
from jax import lax
from jax.sharding import PartitionSpec as P

HEAD_DIM = 64
CONV = 4
BLOCK = 256


HIGH = lax.Precision.HIGHEST
EPS = 1e-05


def from_behind(value, axis, steps):
    count = lax.axis_size(axis)
    initial, last = (max(0, -steps), min(count, count - steps))
    return lax.ppermute(value, axis, [(source, source + steps) for source in range(initial, last)])


def prefix(array, axis, join, neutral, backward):
    count = lax.axis_size(axis)
    place = lax.axis_index(axis)
    ahead = count - 1 - place if backward else place
    gathered = jax.tree.map(
        lambda a, kind: lax.all_gather(a.astype(kind), axis), array, (jnp.bfloat16, jnp.bfloat16)
    )
    state = jax.tree.map(lambda a, e: jnp.zeros_like(a) + jnp.asarray(e, a.dtype), array, neutral)

    def one(step, state):
        source = count - 1 - step if backward else step
        return join(
            state,
            jax.tree.map(
                lambda a, own: lax.dynamic_index_in_dim(a, source, 0, False).astype(own.dtype),
                gathered,
                array,
            ),
        )

    return lax.fori_loop(0, ahead, one, state)


def token_norm(values, gain):
    scale = lax.rsqrt(jnp.mean(values * values, axis=1, keepdims=True) + EPS)
    return values * scale * gain[None, :]


def gate_norm(mixer_out, gate_z, gain):
    gated = mixer_out * jax.nn.silu(gate_z)
    scale = lax.rsqrt(jnp.mean(gated * gated, axis=1, keepdims=True) + EPS)
    return gated * scale * gain[None, :]


def chain_pairs(earlier, later):
    return (earlier[0] * later[0], later[0][None, :] * earlier[1] + later[1])


def causal_conv(extended, seg_ext, weight, bias, length):
    seg_here = seg_ext[CONV - 1 :]
    summed = jnp.zeros((length, extended.shape[1]), jnp.float32) + bias[None, :]
    for tap in range(CONV):
        same_doc = (seg_ext[tap : tap + length] == seg_here).astype(jnp.float32)
        summed = summed + weight[tap][None, :] * extended[tap : tap + length] * same_doc[:, None]
    return jax.nn.silu(summed)


def make_mixer(seg_ext, head_lo, channel_lo):

    def mixer(
        x_raw,
        bc_raw,
        dt_raw,
        tail_x,
        tail_bc,
        conv_x,
        bias_x,
        conv_bc,
        bias_bc,
        dt_bias,
        a_log,
        d_skip,
    ):
        length = x_raw.shape[0]
        chan_width = x_raw.shape[1]
        n_state = bc_raw.shape[1] // 2
        local_heads = (chan_width - 1) // HEAD_DIM + 2
        seg_here = seg_ext[CONV - 1 :]
        x_conv = causal_conv(jnp.concatenate([tail_x, x_raw], 0), seg_ext, conv_x, bias_x, length)
        bc_conv = causal_conv(
            jnp.concatenate([tail_bc, bc_raw], 0), seg_ext, conv_bc, bias_bc, length
        )
        b_mat = bc_conv[:, :n_state]
        c_mat = bc_conv[:, n_state:]
        step_size = jax.nn.softplus(dt_raw + dt_bias[None, :])
        log_decay = -step_size * jnp.exp(a_log)[None, :]
        padding = jnp.zeros((length, local_heads - 1), jnp.float32)
        step_local = lax.dynamic_slice_in_dim(
            jnp.concatenate([step_size, padding], 1), head_lo, local_heads, 1
        )
        decay_local = lax.dynamic_slice_in_dim(
            jnp.concatenate([log_decay, padding], 1), head_lo, local_heads, 1
        )
        skip_local = lax.dynamic_slice_in_dim(
            jnp.concatenate([d_skip, jnp.zeros((local_heads - 1,), jnp.float32)]),
            head_lo,
            local_heads,
        )
        owner = (channel_lo + jnp.arange(chan_width, dtype=jnp.int32)) // HEAD_DIM - head_lo
        select = (owner[None, :] == jnp.arange(local_heads, dtype=jnp.int32)[:, None]).astype(
            jnp.float32
        )
        x_step = x_conv * jnp.dot(step_local, select, precision=HIGH)
        n_blocks = length // BLOCK
        seg_before = seg_ext[CONV - 2 : CONV - 2 + length].reshape(n_blocks, BLOCK)[:, 0]

        def block_step(state, inputs):
            x_block, b_block, c_block, decay_block, seg_block, seg_prior = inputs
            cum_decay = jnp.cumsum(decay_block, axis=0)
            positions = jnp.arange(BLOCK, dtype=jnp.int32)
            same_doc = (seg_block[:, None] == seg_block[None, :]) & (
                positions[:, None] >= positions[None, :]
            )
            log_gap = cum_decay.T[:, :, None] - cum_decay.T[:, None, :]
            weights = jnp.exp(jnp.where(same_doc[None], log_gap, -jnp.inf))
            scores = jnp.dot(c_block, b_block.T, precision=HIGH)
            per_head = jnp.einsum("jts,sc->jtc", weights * scores[None], x_block, precision=HIGH)
            inside = jnp.sum(per_head * select[:, None, :], axis=0)
            entering = jnp.exp(cum_decay) * (seg_block == seg_prior).astype(jnp.float32)[:, None]
            enter_block = jnp.dot(entering, select, precision=HIGH)
            from_state = jnp.dot(c_block, state, precision=HIGH) * enter_block
            keep_tail = jnp.exp(
                jnp.where(
                    (seg_block == seg_block[BLOCK - 1])[:, None],
                    cum_decay[BLOCK - 1][None, :] - cum_decay,
                    -jnp.inf,
                )
            )
            tail_channels = jnp.dot(keep_tail, select, precision=HIGH)
            new_state = enter_block[BLOCK - 1][None, :] * state + jnp.dot(
                b_block.T, x_block * tail_channels, precision=HIGH
            )
            return (new_state, inside + from_state)

        inputs = (
            x_step.reshape(n_blocks, BLOCK, chan_width),
            b_mat.reshape(n_blocks, BLOCK, n_state),
            c_mat.reshape(n_blocks, BLOCK, n_state),
            decay_local.reshape(n_blocks, BLOCK, local_heads),
            seg_here.reshape(n_blocks, BLOCK),
            seg_before,
        )
        final_state, block_out = lax.scan(
            jax.checkpoint(block_step), jnp.zeros((n_state, chan_width), jnp.float32), inputs
        )
        skip_channels = jnp.dot(skip_local, select, precision=HIGH)
        mixer_out = block_out.reshape(length, chan_width) + x_conv * skip_channels[None, :]
        part_cum = jnp.cumsum(decay_local, axis=0)
        carried_in = (seg_here == seg_ext[CONV - 2]).astype(jnp.float32)
        enter = jnp.dot(jnp.exp(part_cum) * carried_in[:, None], select, precision=HIGH)
        return (mixer_out, final_state, enter, c_mat)

    return mixer


def on_device(
    hidden,
    cotangent,
    seg_ids,
    norm_gain,
    in_weight,
    conv_weight,
    conv_bias,
    dt_bias,
    a_log,
    d_skip,
    out_gain,
    out_weight,
):
    gains_in, w_in, w_conv, b_conv, gains_out, w_out = (
        lax.all_gather(norm_gain, "shard", axis=0, tiled=True),
        lax.all_gather(in_weight, "shard", axis=0, tiled=True),
        lax.all_gather(conv_weight, "shard", axis=1, tiled=True),
        lax.all_gather(conv_bias, "shard", axis=0, tiled=True),
        lax.all_gather(out_gain, "shard", axis=0, tiled=True),
        lax.all_gather(out_weight, "shard", axis=0, tiled=True),
    )
    seq_count = lax.axis_size("seq")
    shard_count = lax.axis_size("shard")
    seq_rank = lax.axis_index("seq")
    shard_rank = lax.axis_index("shard")
    tok_len = hidden.shape[0]
    inner_width = w_out.shape[0]
    n_state = (w_conv.shape[1] - inner_width) // 2
    chan_width = inner_width // seq_count
    part_len = tok_len * seq_count
    hidden_f = hidden.astype(jnp.float32)
    gains_f = gains_in.astype(jnp.float32)
    normed_in = token_norm(hidden_f, gains_f).astype(jnp.bfloat16)
    projected = jnp.dot(normed_in, w_in, preferred_element_type=jnp.float32).astype(jnp.bfloat16)
    gate_z = projected[:, :inner_width]
    x_tokens = projected[:, inner_width : 2 * inner_width]
    shared_tokens = projected[:, 2 * inner_width :]
    x_heads = lax.all_to_all(x_tokens, "seq", split_axis=1, concat_axis=0, tiled=True)
    shared = lax.all_gather(shared_tokens, "seq", axis=0, tiled=True)
    bc_heads = shared[:, : 2 * n_state]
    tail_x, tail_bc = from_behind(
        (x_heads[part_len - CONV + 1 :], bc_heads[part_len - CONV + 1 :]), "shard", 1
    )
    lead = jnp.full((CONV - 1,), -1, jnp.int32)
    seg_all = jnp.concatenate([lead, seg_ids])
    seg_ext = lax.dynamic_slice_in_dim(seg_all, shard_rank * part_len, part_len + CONV - 1)
    channel_lo = seq_rank * chan_width
    head_lo = channel_lo // HEAD_DIM
    conv_f = w_conv.astype(jnp.float32)
    bias_f = b_conv.astype(jnp.float32)
    primals = (
        x_heads.astype(jnp.float32),
        bc_heads.astype(jnp.float32),
        shared[:, 2 * n_state :].astype(jnp.float32),
        tail_x.astype(jnp.float32),
        tail_bc.astype(jnp.float32),
        lax.dynamic_slice_in_dim(conv_f, channel_lo, chan_width, 1),
        lax.dynamic_slice_in_dim(bias_f, channel_lo, chan_width, 0),
        conv_f[:, inner_width:],
        bias_f[inner_width:],
        dt_bias.astype(jnp.float32),
        a_log.astype(jnp.float32),
        d_skip.astype(jnp.float32),
    )
    mixer = make_mixer(seg_ext, head_lo, channel_lo)
    mixer_outs, mixer_pull = jax.vjp(mixer, *primals)
    local_out, state_local, enter, c_mat = mixer_outs
    identity = (jnp.ones((chan_width,), jnp.float32), jnp.zeros((n_state, chan_width), jnp.float32))
    state_in = prefix((enter[part_len - 1], state_local), "shard", chain_pairs, identity, False)[1]
    carried = jnp.dot(c_mat, state_in, precision=HIGH)
    mixer_full = local_out + carried * enter
    mixer_tokens = lax.all_to_all(
        mixer_full.astype(jnp.bfloat16), "seq", split_axis=0, concat_axis=1, tiled=True
    )
    normed_f, gate_pull = jax.vjp(
        gate_norm,
        mixer_tokens.astype(jnp.float32),
        gate_z.astype(jnp.float32),
        gains_out.astype(jnp.float32),
    )
    normed_out = normed_f.astype(jnp.bfloat16)
    branch = jnp.dot(normed_out, w_out, preferred_element_type=jnp.float32)
    block_out = (hidden_f + branch).astype(jnp.bfloat16)
    grad_out_w = lax.dot_general(
        normed_out, cotangent, (((0,), (0,)), ((), ())), preferred_element_type=jnp.float32
    )
    d_normed = lax.dot_general(
        cotangent, w_out, (((1,), (1,)), ((), ())), preferred_element_type=jnp.float32
    )
    d_mixer, d_gate_z, d_gain_out = gate_pull(d_normed)
    d_heads = lax.all_to_all(
        d_mixer.astype(jnp.bfloat16), "seq", split_axis=1, concat_axis=0, tiled=True
    ).astype(jnp.float32)
    weighted = d_heads * enter
    d_state_local = jnp.dot(c_mat.T, weighted, precision=HIGH)
    d_state_out = prefix(
        (enter[part_len - 1], d_state_local), "shard", chain_pairs, identity, True
    )[1]
    d_enter = d_heads * carried
    d_enter = d_enter.at[part_len - 1].add(jnp.sum(d_state_out * state_in, axis=0))
    d_c_mat = jnp.dot(weighted, state_in.T, precision=HIGH)
    mixer_grads = mixer_pull((d_heads, d_state_out, d_enter, d_c_mat))
    (
        d_x_raw,
        d_bc_raw,
        d_dt_raw,
        d_tail_x,
        d_tail_bc,
        d_conv_x,
        d_bias_x,
        d_conv_bc,
        d_bias_bc,
        d_dt_bias,
        d_a_log,
        d_d_skip,
    ) = mixer_grads
    back_x, back_bc = from_behind((d_tail_x, d_tail_bc), "shard", -1)
    d_x_raw = d_x_raw.at[part_len - CONV + 1 :].add(back_x)
    d_bc_raw = d_bc_raw.at[part_len - CONV + 1 :].add(back_bc)
    d_x_tokens = lax.all_to_all(
        d_x_raw.astype(jnp.bfloat16), "seq", split_axis=0, concat_axis=1, tiled=True
    )
    d_shared = lax.psum_scatter(
        jnp.concatenate([d_bc_raw, d_dt_raw], 1).astype(jnp.bfloat16),
        "seq",
        scatter_dimension=0,
        tiled=True,
    ).astype(jnp.float32)
    d_projected = jnp.concatenate([d_gate_z, d_x_tokens.astype(jnp.float32), d_shared], 1).astype(
        jnp.bfloat16
    )
    grad_in_w = lax.dot_general(
        normed_in, d_projected, (((0,), (0,)), ((), ())), preferred_element_type=jnp.float32
    )
    d_normed_in = lax.dot_general(
        d_projected, w_in, (((1,), (1,)), ((), ())), preferred_element_type=jnp.float32
    )
    _, norm_pull = jax.vjp(token_norm, hidden_f, gains_f)
    d_hidden_norm, d_gain_in = norm_pull(d_normed_in)
    grad_hidden = cotangent.astype(jnp.float32) + d_hidden_norm
    conv_grad = jnp.zeros(w_conv.shape, jnp.float32)
    conv_grad = lax.dynamic_update_slice(conv_grad, d_conv_x, (jnp.int32(0), channel_lo))
    conv_grad = conv_grad.at[:, inner_width:].set(d_conv_bc)
    bias_grad = jnp.zeros(b_conv.shape, jnp.float32)
    bias_grad = lax.dynamic_update_slice(bias_grad, d_bias_x, (channel_lo,))
    bias_grad = bias_grad.at[inner_width:].set(d_bias_bc)
    head_grads = jnp.concatenate([d_dt_bias, d_a_log, d_d_skip])
    n_heads = dt_bias.shape[0]
    head_rows = jnp.broadcast_to(
        head_grads[None, :], (shard_count * seq_count, head_grads.shape[0])
    )
    partial_sums = (
        lax.psum_scatter(
            d_gain_in.astype(jnp.bfloat16), "shard", scatter_dimension=0, tiled=True
        ).astype(jnp.float32),
        lax.psum_scatter(
            grad_in_w.astype(jnp.bfloat16), "shard", scatter_dimension=0, tiled=True
        ).astype(jnp.float32),
        lax.psum_scatter(
            conv_grad.astype(jnp.bfloat16), "shard", scatter_dimension=1, tiled=True
        ).astype(jnp.float32),
        lax.psum_scatter(
            bias_grad.astype(jnp.bfloat16), "shard", scatter_dimension=0, tiled=True
        ).astype(jnp.float32),
        lax.psum_scatter(
            d_gain_out.astype(jnp.bfloat16), "shard", scatter_dimension=0, tiled=True
        ).astype(jnp.float32),
        lax.psum_scatter(
            grad_out_w.astype(jnp.bfloat16), "shard", scatter_dimension=0, tiled=True
        ).astype(jnp.float32),
        lax.psum_scatter(
            head_rows.astype(jnp.bfloat16), "shard", scatter_dimension=0, tiled=True
        ).astype(jnp.float32),
    )
    reduced = (
        lax.psum_scatter(
            partial_sums[0].astype(jnp.bfloat16), "seq", scatter_dimension=0, tiled=True
        ).astype(jnp.float32),
        lax.psum_scatter(
            partial_sums[1].astype(jnp.bfloat16), "seq", scatter_dimension=0, tiled=True
        ).astype(jnp.float32),
        lax.psum_scatter(
            partial_sums[2].astype(jnp.bfloat16), "seq", scatter_dimension=1, tiled=True
        ).astype(jnp.float32),
        lax.psum_scatter(
            partial_sums[3].astype(jnp.bfloat16), "seq", scatter_dimension=0, tiled=True
        ).astype(jnp.float32),
        lax.psum_scatter(
            partial_sums[4].astype(jnp.bfloat16), "seq", scatter_dimension=0, tiled=True
        ).astype(jnp.float32),
        lax.psum_scatter(
            partial_sums[5].astype(jnp.bfloat16), "seq", scatter_dimension=0, tiled=True
        ).astype(jnp.float32),
        lax.psum_scatter(
            partial_sums[6].astype(jnp.bfloat16), "seq", scatter_dimension=0, tiled=True
        ).astype(jnp.float32),
    )
    head_total = reduced[6][0]
    return (
        block_out,
        grad_hidden,
        reduced[0],
        reduced[1],
        reduced[2],
        reduced[3],
        head_total[:n_heads],
        head_total[n_heads : 2 * n_heads],
        head_total[2 * n_heads :],
        reduced[4],
        reduced[5],
    )


def solution(mesh):
    return jax.shard_map(
        on_device,
        mesh=mesh,
        in_specs=(
            P(("shard", "seq"), None),
            P(("shard", "seq"), None),
            P(),
            P("shard"),
            P("shard", None),
            P(None, "shard"),
            P("shard"),
            P(),
            P(),
            P(),
            P("shard"),
            P("shard", None),
        ),
        out_specs=(
            P(("shard", "seq"), None),
            P(("shard", "seq"), None),
            P(("shard", "seq")),
            P(("shard", "seq"), None),
            P(None, ("shard", "seq")),
            P(("shard", "seq")),
            P(),
            P(),
            P(),
            P(("shard", "seq")),
            P(("shard", "seq"), None),
        ),
        check_vma=False,
    )
```

profile of v0, /device:TPU:0, one launch (start us, length us, event | category | flops | bytes accessed | tf_op | source)
XLA Modules:
  0.0 2106.3 jit_solution(14078692126944660812)
XLA Ops:
  8.0 6.1 all-gather.2
  15.2 122.0 %all-gather.10.cloned.1.call-done = bf16[1536,6448]{0,1:T(8,128)(2,1)} async-done(((bf16[384,6448]{0,1:T(8,128)(2,1)}), bf16[1536,6448]{0,1:T(8,128)(2,1)}) %all-gather.10.cloned.1.call-update) | async-done | bytes 19808272 | tf_op jit(solution)/shard_map/all_gather | solution.py:182
  137.2 15.2 convolution_convert_fusion.2
  159.5 5.2 all-gather.3
  166.3 6.5 all-reduce.24
  179.9 5.3 all-to-all-start
  185.2 47.3 %all-gather.12.cloned.1.call-done = bf16[4096,304]{0,1:T(8,128)(2,1)} async-done(((bf16[512,304]{0,1:T(8,128)(2,1)}), bf16[4096,304]{0,1:T(8,128)(2,1)}) %all-gather.12.cloned.1.call-update) | async-done | bytes 2490384 | tf_op jit(solution)/shard_map/all_gather | solution.py:205
  250.2 5.2 all-gather.4
  256.3 5.0 fusion.151
  270.5 4.9 all-to-all-done
  286.1 19.9 fusion.198
  309.5 309.7 %while.75 = (s32[]{:T(128)}, f32[128,384]{1,0:T(8,128)S(1)}, f32[16,256,384]{2,1,0:T(8,128)}, f32[16,128,384]{2,1,0:T(8,128)}, f32[16,256,7]{1,2,0:T(8,128)}, /*...) while((s32[]{:T(128)}, f32[128,384]{1,0:T(8,128)S(1)}, ...), condition=%wide.region_5.6_spmd.clone.clone.clone, body=%wide.region_1.5_spmd.clone.clone.clone.sunk | while | flops 2536740608 | bytes 5860804 | solution.py:153
  619.2 6.9 all-gather
  626.6 12.8 fusion.144
  642.3 12.3 all-to-all-start.1
  654.6 5.2 all-gather.5
  659.8 66.1 %all-to-all-done.1 = bf16[8,512,384]{1,2,0:T(8,128)(2,1)S(1)} async-done(((bf16[8,512,384]{1,2,0:T(8,128)(2,1)}), bf16[8,512,384]{1,2,0:T(8,128)(2,1)S(1)}, u32[]{:S(2)}, u32[]{:S(2)}) %all-to-all-start.1) | async-done | bytes 3145760 | tf_op jit(solution)/shard_map/all_to_all | solution.py:238
  725.9 5.3 multiply_reduce_fusion.9
  731.9 12.6 multiply_reduce_fusion.3
  744.6 7.7 fusion.138
  756.1 70.7 %all-to-all-done.2 = bf16[512,8,384]{0,2,1:T(8,128)(2,1)S(1)} async-done(((bf16[512,8,384]{0,2,1:T(8,128)(2,1)}), bf16[512,8,384]{0,2,1:T(8,128)(2,1)S(1)}, u32[]{:S(2)}, u32[]{:S(2)}) %all-to-all-start.2) | async-done | bytes 3145760 | tf_op jit(solution)/shard_map/all_to_all | solution.py:257
  830.3 6.6 copy.137
  836.9 5.4 bitcast_multiply_fusion.4
  847.0 6.1 all-gather.1
  860.6 557.6 %while.74 = (s32[]{:T(128)}, f32[128,384]{1,0:T(8,128)S(1)}, f32[16,256,384]{2,1,0:T(8,128)}, f32[16,256,128]{2,1,0:T(8,128)}, f32[16,256,128]{2,1,0:T(8,128)}, ...) while((s32[]{:T(128)}, f32[128,384]{1,0:T(8,128)S(1)}, ...), condition=%wide.region_24.25_spmd.clone, body=%wide.region_14.24_spmd.clone.sunk | while | flops 5326403584 | bytes 15732097 | solution.py:153
  886.5 8.8 reduce-window.100
  921.3 8.8 reduce-window.100
  956.0 8.8 reduce-window.100
  990.8 8.8 reduce-window.100
  1025.6 8.8 reduce-window.100
  1060.4 8.8 reduce-window.100
  1095.2 8.8 reduce-window.100
  1130.0 8.8 reduce-window.100
  1164.8 8.8 reduce-window.100
  1199.7 8.8 reduce-window.100
  1234.5 8.8 reduce-window.100
  1269.3 8.8 reduce-window.100
  1304.2 8.8 reduce-window.100
  1339.0 8.8 reduce-window.100
  1373.8 8.8 reduce-window.100
  1408.6 8.8 reduce-window.100
  1424.2 10.2 convolution_add_fusion.4
  1434.5 6.2 multiply_reduce_fusion.12
  1440.7 5.1 broadcast_multiply_fusion.1
  1445.8 11.0 pad_add_fusion.1
  1458.8 23.2 %multiply_reduce_fusion.6 = (f32[384]{0:T(512)}, f32[384]{0:T(512)}, f32[384]{0:T(512)}, bf16[384]{0:T(512)(128)(2,1)}, f32[384]{0:T(512)}, /*index=5*/f32[4096,...) fusion(f32[4096,384]{1,0:T(8,128)} %bitcast_convert_fusion, ...), kind=kLoop, calls=%fused_computation.197 | loop fusion | flops 51902208 | bytes 59832576 | tf_op jit(solution)/shard_map/transpose(jvp())/reduce_sum | solution.py:64
  1486.1 5.7 fusion.161
  1491.8 8.7 reduce-window.80
  1501.1 5.8 fusion.175
  1521.1 10.4 convolution_convert_fusion.1
  1532.2 5.8 broadcast_multiply_fusion
  1548.5 4.7 copy.141
  1557.8 83.6 %reduce-scatter.15.cloned.1.call-done = bf16[512,304]{0,1:T(8,128)(2,1)} async-done(((bf16[4096,304]{0,1:T(8,128)(2,1)}), bf16[512,304]{0,1:T(8,128)(2,1)}) %reduce-scatter.15.cloned.1.call-update) | async-done | bytes 311312 | tf_op jit(solution)/shard_map/reduce_scatter | solution.py:289
  1641.4 17.4 convolution_convert_fusion
  1658.9 25.0 %copy.152 = bf16[1536,6448]{1,0:T(8,128)(2,1)} copy(bf16[1536,6448]{0,1:T(8,128)(2,1)} %convolution_convert_fusion) | data formatting | bytes 39616512
  1687.2 33.3 %reduce-scatter.19.cloned.1.call-done = bf16[768,1536]{1,0:T(8,128)(2,1)} async-done(((bf16[3072,1536]{1,0:T(8,128)(2,1)}), bf16[768,1536]{1,0:T(8,128)(2,1)}) %reduce-scatter.19.cloned.1.call-update) | async-done | bytes 2359312 | tf_op jit(solution)/shard_map/reduce_scatter | solution.py:334
  1720.5 149.7 %reduce-scatter.23.cloned.1.call-done = bf16[384,6448]{1,0:T(8,128)(2,1)} async-done(((bf16[1536,6448]{1,0:T(8,128)(2,1)}), bf16[384,6448]{1,0:T(8,128)(2,1)}) %reduce-scatter.23.cloned.1.call-update) | async-done | bytes 4952080
  1874.8 11.1 fusion.159
  1886.2 10.9 reduce-scatter.27.cloned.1.call-done
  1898.2 20.3 fusion.155
  1918.4 10.2 all-reduce.34
  1928.9 37.7 %all-reduce.33 = (bf16[384]{0:T(512)(128)(2,1)S(1)}, bf16[4,832]{1,0:T(4,128)(2,1)S(1)}, bf16[832]{0:T(1024)(128)(2,1)S(1)}, bf16[8,144]{1,0:T(8,128)(2,1)S(1)}, bf16[768]{0:T(1024)(128)(2,1)S(1)}) all-reduce(bf16[384]{0:T(512)(128)(2,1)S(1)} %dynamic-slice.41, ...), channel_id=6, replica_groups=mesh['shard'=4,'seq'=8] {'seq'}, use_global_device_ids=true, to_apply=%region_32.33.clone | all-reduce | flops 6464 | bytes 25856
  1974.7 17.7 reduce-scatter.21.cloned.1.call-done
  1994.2 100.6 %reduce-scatter.25.cloned.1.call-done = bf16[48,6448]{1,0:T(8,128)(2,1)} async-done(((bf16[384,6448]{1,0:T(8,128)(2,1)}), bf16[48,6448]{1,0:T(8,128)(2,1)}) %reduce-scatter.25.cloned.1.call-update) | async-done | bytes 619024
  (1492 shorter events, 866.8 us)
Async XLA Ops:
  7.2 130.0 %all-gather.10.cloned.1.call-start = ((), (), s32[]{:S(2)}) async-start(), calls=%async_computation.11 | async-start | bytes 24760320 | tf_op jit(solution)/shard_map/all_gather | solution.py:182
  7.9 224.5 %all-gather.12.cloned.1.call-start = ((), (), s32[]{:S(2)}) async-start(), calls=%async_computation.12 | async-start | bytes 2801664 | tf_op jit(solution)/shard_map/all_gather | solution.py:205
  14.1 138.3 %copy-start.32 = (f32[1536]{0:T(1024)}, f32[1536]{0:T(1024)S(1)}, u32[]{:S(2)}) copy-start(f32[1536]{0:T(1024)S(1)} %reshape.690) | copy-start | bytes 18436
  15.1 137.3 %copy-start.56 = (f32[512]{0:T(512)}, f32[512]{0:T(512)S(1)}, u32[]{:S(2)}) copy-start(f32[512]{0:T(512)S(1)} %fusion.186) | copy-start | bytes 6148
  15.1 141.6 %copy-start.85 = (bf16[48]{0:T(256)(128)(2,1)S(1)}, bf16[48]{0:T(256)(128)(2,1)}, u32[]{:S(2)}) copy-start(bf16[48]{0:T(256)(128)(2,1)} %param.37) | copy-start | bytes 292
  15.1 141.6 %copy-start.87 = (bf16[48]{0:T(256)(128)(2,1)S(1)}, bf16[48]{0:T(256)(128)(2,1)}, u32[]{:S(2)}) copy-start(bf16[48]{0:T(256)(128)(2,1)} %param.38) | copy-start | bytes 292
  15.2 141.6 %copy-start.27 = (s32[16384]{0:T(1024)S(1)}, s32[16384]{0:T(1024)}, u32[]{:S(2)}) copy-start(s32[16384]{0:T(1024)} %param.32) | copy-start | bytes 196612
  15.2 144.3 %copy-start.61 = (bf16[4,832]{1,0:T(4,128)(2,1)S(1)}, bf16[4,832]{1,0:T(4,128)(2,1)}, u32[]{:S(2)}) copy-start(bf16[4,832]{1,0:T(4,128)(2,1)} %param.35) | copy-start | bytes 19972
  15.2 149.6 %copy-start.71 = (u32[32]{0:T(128)S(1)}, u32[32]{0:T(128)}, u32[]{:S(2)}) copy-start(u32[32]{0:T(128)} %constant.423) | copy-start | bytes 388
  15.2 150.9 %copy-start.72 = (bf16[832]{0:T(1024)(128)(2,1)S(1)}, bf16[832]{0:T(1024)(128)(2,1)}, u32[]{:S(2)}) copy-start(bf16[832]{0:T(1024)(128)(2,1)} %param.36) | copy-start | bytes 4996
  15.2 160.0 %copy-start.86 = (bf16[48]{0:T(256)(128)(2,1)S(1)}, bf16[48]{0:T(256)(128)(2,1)}, u32[]{:S(2)}) copy-start(bf16[48]{0:T(256)(128)(2,1)} %param.39) | copy-start | bytes 292
  155.9 576.0 %all-gather.14.cloned.1.call-start = ((), (), s32[]{:S(2)}) async-start(), calls=%async_computation.13 | async-start | bytes 11796480 | tf_op jit(solution)/shard_map/all_gather | solution.py:186
  156.7 80.1 %copy-start.75 = (f32[48]{0:T(128)}, f32[48]{0:T(128)S(1)}, u32[]{:S(2)}) copy-start(f32[48]{0:T(128)S(1)} %convert_element_type.243) | copy-start | bytes 580
  156.8 80.0 %copy-start.77 = (f32[48]{0:T(128)}, f32[48]{0:T(128)S(1)}, u32[]{:S(2)}) copy-start(f32[48]{0:T(128)S(1)} %convert_exponential_fusion) | copy-start | bytes 580
  158.1 87.2 %copy-start.30 = (f32[4096]{0:T(1024)}, f32[4096]{0:T(1024)S(1)}, u32[]{:S(2)}) copy-start(f32[4096]{0:T(1024)S(1)} %get-tuple-element.1069) | copy-start | bytes 49156
  174.6 81.7 %copy-start.36 = (f32[1,256]{1,0:T(1,128)}, f32[1,256]{1,0:T(1,128)S(1)}, u32[]{:S(2)}) copy-start(f32[1,256]{1,0:T(1,128)S(1)} %get-tuple-element.1109) | copy-start | bytes 3076
  174.6 81.7 %copy-start.38 = (f32[1,256]{1,0:T(1,128)}, f32[1,256]{1,0:T(1,128)S(1)}, u32[]{:S(2)}) copy-start(f32[1,256]{1,0:T(1,128)S(1)} %get-tuple-element.1110) | copy-start | bytes 3076
  174.6 81.7 %copy-start.40 = (f32[1,256]{1,0:T(1,128)}, f32[1,256]{1,0:T(1,128)S(1)}, u32[]{:S(2)}) copy-start(f32[1,256]{1,0:T(1,128)S(1)} %get-tuple-element.1111) | copy-start | bytes 3076
  179.9 95.5 %all-to-all-start = ((bf16[512,8,384]{0,2,1:T(8,128)(2,1)}), bf16[512,8,384]{0,2,1:T(8,128)(2,1)S(1)}, u32[]{:S(2)}, u32[]{:S(2)}) async-start(bf16[512,8,384]{0,2,1:T(8,128)(2,1)} %bitcast.462), calls=%async_computation | async-start | bytes 6291456 | tf_op jit(solution)/shard_map/all_to_all | solution.py:204
  234.0 21.4 %collective-permute-start = (bf16[3,256]{0,1:T(8,128)(2,1)}, bf16[3,256]{0,1:T(8,128)(2,1)}, u32[]{:S(2)}, u32[]{:S(2)}) collective-permute-start(bf16[3,256]{0,1:T(8,128)(2,1)} %slice.392), channel_id=1, source_target_pairs={{0,8},{8,16},{16,24},{1,9},{9,17},{17,25},{2,10},{10,18},{18,26},{... | collective-permute-start | bytes 4616 | tf_op jit(solution)/shard_map/ppermute | solution.py:18
  248.9 7.4 copy-start.42
  248.9 7.4 copy-start.64
  250.2 11.1 copy-start.3
  280.7 5.3 collective-permute-start.1
  309.5 317.1 %copy-start.69 = (f32[384]{0:T(512)S(1)}, f32[384]{0:T(512)}, u32[]{:S(2)}) copy-start(f32[384]{0:T(512)} %convolution_reduce_fusion) | copy-start | bytes 4612
  642.3 12.3 copy-start.73
  642.3 83.7 %all-to-all-start.1 = ((bf16[8,512,384]{1,2,0:T(8,128)(2,1)}), bf16[8,512,384]{1,2,0:T(8,128)(2,1)S(1)}, u32[]{:S(2)}, u32[]{:S(2)}) async-start(bf16[8,512,384]{1,2,0:T(8,128)(2,1)} %copy.135), calls=%async_computation.1 | async-start | bytes 6291456 | tf_op jit(solution)/shard_map/all_to_all | solution.py:238
  731.9 12.7 slice-start.2
  731.9 12.7 slice-start.3
  731.9 12.7 copy-start.59
  752.2 74.6 %all-to-all-start.2 = ((bf16[512,8,384]{0,2,1:T(8,128)(2,1)}), bf16[512,8,384]{0,2,1:T(8,128)(2,1)S(1)}, u32[]{:S(2)}, u32[]{:S(2)}) async-start(bf16[512,8,384]{0,2,1:T(8,128)(2,1)} %bitcast.464), calls=%async_computation.2 | async-start | bytes 6291456 | tf_op jit(solution)/shard_map/all_to_all | solution.py:257
  755.9 885.5 %reduce-scatter.15.cloned.1.call-start = ((), (), s32[]{:S(2)}) async-start(), calls=%async_computation.14 | async-start | bytes 2801664 | tf_op jit(solution)/shard_map/reduce_scatter | solution.py:289
  1421.1 13.3 copy-start.15
  1424.2 10.2 copy-start.4
  1424.2 10.2 copy-start.11
  1424.2 10.2 copy-start.18
  1445.8 11.0 copy-start
  1445.8 13.0 slice-start
  1445.8 13.0 slice-start.1
  1458.8 25.9 %copy-start.58 = (f32[384]{0:T(512)S(1)}, f32[384]{0:T(512)}, u32[]{:S(2)}) copy-start(f32[384]{0:T(512)} %multiply_reduce_fusion.15) | copy-start | bytes 4612
  1458.8 27.3 %copy-start.25 = (f32[1,7,32,128]{3,2,1,0:T(8,128)S(1)}, f32[1,7,32,128]{3,2,1,0:T(8,128)}, u32[]{:S(2)}) copy-start(f32[1,7,32,128]{3,2,1,0:T(8,128)} %copy-done.24) | copy-start | bytes 344068
  1458.8 27.3 %copy-start.31 = (f32[4096]{0:T(1024)S(1)}, f32[4096]{0:T(1024)}, u32[]{:S(2)}) copy-start(f32[4096]{0:T(1024)} %copy-done.30) | copy-start | bytes 49156
  1491.8 16.4 copy-start.29
  1501.1 11.0 copy-start.76
  1501.1 11.0 copy-start.78
  1501.1 13.9 copy-start.16
  1506.9 10.3 collective-permute-start.3
  1521.1 199.4 %reduce-scatter.19.cloned.1.call-start = ((), (), s32[]{:S(2)}) async-start(), calls=%async_computation.16 | async-start | bytes 11796480 | tf_op jit(solution)/shard_map/reduce_scatter | solution.py:334
  1538.0 9.2 collective-permute-start.2
  1553.2 88.3 %copy-start.22 = (bf16[512,1536]{1,0:T(8,128)(2,1)S(1)}, bf16[512,1536]{1,0:T(8,128)(2,1)}, u32[]{:S(2)}) copy-start(bf16[512,1536]{1,0:T(8,128)(2,1)} %param.30) | copy-start | bytes 4718596
  1553.2 88.3 %copy-start.33 = (f32[1536]{0:T(1024)S(1)}, f32[1536]{0:T(1024)}, u32[]{:S(2)}) copy-start(f32[1536]{0:T(1024)} %copy-done.32) | copy-start | bytes 18436
  1553.2 88.3 %copy-start.57 = (f32[512]{0:T(512)S(1)}, f32[512]{0:T(512)}, u32[]{:S(2)}) copy-start(f32[512]{0:T(512)} %copy-done.56) | copy-start | bytes 6148
  1553.2 88.3 %all-to-all-start.3 = ((bf16[8,512,384]{1,2,0:T(8,128)(2,1)}), bf16[8,512,384]{1,2,0:T(8,128)(2,1)}, u32[]{:S(2)}, u32[]{:S(2)}) async-start(bf16[8,512,384]{1,2,0:T(8,128)(2,1)} %copy.141), calls=%async_computation.3 | async-start | bytes 6291456 | tf_op jit(solution)/shard_map/all_to_all | solution.py:286
  1557.8 312.5 %reduce-scatter.23.cloned.1.call-start = ((), (), s32[]{:S(2)}) async-start(), calls=%async_computation.18 | async-start | bytes 25067520
  1684.0 213.1 %reduce-scatter.27.cloned.1.call-start = ((), (), s32[]{:S(2)}) async-start(), calls=%async_computation.20 | async-start | bytes 1064960
  1685.9 186.3 %copy-start.89 = (u32[32]{0:T(128)S(1)}, u32[32]{0:T(128)}, u32[]{:S(2)}) copy-start(u32[32]{0:T(128)} %constant.433) | copy-start | bytes 388
  1686.1 242.8 %reduce-scatter.17.cloned.1.call-start = ((), (), s32[]{:S(2)}) async-start(), calls=%async_computation.15 | async-start | bytes 20480 | tf_op jit(solution)/shard_map/reduce_scatter | solution.py:337
  1687.1 305.3 %reduce-scatter.21.cloned.1.call-start = ((), (), s32[]{:S(2)}) async-start(), calls=%async_computation.17 | async-start | bytes 2654208 | tf_op jit(solution)/shard_map/reduce_scatter | solution.py:357
  1720.5 374.4 %reduce-scatter.25.cloned.1.call-start = ((), (), s32[]{:S(2)}) async-start(), calls=%async_computation.19 | async-start | bytes 5640192
  1874.8 11.2 copy-start.63
  1874.8 11.4 copy-start.81
  1898.2 20.3 copy-start.62
  1898.2 72.1 %copy-start.35 = (f32[512]{0:T(512)S(1)}, f32[512]{0:T(512)}, u32[]{:S(2)}) copy-start(f32[512]{0:T(512)} %copy-done.34) | copy-start | bytes 6148
  1898.2 72.1 %copy-start.23 = (bf16[512,1536]{1,0:T(8,128)(2,1)S(1)}, bf16[512,1536]{1,0:T(8,128)(2,1)}, u32[]{:S(2)}) copy-start(bf16[512,1536]{1,0:T(8,128)(2,1)} %param.31) | copy-start | bytes 4718596
  (48 other events, 153.2 us)
Sparse Core Ops, SparseCore 0:
  9.6 127.5 all-gather.9
  156.0 76.4 all-gather.11
  234.0 75.5 all-gather.13
  1521.2 120.1 reduce-scatter.14
  1644.0 76.3 reduce-scatter.18
  1723.1 147.1 reduce-scatter.22
  1873.4 23.6 reduce-scatter.26
  1900.2 19.3 reduce-scatter.16
  1923.1 69.2 reduce-scatter.20
  1995.9 98.9 reduce-scatter.24
where the time goes:
time: 2120 us; the launch traced here: 2110 us
  waiting for transfers between devices  708 us (33%)
  matrix products  579 us (27%)
  other arithmetic  393 us (19%)
  local copies, waits for them, and re-layouts  278 us (13%)
  blocking collectives  89 us (4%)
  starting transfers between devices  33.7 us (2%)
    unnamed x13, waiting for transfers between devices  263 us
    another operation x102, other arithmetic  231 us
    dot_general x48, matrix products, block_step(): jnp.einsum('jts,sc->jtc', weights * scores[None], x_block, precision=HIGH)  198 us
    all_gather x1, waiting for transfers between devices, on_device(): lax.all_gather(in_weight, 'shard', axis=0, tiled=True)  122 us
    reduce_scatter x1, waiting for transfers between devices, on_device(): lax.psum_scatter(jnp.concatenate([d_bc_raw, d_dt_raw], 1).astype(jnp.bflo...  83.6 us
    all_to_all x1, waiting for transfers between devices, on_device(): lax.all_to_all(d_mixer.astype(jnp.bfloat16), 'seq', split_axis=1, concat_...  70.7 us
    all_to_all x1, waiting for transfers between devices, on_device(): lax.all_to_all(mixer_full.astype(jnp.bfloat16), 'seq', split_axis=0, conc...  66.1 us
    dot_general x64, matrix products, block_step(): scores = jnp.dot(c_block, b_block.T, precision=HIGH)  64.3 us
  transfers between devices with their start and end apart: 18, of which 11 were waited for; matrix products, arithmetic and copies ran while one was open for 25% of the time, Pallas kernels for 0%

commit v1 on v0

v1 whole, which is shorter than its diff:
```python
import jax
import jax.numpy as jnp
from jax import lax
from jax.experimental import pallas as pl
from jax.experimental.pallas import tpu as pltpu
from jax.sharding import PartitionSpec as P

HEAD_DIM = 64
CONV = 4
EPS = 1e-05
HALO = 8
GROUP = 4
WIDE = GROUP * HEAD_DIM
TILE = 128
HIGH = lax.Precision.HIGHEST
ALL = ("shard", "seq")
f32 = jnp.float32
bf16 = jnp.bfloat16


def mm(a, b):
    return jnp.dot(a, b, preferred_element_type=f32)


def mm_nt(a, b):
    return lax.dot_general(a, b, (((1,), (1,)), ((), ())), preferred_element_type=f32)


def mm_tn(a, b):
    return lax.dot_general(a, b, (((0,), (0,)), ((), ())), preferred_element_type=f32)


def spread(columns, first, stride):
    rows = columns.shape[0]
    lane = lax.broadcasted_iota(jnp.int32, (rows, 2 * HEAD_DIM), 1)
    out = []
    for pair in range(GROUP // 2):
        at = first + 2 * pair * stride
        low = columns[:, at : at + 1]
        top = columns[:, at + stride : at + stride + 1]
        out.append(jnp.where(lane < HEAD_DIM, low, top))
    return jnp.concatenate(out, axis=1)


def conv_rows(wide, taps, masks, start, rows):
    pre = taps[CONV : CONV + 1, :] + taps[CONV - 1 : CONV, :] * wide[pl.ds(HALO + start, rows), :]
    for tap in range(CONV - 1):
        shifted = wide[pl.ds(HALO - CONV + 1 + tap + start, rows), :]
        pre = pre + taps[tap : tap + 1, :] * shifted * masks[pl.ds(start, rows), tap : tap + 1]
    return pre


def forward_kernel(
    raw, taps, masks, seg_row, aux, aux_row, y_out, state_out, bc_out, ct_out, wide, score, bt, xs
):
    length = y_out.shape[0]
    n_state = bt.shape[0]
    step = pl.program_id(0)
    wide[...] = raw[...].astype(f32)

    @pl.when(step == 0)
    def _():
        for start in range(0, length, TILE):
            rows = pl.ds(start, TILE)
            pre = conv_rows(wide, taps, masks, start, TILE)
            both = pre * jax.nn.sigmoid(pre)
            bc_out[rows, :] = both.astype(bf16)
            bt[:, rows] = both[:, :n_state].T.astype(bf16)
            ct_out[:, rows] = both[:, n_state:].T.astype(bf16)
        for start in range(0, length, TILE):
            rows = pl.ds(start, TILE)
            product = mm(bc_out[rows, n_state:], bt[...])
            here = lax.broadcasted_iota(jnp.int32, (TILE, length), 0) + start
            there = lax.broadcasted_iota(jnp.int32, (TILE, length), 1)
            seen = (masks[rows, 6:7] == seg_row[0:1, :]) & (here >= there)
            score[rows, :] = jnp.where(seen, product, 0.0)

    @pl.when(step > 0)
    def _():
        for start in range(0, length, TILE):
            rows = pl.ds(start, TILE)
            pre = conv_rows(wide, taps, masks, start, TILE)
            x = pre * jax.nn.sigmoid(pre)
            columns = aux[0, rows, :]
            scaled = (x * spread(columns, 1, 4)).astype(bf16)
            xs[rows, :] = scaled
            y_out[rows, :] = x * taps[5:6, :]
        for start in range(0, length, TILE):
            rows = pl.ds(start, TILE)
            seen = start + TILE
            columns = aux[0, rows, :]
            for head in range(GROUP):
                lanes = slice(head * HEAD_DIM, (head + 1) * HEAD_DIM)
                gap = columns[:, 4 * head : 4 * head + 1] - aux_row[0, head : head + 1, :seen]
                weight = jnp.exp(jnp.minimum(gap, 0.0)) * score[rows, :seen]
                y_out[rows, lanes] += mm(weight.astype(bf16), xs[:seen, lanes])
        kept = []
        for start in range(0, length, TILE):
            rows = pl.ds(start, TILE)
            kept.append((xs[rows, :].astype(f32) * spread(aux[0, rows, :], 2, 4)).astype(bf16))
        state_out[...] = mm(bt[...], jnp.concatenate(kept, 0)).astype(bf16)


def gate_kernel(
    y_in, z_in, dn_in, bc, ct, enter, state, gain, mo_out, norm_out, dz_out, dy_out, ds_out,
    dc_out, dg_out, gated_s, silu_s, ds_acc
):
    rows = y_in.shape[0]
    width = y_in.shape[1]
    n_state = state.shape[0]
    step = pl.program_id(0)
    lane = lax.broadcasted_iota(jnp.int32, (rows, 2 * HEAD_DIM), 1)
    c_mat = bc[:, n_state:]

    @pl.when(step == 0)
    def _():
        ds_acc[...] = jnp.zeros_like(ds_acc)
        dg_out[...] = jnp.zeros_like(dg_out)

    def entering(block):
        low = enter[:, 2 * block : 2 * block + 1]
        top = enter[:, 2 * block + 1 : 2 * block + 2]
        return jnp.where(lane < HEAD_DIM, low, top)

    square = jnp.zeros((rows, 2 * HEAD_DIM), f32)
    cross = jnp.zeros((rows, 2 * HEAD_DIM), f32)
    for block in range(width // (2 * HEAD_DIM)):
        lanes = slice(block * 2 * HEAD_DIM, (block + 1) * 2 * HEAD_DIM)
        mo = y_in[:, lanes] + entering(block) * mm(c_mat, state[:, lanes])
        mo_out[:, lanes] = mo
        z = z_in[:, lanes].astype(f32)
        silu = z * jax.nn.sigmoid(z)
        gated = mo.astype(bf16).astype(f32) * silu
        gated_s[:, lanes] = gated
        silu_s[:, lanes] = silu
        square = square + gated * gated
        cross = cross + gated * (dn_in[:, lanes] * gain[0:1, lanes])
    scale = lax.rsqrt(jnp.sum(square, axis=1, keepdims=True) * (1.0 / width) + EPS)
    pull = scale * scale * scale * (jnp.sum(cross, axis=1, keepdims=True) * (1.0 / width))
    dc = jnp.zeros((rows, n_state), f32)
    for block in range(width // (2 * HEAD_DIM)):
        lanes = slice(block * 2 * HEAD_DIM, (block + 1) * 2 * HEAD_DIM)
        gated = gated_s[:, lanes]
        silu = silu_s[:, lanes]
        dn = dn_in[:, lanes]
        hat = gated * scale
        norm_out[:, lanes] = (hat * gain[0:1, lanes]).astype(bf16)
        part = dn * hat
        total = part[0:8, :]
        for at in range(8, rows, 8):
            total = total + part[at : at + 8, :]
        dg_out[:, lanes] += total
        d_gated = scale * (dn * gain[0:1, lanes]) - gated * pull
        dy = (d_gated * silu).astype(bf16)
        dy_out[:, lanes] = dy
        z = z_in[:, lanes].astype(f32)
        sig = jax.nn.sigmoid(z)
        mo = mo_out[:, lanes].astype(bf16).astype(f32)
        dz_out[:, lanes] = (d_gated * mo * (sig + silu * (1.0 - sig))).astype(bf16)
        weighted = (dy.astype(f32) * entering(block)).astype(bf16)
        ds_acc[:, lanes] += mm(ct[...], weighted)
        dc = dc + mm_nt(weighted, state[:, lanes])
    dc_out[...] = dc

    @pl.when(step == pl.num_programs(0) - 1)
    def _():
        ds_out[...] = ds_acc[...].astype(bf16)


def inside_kernel(
    raw, taps, masks, seg_row, aux, aux_row, bc, ct, dy, dxs_out, db_out, dc_out, wide, score, pair,
    xs
):
    length = dxs_out.shape[0]
    n_state = ct.shape[0]
    step = pl.program_id(0)
    wide[...] = raw[...].astype(f32)

    @pl.when(step == 0)
    def _():
        pair[...] = jnp.zeros_like(pair)
        for start in range(0, length, TILE):
            rows = pl.ds(start, TILE)
            product = mm(bc[rows, :n_state], ct[...])
            here = lax.broadcasted_iota(jnp.int32, (TILE, length), 0) + start
            there = lax.broadcasted_iota(jnp.int32, (TILE, length), 1)
            seen = (masks[rows, 6:7] == seg_row[0:1, :]) & (here <= there)
            score[rows, :] = jnp.where(seen, product, 0.0)

    for start in range(0, length, TILE):
        rows = pl.ds(start, TILE)
        pre = conv_rows(wide, taps, masks, start, TILE)
        x = pre * jax.nn.sigmoid(pre)
        xs[rows, :] = (x * spread(aux[0, rows, :], 1, 4)).astype(bf16)
    for start in range(0, length, TILE):
        rows = pl.ds(start, TILE)
        columns = aux[0, rows, :]
        gathered = None
        for head in range(GROUP):
            lanes = slice(head * HEAD_DIM, (head + 1) * HEAD_DIM)
            gap = aux_row[0, head : head + 1, start:] - columns[:, 4 * head : 4 * head + 1]
            decay = jnp.exp(jnp.minimum(gap, 0.0))
            weight = (decay * score[rows, start:]).astype(bf16)
            dxs_out[rows, lanes] = mm(weight, dy[start:, lanes])
            crossed = decay * mm_nt(xs[rows, lanes], dy[start:, lanes])
            gathered = crossed if gathered is None else gathered + crossed
        pair[rows, start:] += gathered

    @pl.when(step == pl.num_programs(0) - 1)
    def _():
        for start in range(0, length, TILE):
            rows = pl.ds(start, TILE)
            here = lax.broadcasted_iota(jnp.int32, (TILE, length), 0) + start
            there = lax.broadcasted_iota(jnp.int32, (TILE, length), 1)
            seen = (masks[rows, 6:7] == seg_row[0:1, :]) & (here <= there)
            part = jnp.where(seen, pair[rows, :], 0.0).astype(bf16)
            db_out[rows, :] = mm(part, bc[:, n_state:])
            if start == 0:
                dc_out[...] = mm_tn(part, bc[rows, :n_state])
            else:
                dc_out[...] += mm_tn(part, bc[rows, :n_state])


def outside_kernel(
    raw, taps, masks, aux, bc, dy, mo, dxs_in, d_state, state, db_in, dc_in, dc_more,
    d_out, first_out, last_out, sums_out, red_out, wide, d_pre, db_acc
):
    length = d_out.shape[0]
    n_state = bc.shape[1] // 2
    step = pl.program_id(0)
    last_step = pl.num_programs(0) - 1
    wide[...] = raw[...].astype(f32)

    @pl.when(step == 0)
    def _():
        db_acc[...] = jnp.zeros_like(db_acc)

    d_pre[pl.ds(length, HALO), :] = jnp.zeros((HALO, d_pre.shape[1]), f32)
    zero = jnp.zeros((1, d_pre.shape[1]), f32)

    @pl.when(step < last_step)
    def _():
        skip_sum, keep_sum = (zero, zero)
        ds = d_state[...]
        lane = lax.broadcasted_iota(jnp.int32, (TILE, 2 * HEAD_DIM), 1)
        for start in range(0, length, TILE):
            rows = pl.ds(start, TILE)
            columns = aux[0, rows, :]
            pre = conv_rows(wide, taps, masks, start, TILE)
            sig = jax.nn.sigmoid(pre)
            x = pre * sig
            stepped = spread(columns, 1, 4)
            scaled = (x * stepped).astype(bf16)
            keep = spread(columns, 2, 4)
            carried = keep * mm(bc[rows, :n_state], ds)
            dxs = dxs_in[rows, :] + carried
            kept = (scaled.astype(f32) * keep).astype(bf16)
            db_acc[rows, :] += mm_nt(kept, ds)
            grad = dy[rows, :].astype(f32)
            keep_sum = keep_sum + jnp.sum(scaled.astype(f32) * carried, 0, keepdims=True)
            skip_sum = skip_sum + jnp.sum(grad * x, 0, keepdims=True)
            change = grad * (mo[rows, :] - taps[5:6, :] * x) - scaled.astype(f32) * dxs
            direct = x * dxs
            found = jnp.zeros((TILE, 2 * HEAD_DIM), f32)
            for head in range(GROUP):
                lanes = slice(head * HEAD_DIM, (head + 1) * HEAD_DIM)
                one = jnp.sum(change[:, lanes], 1, keepdims=True)
                two = jnp.sum(direct[:, lanes], 1, keepdims=True)
                found = jnp.where(lane == head, one, found)
                found = jnp.where(lane == GROUP + head, two, found)
            red_out[0, rows, :] = found[:, : red_out.shape[2]]
            d_x = taps[5:6, :] * grad + stepped * dxs
            d_pre[rows, :] = d_x * (sig + x * (1.0 - sig))
        met = jnp.sum(ds.astype(f32) * state[...].astype(f32), 0, keepdims=True)
        sums_out[5:6, :] = skip_sum
        sums_out[6:7, :] = keep_sum
        sums_out[7:8, :] = met

    @pl.when(step == last_step)
    def _():
        for start in range(0, length, TILE):
            rows = pl.ds(start, TILE)
            pre = conv_rows(wide, taps, masks, start, TILE)
            sig = jax.nn.sigmoid(pre)
            slope = sig + pre * sig * (1.0 - sig)
            d_b = db_in[rows, :] + db_acc[rows, :]
            d_c = dc_in[rows, :] + dc_more[rows, :]
            d_pre[rows, :] = jnp.concatenate([d_b, d_c], 1) * slope
        sums_out[5:8, :] = jnp.zeros((3, d_pre.shape[1]), f32)

    totals = [zero] * (CONV + 1)
    for start in range(0, length, TILE):
        rows = pl.ds(start, TILE)
        grad = d_pre[rows, :]
        totals[CONV] = totals[CONV] + jnp.sum(grad, 0, keepdims=True)
        here = wide[pl.ds(HALO + start, TILE), :]
        totals[CONV - 1] = totals[CONV - 1] + jnp.sum(grad * here, 0, keepdims=True)
        back = taps[CONV - 1 : CONV, :] * grad
        for tap in range(CONV - 1):
            shifted = wide[pl.ds(HALO - CONV + 1 + tap + start, TILE), :]
            masked = grad * masks[rows, tap : tap + 1]
            totals[tap] = totals[tap] + jnp.sum(masked * shifted, 0, keepdims=True)
            ahead = d_pre[pl.ds(start + CONV - 1 - tap, TILE), :]
            back = back + taps[tap : tap + 1, :] * ahead * masks[rows, 3 + tap : 4 + tap]
        d_out[rows, :] = back.astype(bf16)
        if start + TILE == length:
            last_out[...] = back[TILE - HALO :, :]
    first_out[...] = d_pre[pl.ds(0, HALO), :]
    for tap in range(CONV + 1):
        sums_out[tap : tap + 1, :] = totals[tap]


def scan_devices(local, decay, backward):
    shards, places = (lax.axis_size("shard"), lax.axis_size("seq"))
    shard, place = (lax.axis_index("shard"), lax.axis_index("seq"))
    n_state, inner = local.shape
    width = inner // places
    split = local.reshape(n_state, places, width).transpose(1, 0, 2)
    mine = lax.all_to_all(split, "seq", split_axis=0, concat_axis=0, tiled=True).astype(f32)
    decay = lax.dynamic_slice_in_dim(decay.reshape(shards, places, inner), place * width, width, 2)
    own = lax.dynamic_index_in_dim(decay, shard, 0, False)
    order = range(places - 1, -1, -1) if backward else range(places)
    state = jnp.zeros((n_state, width), f32)
    for at in order:
        state = own[at][None, :] * state + mine[at]
    parts = lax.all_gather(state.astype(bf16), "shard").astype(f32)
    whole = jnp.prod(decay, axis=1)
    state = jnp.zeros((n_state, width), f32)
    for at in range(shards - 1, -1, -1) if backward else range(shards):
        counted = (at > shard) if backward else (at < shard)
        state = jnp.where(counted, whole[at][None, :] * state + parts[at], state)
    entering = [None] * places
    for at in order:
        entering[at] = state.astype(bf16)
        state = own[at][None, :] * state + mine[at]
    back = lax.all_to_all(jnp.stack(entering), "seq", split_axis=0, concat_axis=0, tiled=True)
    return back.transpose(1, 0, 2).reshape(n_state, inner)


def on_device(
    hidden,
    cotangent,
    seg_ids,
    norm_gain,
    in_weight,
    conv_weight,
    conv_bias,
    dt_bias,
    a_log,
    d_skip,
    out_gain,
    out_weight,
):
    shards, places = (lax.axis_size("shard"), lax.axis_size("seq"))
    shard, place = (lax.axis_index("shard"), lax.axis_index("seq"))
    devices = shards * places
    me = shard * places + place
    length, width = hidden.shape
    heads = dt_bias.shape[0]
    inner = out_weight.shape[0] * shards
    channels = conv_bias.shape[0] * shards
    n_state = (channels - inner) // 2
    groups = inner // WIDE
    start = me * length

    small = jnp.concatenate(
        [norm_gain, conv_weight.reshape(-1), conv_bias, out_gain]
    )
    small = lax.all_gather(small, "shard")
    at = 0
    gain_in = small[:, at : at + norm_gain.shape[0]].reshape(-1).astype(f32)
    at += norm_gain.shape[0]
    taps = small[:, at : at + conv_weight.size].reshape(shards, CONV, -1)
    taps = taps.transpose(1, 0, 2).reshape(CONV, channels).astype(f32)
    at += conv_weight.size
    bias = small[:, at : at + conv_bias.shape[0]].reshape(-1).astype(f32)
    at += conv_bias.shape[0]
    gain_out = small[:, at:].reshape(-1).astype(f32)
    w_x = lax.all_gather(in_weight[:, inner:], "shard", axis=0, tiled=True)
    w_z = lax.all_gather(in_weight[:, :inner], "shard", axis=0, tiled=True)
    w_out = lax.all_gather(out_weight, "shard", axis=0, tiled=True)
    skip_wide = jnp.repeat(d_skip.astype(f32), HEAD_DIM)
    rows = jnp.concatenate([skip_wide, jnp.zeros((channels - inner,), f32)])
    taps8 = jnp.concatenate([taps, bias[None], rows[None], jnp.zeros((2, channels), f32)], 0)

    edge = jnp.full((HALO,), -1, jnp.int32)
    padded = jnp.concatenate([edge, seg_ids, edge - 1])
    near = lax.dynamic_slice_in_dim(padded, start, length + 2 * HALO)
    seg = near[HALO : HALO + length]
    fwd_masks = [near[HALO - CONV + 1 + k : HALO - CONV + 1 + k + length] == seg for k in range(3)]
    spot = jnp.arange(length, dtype=jnp.int32)
    bwd_masks = [
        (near[HALO + CONV - 1 - k : HALO + CONV - 1 - k + length] == seg)
        & (spot + CONV - 1 - k < length)
        for k in range(3)
    ]
    masks = jnp.stack(
        [m.astype(f32) for m in fwd_masks + bwd_masks] + [seg.astype(f32), jnp.zeros((length,), f32)],
        1,
    )
    seg_row = jnp.broadcast_to(seg.astype(f32)[None, :], (8, length))
    from_before = seg == near[HALO - 1]
    to_last = seg == seg[length - 1]

    behind = lax.ppermute(
        hidden[length - HALO :], ALL, [(i, i + 1) for i in range(devices - 1)]
    )
    hidden_f = jnp.concatenate([behind, hidden], 0).astype(f32)
    scale_in = lax.rsqrt(jnp.mean(hidden_f * hidden_f, axis=1, keepdims=True) + EPS)
    normed_ext = (hidden_f * scale_in * gain_in[None, :]).astype(bf16)
    normed_in = normed_ext[HALO:]
    proj = mm(normed_ext, w_x).astype(bf16)
    dt_raw = proj[HALO:, channels:].astype(f32)
    shifted = dt_raw + dt_bias.astype(f32)[None, :]
    step_size = jax.nn.softplus(shifted)
    rate = jnp.exp(a_log.astype(f32))
    log_decay = -step_size * rate[None, :]
    lower = (spot[:, None] >= spot[None, :]).astype(f32)
    cum = jnp.dot(lower, log_decay, precision=HIGH)
    keep = jnp.where(to_last[:, None], jnp.exp(cum[length - 1][None, :] - cum), 0.0)
    enter = jnp.where(from_before[:, None], jnp.exp(cum), 0.0)
    aux = jnp.stack([cum, step_size, keep, enter], -1).reshape(length, groups, 4 * GROUP)
    aux = aux.transpose(1, 0, 2)
    aux_row = cum.T.reshape(groups, GROUP, length)
    decays = lax.all_gather(enter[length - 1], ALL)
    decays = jnp.repeat(decays.reshape(devices, heads), HEAD_DIM, axis=1)

    big = pltpu.CompilerParams(vmem_limit_bytes=56 * 1024 * 1024)

    def whole(shape):
        return pl.BlockSpec(shape, lambda g: (0,) * len(shape))

    def group_of(g):
        return jnp.maximum(g - 1, 0)

    order = lambda g: jnp.where(g == 0, groups, g - 1)
    y_local, state_local, bc, ct = pl.pallas_call(
        forward_kernel,
        grid=(groups + 1,),
        in_specs=[
            pl.BlockSpec((length + HALO, WIDE), lambda g: (0, order(g))),
            pl.BlockSpec((8, WIDE), lambda g: (0, order(g))),
            whole((length, 8)),
            whole((8, length)),
            pl.BlockSpec((1, length, 4 * GROUP), lambda g: (group_of(g), 0, 0)),
            pl.BlockSpec((1, GROUP, length), lambda g: (group_of(g), 0, 0)),
        ],
        out_specs=[
            pl.BlockSpec((length, WIDE), lambda g: (0, group_of(g))),
            pl.BlockSpec((n_state, WIDE), lambda g: (0, group_of(g))),
            whole((length, 2 * n_state)),
            whole((n_state, length)),
        ],
        out_shape=[
            jax.ShapeDtypeStruct((length, inner), f32),
            jax.ShapeDtypeStruct((n_state, inner), bf16),
            jax.ShapeDtypeStruct((length, 2 * n_state), bf16),
            jax.ShapeDtypeStruct((n_state, length), bf16),
        ],
        scratch_shapes=[
            pltpu.VMEM((length + HALO, WIDE), f32),
            pltpu.VMEM((length, length), f32),
            pltpu.VMEM((n_state, length), bf16),
            pltpu.VMEM((length, WIDE), bf16),
        ],
        compiler_params=big,
        cost_estimate=pl.CostEstimate(
            flops=4 * length * length * inner, bytes_accessed=10 * length * inner, transcendentals=0
        ),
        name="mixer_forward",
    )(proj, taps8, masks, seg_row, aux, aux_row)

    state_in = scan_devices(state_local, decays, False)
    gate_z = mm(normed_in, w_z).astype(bf16)
    d_normed = mm_nt(cotangent, w_out)

    block = TILE
    tall = lambda dim: pl.BlockSpec((block, dim), lambda g: (g, 0))
    mo, normed_out, d_z, d_y, d_state_local, dc_more, d_gain = pl.pallas_call(
        gate_kernel,
        grid=(length // block,),
        in_specs=[
            tall(inner),
            tall(inner),
            tall(inner),
            tall(2 * n_state),
            pl.BlockSpec((n_state, block), lambda g: (0, g)),
            tall(heads),
            whole((n_state, inner)),
            whole((1, inner)),
        ],
        out_specs=[
            tall(inner),
            tall(inner),
            tall(inner),
            tall(inner),
            whole((n_state, inner)),
            tall(n_state),
            whole((8, inner)),
        ],
        out_shape=[
            jax.ShapeDtypeStruct((length, inner), f32),
            jax.ShapeDtypeStruct((length, inner), bf16),
            jax.ShapeDtypeStruct((length, inner), bf16),
            jax.ShapeDtypeStruct((length, inner), bf16),
            jax.ShapeDtypeStruct((n_state, inner), bf16),
            jax.ShapeDtypeStruct((length, n_state), f32),
            jax.ShapeDtypeStruct((8, inner), f32),
        ],
        scratch_shapes=[
            pltpu.VMEM((block, inner), f32),
            pltpu.VMEM((block, inner), f32),
            pltpu.VMEM((n_state, inner), f32),
        ],
        compiler_params=big,
        cost_estimate=pl.CostEstimate(
            flops=8 * length * n_state * inner, bytes_accessed=22 * length * inner, transcendentals=0
        ),
        name="mixer_gate",
    )(y_local, gate_z, d_normed, bc, ct, enter, state_in, gain_out[None, :])

    block_out = (hidden.astype(f32) + mm(normed_out, w_out)).astype(bf16)
    grad_out_w = mm_tn(normed_out, cotangent).astype(bf16)
    grad_z_w = mm_tn(normed_in, d_z).astype(bf16)
    d_state = scan_devices(d_state_local, decays, True)

    dxs, db_in, dc_in = pl.pallas_call(
        inside_kernel,
        grid=(groups,),
        in_specs=[
            pl.BlockSpec((length + HALO, WIDE), lambda g: (0, g)),
            pl.BlockSpec((8, WIDE), lambda g: (0, g)),
            whole((length, 8)),
            whole((8, length)),
            pl.BlockSpec((1, length, 4 * GROUP), lambda g: (g, 0, 0)),
            pl.BlockSpec((1, GROUP, length), lambda g: (g, 0, 0)),
            whole((length, 2 * n_state)),
            whole((n_state, length)),
            pl.BlockSpec((length, WIDE), lambda g: (0, g)),
        ],
        out_specs=[
            pl.BlockSpec((length, WIDE), lambda g: (0, g)),
            whole((length, n_state)),
            whole((length, n_state)),
        ],
        out_shape=[
            jax.ShapeDtypeStruct((length, inner), f32),
            jax.ShapeDtypeStruct((length, n_state), f32),
            jax.ShapeDtypeStruct((length, n_state), f32),
        ],
        scratch_shapes=[
            pltpu.VMEM((length + HALO, WIDE), f32),
            pltpu.VMEM((length, length), f32),
            pltpu.VMEM((length, length), f32),
            pltpu.VMEM((length, WIDE), bf16),
        ],
        compiler_params=big,
        cost_estimate=pl.CostEstimate(
            flops=8 * length * length * inner, bytes_accessed=10 * length * inner, transcendentals=0
        ),
        name="mixer_inside",
    )(proj, taps8, masks, seg_row, aux, aux_row, bc, ct, d_y)

    kept = lambda g: jnp.minimum(g, groups - 1)
    d_xbc, first, last, sums, reduced = pl.pallas_call(
        outside_kernel,
        grid=(groups + 1,),
        in_specs=[
            pl.BlockSpec((length + HALO, WIDE), lambda g: (0, g)),
            pl.BlockSpec((8, WIDE), lambda g: (0, g)),
            whole((length, 8)),
            pl.BlockSpec((1, length, 4 * GROUP), lambda g: (kept(g), 0, 0)),
            whole((length, 2 * n_state)),
            pl.BlockSpec((length, WIDE), lambda g: (0, kept(g))),
            pl.BlockSpec((length, WIDE), lambda g: (0, kept(g))),
            pl.BlockSpec((length, WIDE), lambda g: (0, kept(g))),
            pl.BlockSpec((n_state, WIDE), lambda g: (0, kept(g))),
            pl.BlockSpec((n_state, WIDE), lambda g: (0, kept(g))),
            whole((length, n_state)),
            whole((length, n_state)),
            whole((length, n_state)),
        ],
        out_specs=[
            pl.BlockSpec((length, WIDE), lambda g: (0, g)),
            pl.BlockSpec((HALO, WIDE), lambda g: (0, g)),
            pl.BlockSpec((HALO, WIDE), lambda g: (0, g)),
            pl.BlockSpec((8, WIDE), lambda g: (0, g)),
            pl.BlockSpec((1, length, 2 * GROUP), lambda g: (kept(g), 0, 0)),
        ],
        out_shape=[
            jax.ShapeDtypeStruct((length, channels), bf16),
            jax.ShapeDtypeStruct((HALO, channels), f32),
            jax.ShapeDtypeStruct((HALO, channels), f32),
            jax.ShapeDtypeStruct((8, channels), f32),
            jax.ShapeDtypeStruct((groups, length, 2 * GROUP), f32),
        ],
        scratch_shapes=[
            pltpu.VMEM((length + HALO, WIDE), f32),
            pltpu.VMEM((length + HALO, WIDE), f32),
            pltpu.VMEM((length, n_state), f32),
        ],
        compiler_params=big,
        cost_estimate=pl.CostEstimate(
            flops=8 * length * n_state * inner, bytes_accessed=16 * length * inner, transcendentals=0
        ),
        name="mixer_outside",
    )(proj, taps8, masks, aux, bc, d_y, mo, dxs, d_state, state_in, db_in, dc_in, dc_more)

    ahead = lax.ppermute(first, ALL, [(i + 1, i) for i in range(devices - 1)])
    joined = jnp.concatenate([jnp.zeros((HALO, channels), f32), ahead], 0)
    seg_end = near[length : length + 2 * HALO]
    for tap in range(CONV - 1):
        lead = CONV - 1 - tap
        same = (seg_end[lead : lead + HALO] == seg_end[:HALO]).astype(f32)[:, None]
        last = last + taps[tap][None, :] * joined[lead : lead + HALO] * same
    d_xbc = lax.dynamic_update_slice_in_dim(d_xbc, last.astype(bf16), length - HALO, 0)

    reduced = reduced.reshape(groups, length, 2, GROUP).transpose(2, 1, 0, 3).reshape(2, length, heads)
    to_head = lambda row: row[:inner].reshape(heads, HEAD_DIM).sum(1)
    tail = to_head(sums[6]) + enter[length - 1] * to_head(sums[7])
    d_cum = reduced[0].at[length - 1].add(tail)
    d_log = jnp.dot(lower.T, d_cum, precision=HIGH)
    d_step = reduced[1] - rate[None, :] * d_log
    d_dt = d_step * jax.nn.sigmoid(shifted)
    grad_a = jnp.sum(d_log * log_decay, 0)
    grad_dt = jnp.sum(d_dt, 0)
    grad_skip = to_head(sums[5])

    d_proj = jnp.concatenate([d_xbc, d_dt.astype(bf16)], 1)
    grad_x_w = mm_tn(normed_in, d_proj).astype(bf16)
    d_normed_in = mm_nt(d_z, w_z) + mm_nt(d_proj, w_x)
    base = hidden_f[HALO:]
    scale = scale_in[HALO:]
    d_hat = d_normed_in * gain_in[None, :]
    mean = jnp.mean(d_hat * base, axis=1, keepdims=True)
    grad_hidden = cotangent.astype(f32) + scale * d_hat - base * (scale * scale * scale * mean)
    grad_gain_in = jnp.sum(d_normed_in * base * scale, 0)
    grad_gain_out = jnp.sum(d_gain, 0)

    scatter = lambda a: lax.psum_scatter(a, ALL, scatter_dimension=0, tiled=True)
    out_w = scatter(grad_out_w).astype(f32)
    z_w = scatter(grad_z_w).astype(f32)
    x_w = scatter(grad_x_w).astype(f32)
    pieces = [
        grad_gain_in,
        sums[:CONV].reshape(-1),
        sums[CONV],
        grad_gain_out,
        grad_dt,
        grad_a,
        grad_skip,
    ]
    total = lax.psum(jnp.concatenate(pieces), ALL)
    found, at = ([], 0)
    for piece in pieces:
        found.append(total[at : at + piece.shape[0]])
        at += piece.shape[0]

    def part(vector):
        size = vector.shape[-1] // devices
        return lax.dynamic_slice_in_dim(vector, me * size, size, vector.ndim - 1)

    return (
        block_out,
        grad_hidden,
        part(found[0]),
        jnp.concatenate([z_w, x_w], 1),
        part(found[1].reshape(CONV, channels)),
        part(found[2]),
        found[4],
        found[5],
        found[6],
        part(found[3]),
        out_w,
    )


def solution(mesh):
    return jax.shard_map(
        on_device,
        mesh=mesh,
        in_specs=(
            P(ALL, None),
            P(ALL, None),
            P(),
            P("shard"),
            P("shard", None),
            P(None, "shard"),
            P("shard"),
            P(),
            P(),
            P(),
            P("shard"),
            P("shard", None),
        ),
        out_specs=(
            P(ALL, None),
            P(ALL, None),
            P(ALL),
            P(ALL, None),
            P(None, ALL),
            P(ALL),
            P(),
            P(),
            P(),
            P(ALL),
            P(ALL, None),
        ),
        check_vma=False,
    )
```

time: 2120 us -> 1030 us (0.49)
  matrix products: 579 us -> 94.6 us
  other arithmetic: 393 us -> 26.9 us
  local copies, waits for them, and re-layouts: 278 us -> 38.1 us
  Pallas kernels: 0 us -> 160 us
  waiting for transfers between devices: 708 us -> 567 us
    dot_general x335 -> x11, matrix products: 579 us -> 94.6 us  [the longest x3 32.8 us: mm_nt(): lax.dot_general(a, b, (((1,), (1,)), ((), ())), preferred_element_type=f32)]
    reduce_scatter x4 -> x3, waiting for transfers between devices: 135 us -> 423 us  [on_device(): lax.psum_scatter(a, ALL, scatter_dimension=0, tiled=True)]
    unnamed x13 -> x7, waiting for transfers between devices: 263 us -> 0.78 us
    another operation x102 -> x5, other arithmetic: 231 us -> 3.37 us  [the longest x3 2.04 us: on_device(): jnp.stack([cum, step_size, keep, enter], -1)]
    pallas_call x0 -> x4, Pallas kernels: none -> 160 us  [the longest x1 52.1 us: on_device(): pl.pallas_call(outside_kernel, grid=(groups + 1,), in_specs=[pl.BlockSpec...]
    all_gather x3, waiting for transfers between devices: 169 us -> 42.8 us  [the longest x1 42.8 us: on_device(): w_x = lax.all_gather(in_weight[:, inner:], 'shard', axis=0, tiled=True)]
    all_to_all x4, waiting for transfers between devices: 142 us -> 19.5 us  [the longest x2 17.8 us: scan_devices(): lax.all_to_all(split, 'seq', split_axis=0, concat_axis=0, tiled=True)]
    psum x0 -> x1, waiting for transfers between devices: none -> 78.4 us  [on_device(): total = lax.psum(jnp.concatenate(pieces), ALL)]
  transfers between devices with their start and end apart: 18 -> 13, of which waited for: 11 -> 8; matrix products, arithmetic and copies ran while one was open for 25% -> 12% of each run, Pallas kernels for 0% -> 9%
where the time goes in v1:
time: 1030 us
  waiting for transfers between devices  567 us (55%)
  Pallas kernels  160 us (16%)
  blocking collectives  99.5 us (10%)
  matrix products  94.6 us (9%)
  local copies, waits for them, and re-layouts  38.1 us (4%)
  other arithmetic  26.9 us (3%)
  starting transfers between devices  24.2 us (2%)
  between operations  16 us (2%)
    reduce_scatter x3, waiting for transfers between devices, on_device(): lax.psum_scatter(a, ALL, scatter_dimension=0, tiled=True)  423 us
    psum x1, waiting for transfers between devices, on_device(): total = lax.psum(jnp.concatenate(pieces), ALL)  78.4 us
    all_gather x1, blocking collectives, on_device(): decays = lax.all_gather(enter[length - 1], ALL)  74.6 us
    pallas_call x1, Pallas kernels, on_device(): pl.pallas_call(outside_kernel, grid=(groups + 1,), in_specs=[pl.BlockSpec...  52.1 us
    pallas_call x1, Pallas kernels, on_device(): pl.pallas_call(forward_kernel, grid=(groups + 1,), in_specs=[pl.BlockSpec...  48.3 us
    all_gather x1, waiting for transfers between devices, on_device(): w_x = lax.all_gather(in_weight[:, inner:], 'shard', axis=0, tiled=True)  42.8 us
    pallas_call x1, Pallas kernels, on_device(): pl.pallas_call(inside_kernel, grid=(groups,), in_specs=[pl.BlockSpec((len...  41.3 us
    dot_general x3, matrix products, mm_nt(): lax.dot_general(a, b, (((1,), (1,)), ((), ())), preferred_element_type=f32)  32.8 us
  transfers between devices with their start and end apart: 13, of which 8 were waited for; matrix products, arithmetic and copies ran while one was open for 12% of the time, Pallas kernels for 9%

profile of v1, /device:TPU:0, one launch (start us, length us, event | category | flops | bytes accessed | tf_op | source)
XLA Modules:
  0.0 1025.6 jit_solution(16985392127127461841)
XLA Ops:
  7.2 3.5 slice.341
  10.8 3.3 slice.356
  15.5 4.9 collective-permute-start
  22.2 12.7 %all-reduce.2 = bf16[21248]{0:T(1024)(128)(2,1)S(1)} all-reduce(bf16[21248]{0:T(1024)(128)(2,1)S(1)} %dynamic-update-slice.3), channel_id=2, replica_groups=mesh['shard'=4,'seq'=8] {'shard'}, use_global_device_ids=true, to_apply=%add.2 | all-reduce | flops 21248 | bytes 84992
  36.5 1.9 broadcast_compare_fusion.1
  38.4 0.7 maximum_maximum_fusion.taps
  39.3 0.8 copy.92.masks
  41.0 42.8 %all-gather.6.cloned.1.call-done = bf16[1536,3376]{0,1:T(8,128)(2,1)} async-done(((bf16[384,3376]{0,1:T(8,128)(2,1)}), bf16[1536,3376]{0,1:T(8,128)(2,1)}) %all-gather.6.cloned.1.call-update) | async-done | bytes 10371088 | tf_op jit(solution)/shard_map/all_gather | solution.py:379
  83.8 10.2 convolution_convert_fusion.3.raw
  94.1 1.7 copy-done.2
  96.8 1.1 fusion.31
  97.9 0.9 select_bitcast_fusion
  99.4 2.2 copy.91
  102.8 48.3 %mixer_forward.1 = (f32[512,3072]{1,0:T(8,128)}, bf16[128,3072]{1,0:T(8,128)(2,1)}, bf16[512,256]{1,0:T(8,128)(2,1)}, bf16[128,512]{1,0:T(8,128)(2,1)}) custom-call(bf16[520,3376]{1,0:T(8,128)(2,1)} %copy-done.2, f32[8,3328]{1,0:T(8,128)} %maximum_maximum_fusion.taps, f32[512,8]{1,0:T(8,128)} %copy.92.masks, f32[8,512]{1,0:T(8,128)} %broadcast_in_dim.29.seg_row, ...), custom_call_target="tpu_custom_call" | custom-call | flops 3221225472 | bytes 15728640 | tf_op jit(solution)/shard_map/mixer_forward/pallas_call | solution.py:437
  151.2 2.1 copy.114
  153.3 5.6 all-to-all-start
  159.5 74.6 %all-gather.1 = f32[32,1,48]{2,1,0:T(1,128)S(1)} all-gather(f32[1,1,48]{2,1,0:T(1,128)S(1)} %slice_bitcast_fusion), channel_id=1, replica_groups=mesh['shard'=4,'seq'=8] {'shard','seq'}, dimensions={0}, use_global_device_ids=true | all-gather | bytes 6336 | tf_op jit(solution)/shard_map/all_gather | solution.py:425
  235.2 6.1 all_gather.32
  241.4 0.7 convert_dynamic-update-slice_fusion.13
  242.8 0.7 convert_dynamic-update-slice_fusion.11
  244.1 0.7 convert_dynamic-update-slice_fusion.9
  245.5 0.7 convert_dynamic-update-slice_fusion.7
  246.9 3.5 all-to-all-start.1
  250.4 9.3 convolution_convert_fusion.4.z_in
  259.8 9.8 fusion.55.dn_in
  269.6 1.7 all-to-all-done.1
  271.3 1.0 copy.107
  272.3 17.9 %mixer_gate.1 = (f32[512,3072]{1,0:T(8,128)}, bf16[512,3072]{1,0:T(8,128)(2,1)}, bf16[512,3072]{1,0:T(8,128)(2,1)}, bf16[512,3072]{1,0:T(8,128)(2,1)}, bf16[128,...) custom-call(f32[512,3072]{1,0:T(8,128)} %get-tuple-element.42.y_in, ...), custom_call_target="tpu_custom_call" | custom-call | flops 1610612736 | bytes 34603008 | tf_op jit(solution)/shard_map/mixer_gate/pallas_call | solution.py:479
  290.2 2.1 copy.113
  292.3 4.4 all-to-all-start.2
  297.1 2.1 maximum_convert_fusion
  299.3 17.8 %all-to-all-done.2 = bf16[8,128,384]{2,1,0:T(8,128)(2,1)S(1)} async-done(((bf16[8,128,384]{2,1,0:T(8,128)(2,1)}), bf16[8,128,384]{2,1,0:T(8,128)(2,1)S(1)}, u32[]{:S(2)}, u32[]{:S(2)}) %all-to-all-start.2) | async-done | bytes 786464 | tf_op jit(solution)/shard_map/all_to_all | solution.py:319
  317.4 6.1 all_gather.33
  323.6 0.8 fusion.30
  329.0 3.7 all-to-all-start.3
  333.1 41.3 %mixer_inside.1 = (f32[512,3072]{1,0:T(8,128)}, f32[512,128]{1,0:T(8,128)}, f32[512,128]{1,0:T(8,128)}) custom-call(bf16[520,3376]{1,0:T(8,128)(2,1)} %copy-done.2, f32[8,3328]{1,0:T(8,128)} %maximum_maximum_fusion.taps, f32[512,8]{1,0:T(8,128)} %copy.92.masks, f32[8,512]{1,0:T(8,128)} %broadcast_in_dim.29.seg_row, f32[12,512,16]{2,1,0:T(8,128)} %bitcast.83, ...), custom_call_target="tpu_custom_call" | custom-call | flops 6442450944 | bytes 15728640 | tf_op jit(solution)/shard_map/mixer_inside/pallas_call | solution.py:527
  374.5 10.5 %fusion.56 = f32[512,1536]{1,0:T(8,128)} fusion(bf16[512,3072]{1,0:T(8,128)(2,1)} %get-tuple-element.47, bf16[1536,3072]{0,1:T(8,128)(2,1)} %all-gather.8.cloned.1.call-done), kind=kOutput, calls=%fused_computation.171 | convolution fusion | flops 4831838208 | bytes 15728640 | tf_op jit(solution)/shard_map/dot_general | solution.py:26
  385.1 1.0 copy.108
  386.1 52.1 %mixer_outside.1 = (bf16[512,3328]{1,0:T(8,128)(2,1)}, f32[8,3328]{1,0:T(8,128)}, f32[8,3328]{1,0:T(8,128)}, f32[8,3328]{1,0:T(8,128)}, f32[12,512,8]{2,1,0:T(8,128)}) custom-call(bf16[520,3376]{1,0:T(8,128)(2,1)} %copy-done.2, f32[8,3328]{1,0:T(8,128)} %maximum_maximum_fusion.taps, f32[512,8]{1,0:T(8,128)} %copy.92.masks, f32[12,512,16]{2,1,0:T(8,128)} %bitcast.84, ...), custom_call_target="tpu_custom_call" | custom-call | flops 1610612736 | bytes 25165824 | tf_op jit(solution)/shard_map/mixer_outside/pallas_call | solution.py:565
  438.2 2.4 copy.99
  441.0 1.3 collective-permute-start.1
  442.8 0.7 fusion.44
  444.4 1.7 fusion.48
  446.1 1.9 collective-permute-done.1
  448.1 0.7 fusion.32
  448.8 12.5 %multiply_reduce_fusion.1 = (f32[1536]{0:T(1024)S(1)}, f32[512]{0:T(512)S(1)}, f32[512,1536]{1,0:T(8,128)}) fusion(f32[520,1536]{1,0:T(8,128)} %maximum_convert_fusion, f32[512]{0:T(512)S(1)} %slice.383, f32[1536]{0:T(1024)S(1)} %copy-done.19, f32[512,1536]{1,0:T(8,128)} %fusion.56, bf16[1536,3376]{0,1:T(8,128)(2,1)} %all-gather.6.cloned.1.call-done, ...), kind=kOutput, calls=%fused_computation.10 | convolution fusion | flops 5322405888 | bytes 23281664 | tf_op jit(solution)/shard_map/dot_general | solution.py:26
  461.3 0.7 concatenate.39
  462.0 9.6 convolution_convert_fusion.1
  471.7 1.3 copy-done.6
  473.1 9.4 convolution_convert_fusion.2
  482.8 10.5 %convolution_convert_fusion = bf16[1536,3376]{1,0:T(8,128)(2,1)} fusion(bf16[512,48]{1,0:T(8,128)(2,1)S(1)} %get-tuple-element.79, bf16[512,3328]{1,0:T(8,128)(2,1)} %fusion.32, bf16[520,1536]{1,0:T(8,128)(2,1)S(1)} %copy-done.6), kind=kOutput, calls=%fused_computation | convolution fusion | flops 5322088448 | bytes 15482880 | tf_op jit(solution)/shard_map/dot_general | solution.py:30
  493.3 10.4 %fusion = bf16[512,1536]{1,0:T(8,128)(2,1)} fusion(bf16[512,3072]{1,0:T(8,128)(2,1)} %get-tuple-element.46, bf16[3072,1536]{1,0:T(8,128)(2,1)} %all-gather.10.cloned.1.call-done, bf16[512,1536]{1,0:T(8,128)(2,1)S(1)} %copy-done), kind=kOutput, calls=%fused_computation.13 | convolution fusion | flops 4834197504 | bytes 15728640 | tf_op jit(solution)/shard_map/dot_general | solution.py:22
  503.8 2.4 multiply_subtract_fusion
  506.2 78.4 %all-reduce.5.cloned.1.call-done = f32[21392]{0:T(1024)} async-done(((f32[21392]{0:T(1024)}), f32[21392]{0:T(1024)}) %all-reduce.5.cloned.1.call-update) | async-done | bytes 85584 | tf_op jit(solution)/shard_map/psum | solution.py:653
  584.6 0.8 slice.467
  585.5 0.7 slice.468
  586.8 0.7 slice.472
  588.1 0.7 slice.466
  590.0 1.4 fusion.52
  591.4 136.4 %reduce-scatter.8.cloned.1.call-done = bf16[96,1536]{1,0:T(8,128)(2,1)} async-done(((bf16[3072,1536]{1,0:T(8,128)(2,1)}), bf16[96,1536]{1,0:T(8,128)(2,1)}) %reduce-scatter.8.cloned.1.call-update) | async-done | bytes 294928 | tf_op jit(solution)/shard_map/reduce_scatter | solution.py:640
  727.8 1.8 convert_element_type.257
  729.7 139.4 %reduce-scatter.4.cloned.1.call-done = bf16[48,3072]{1,0:T(8,128)(2,1)} async-done(((bf16[1536,3072]{1,0:T(8,128)(2,1)}), bf16[48,3072]{1,0:T(8,128)(2,1)}) %reduce-scatter.4.cloned.1.call-update) | async-done | bytes 294928 | tf_op jit(solution)/shard_map/reduce_scatter | solution.py:640
  869.1 147.2 %reduce-scatter.6.cloned.1.call-done = bf16[48,3376]{1,0:T(8,128)(2,1)} async-done(((bf16[1536,3376]{1,0:T(8,128)(2,1)}), bf16[48,3376]{1,0:T(8,128)(2,1)}) %reduce-scatter.6.cloned.1.call-update) | async-done | bytes 324112 | tf_op jit(solution)/shard_map/reduce_scatter | solution.py:640
  1016.3 2.2 maximum_convert_fusion.1
  (213 shorter events, 22.7 us)
Async XLA Ops:
  7.2 76.6 %all-gather.6.cloned.1.call-start = ((), (), s32[]{:S(2)}) async-start(), calls=%async_computation.7 | async-start | bytes 12963840 | tf_op jit(solution)/shard_map/all_gather | solution.py:379
  10.7 239.7 %all-gather.8.cloned.1.call-start = ((), (), s32[]{:S(2)}) async-start(), calls=%async_computation.8 | async-start | bytes 11796480 | tf_op jit(solution)/shard_map/all_gather | solution.py:380
  14.1 1.4 copy-start
  14.1 6.3 copy-start.33
  14.1 6.4 copy-start.43
  14.1 7.6 copy-start.34
  14.1 7.6 copy-start.35
  14.1 7.6 copy-start.36
  14.1 21.3 %copy-start.39 = (bf16[48]{0:T(256)(128)(2,1)S(1)}, bf16[48]{0:T(256)(128)(2,1)}, u32[]{:S(2)}) copy-start(bf16[48]{0:T(256)(128)(2,1)} %param.23) | copy-start | bytes 292
  14.1 21.4 %copy-start.20 = (s32[16384]{0:T(1024)S(1)}, s32[16384]{0:T(1024)}, u32[]{:S(2)}) copy-start(s32[16384]{0:T(1024)} %param.16) | copy-start | bytes 196612
  14.2 25.0 %copy-start.41 = (bf16[48]{0:T(256)(128)(2,1)S(1)}, bf16[48]{0:T(256)(128)(2,1)}, u32[]{:S(2)}) copy-start(bf16[48]{0:T(256)(128)(2,1)} %param.22) | copy-start | bytes 292
  14.2 25.0 %copy-start.42 = (bf16[48]{0:T(256)(128)(2,1)S(1)}, bf16[48]{0:T(256)(128)(2,1)}, u32[]{:S(2)}) copy-start(bf16[48]{0:T(256)(128)(2,1)} %param.21) | copy-start | bytes 292
  14.2 245.5 %all-gather.10.cloned.1.call-start = ((), (), s32[]{:S(2)}) async-start(), calls=%async_computation.9 | async-start | bytes 11796480 | tf_op jit(solution)/shard_map/all_gather | solution.py:381
  15.5 24.6 %collective-permute-start = (bf16[8,1536]{1,0:T(8,128)(2,1)S(1)}, bf16[8,1536]{1,0:T(8,128)(2,1)S(1)}, u32[]{:S(2)}, u32[]{:S(2)}) collective-permute-start(bf16[8,1536]{1,0:T(8,128)(2,1)S(1)} %slice.339), channel_id=1, source_target_pairs={{0,1},{1,2},{2,3},{3,4},{4,5},{5,6},{6,7},{7,8},{8,9},{9,10},{10,1... | collective-permute-start | bytes 73736 | tf_op jit(solution)/shard_map/ppermute | solution.py:405
  35.2 5.3 copy-start.9
  36.5 57.5 %copy-start.31 = (f32[512]{0:T(512)}, f32[512]{0:T(512)S(1)}, u32[]{:S(2)}) copy-start(f32[512]{0:T(512)S(1)} %slice_convert_fusion.3) | copy-start | bytes 6148
  39.1 54.9 %copy-start.44 = (f32[48]{0:T(128)}, f32[48]{0:T(128)S(1)}, u32[]{:S(2)}) copy-start(f32[48]{0:T(128)S(1)} %convert_exponential_fusion) | copy-start | bytes 580
  39.2 54.8 %copy-start.18 = (f32[1536]{0:T(1024)}, f32[1536]{0:T(1024)S(1)}, u32[]{:S(2)}) copy-start(f32[1536]{0:T(1024)S(1)} %reshape.1020) | copy-start | bytes 18436
  39.2 57.6 %copy-start.37 = (f32[48]{0:T(128)}, f32[48]{0:T(128)S(1)}, u32[]{:S(2)}) copy-start(f32[48]{0:T(128)S(1)} %convert_element_type.220) | copy-start | bytes 580
  40.1 53.9 %copy-start.11 = (bf16[8,1536]{1,0:T(8,128)(2,1)}, bf16[8,1536]{1,0:T(8,128)(2,1)S(1)}, u32[]{:S(2)}) copy-start(bf16[8,1536]{1,0:T(8,128)(2,1)S(1)} %collective-permute-done) | copy-start | bytes 73732
  40.5 53.5 %copy-start.29 = (f32[520]{0:T(1024)}, f32[520]{0:T(1024)S(1)}, u32[]{:S(2)}) copy-start(f32[520]{0:T(1024)S(1)} %add_rsqrt_fusion) | copy-start | bytes 6244
  41.0 53.1 %copy-start.5 = (bf16[520,1536]{1,0:T(8,128)(2,1)}, bf16[520,1536]{1,0:T(8,128)(2,1)S(1)}, u32[]{:S(2)}) copy-start(bf16[520,1536]{1,0:T(8,128)(2,1)S(1)} %multiply_convert_fusion) | copy-start | bytes 4792324
  94.1 1.7 copy-start.2
  98.8 60.8 %copy-start.4 = (f32[512,48]{1,0:T(8,128)}, f32[512,48]{1,0:T(8,128)S(1)}, u32[]{:S(2)}) copy-start(f32[512,48]{1,0:T(8,128)S(1)} %get-tuple-element.95.enter) | copy-start | bytes 294916
  98.9 3.4 copy-start.32
  153.3 81.6 %all-to-all-start = ((bf16[8,128,384]{2,1,0:T(8,128)(2,1)}), bf16[8,128,384]{2,1,0:T(8,128)(2,1)S(1)}, u32[]{:S(2)}, u32[]{:S(2)}) async-start(bf16[8,128,384]{2,1,0:T(8,128)(2,1)} %bitcast.80), calls=%async_computation | async-start | bytes 1572864 | tf_op jit(solution)/shard_map/all_to_all | solution.py:319
  234.8 7.3 copy-start.27
  234.8 8.0 copy-start.21
  234.8 7.9 copy-start.23
  234.8 10.7 %copy-start.16 = (f32[384]{0:T(512)}, f32[384]{0:T(512)S(1)}, u32[]{:S(2)}) copy-start(f32[384]{0:T(512)S(1)} %get-tuple-element.67) | copy-start | bytes 4612
  234.8 11.3 %copy-start.25 = (f32[384]{0:T(512)}, f32[384]{0:T(512)S(1)}, u32[]{:S(2)}) copy-start(f32[384]{0:T(512)S(1)} %get-tuple-element.69) | copy-start | bytes 4612
  246.9 24.4 %all-to-all-start.1 = ((bf16[8,128,384]{2,1,0:T(8,128)(2,1)}), bf16[8,128,384]{2,1,0:T(8,128)(2,1)S(1)}, u32[]{:S(2)}, u32[]{:S(2)}) async-start(bf16[8,128,384]{2,1,0:T(8,128)(2,1)} %fusion.29), calls=%async_computation.1 | async-start | bytes 1572864 | tf_op jit(solution)/shard_map/all_to_all | solution.py:336
  290.2 6.5 copy-start.10
  290.2 6.9 copy-start.30
  290.2 6.9 copy-start.12
  292.3 6.9 copy-start.28
  292.3 24.8 %all-to-all-start.2 = ((bf16[8,128,384]{2,1,0:T(8,128)(2,1)}), bf16[8,128,384]{2,1,0:T(8,128)(2,1)S(1)}, u32[]{:S(2)}, u32[]{:S(2)}) async-start(bf16[8,128,384]{2,1,0:T(8,128)(2,1)} %bitcast.78), calls=%async_computation.2 | async-start | bytes 1572864 | tf_op jit(solution)/shard_map/all_to_all | solution.py:319
  297.1 20.1 %copy-start.17 = (f32[384]{0:T(512)S(1)}, f32[384]{0:T(512)}, u32[]{:S(2)}) copy-start(f32[384]{0:T(512)} %copy-done.16) | copy-start | bytes 4612
  297.1 20.1 %copy-start.22 = (f32[384]{0:T(512)S(1)}, f32[384]{0:T(512)}, u32[]{:S(2)}) copy-start(f32[384]{0:T(512)} %copy-done.21) | copy-start | bytes 4612
  297.1 20.1 %copy-start.24 = (f32[384]{0:T(512)S(1)}, f32[384]{0:T(512)}, u32[]{:S(2)}) copy-start(f32[384]{0:T(512)} %copy-done.23) | copy-start | bytes 4612
  297.1 20.1 %copy-start.26 = (f32[384]{0:T(512)S(1)}, f32[384]{0:T(512)}, u32[]{:S(2)}) copy-start(f32[384]{0:T(512)} %copy-done.25) | copy-start | bytes 4612
  329.0 56.0 %all-to-all-start.3 = ((bf16[8,128,384]{2,1,0:T(8,128)(2,1)}), bf16[8,128,384]{2,1,0:T(8,128)(2,1)S(1)}, u32[]{:S(2)}, u32[]{:S(2)}) async-start(bf16[8,128,384]{2,1,0:T(8,128)(2,1)} %convert_dynamic-update-slice_fusion), calls=%async_computation.3 | async-start | bytes 1572864 | tf_op jit(solution)/shard_map/all_to_all | solution.py:336
  332.7 251.9 %all-reduce.5.cloned.1.call-start = ((), (), s32[]{:S(2)}) async-start(), calls=%async_computation.10 | async-start | bytes 172032 | tf_op jit(solution)/shard_map/psum | solution.py:653
  333.1 41.3 %copy-start.15 = (f32[8,3072]{1,0:T(8,128)S(1)}, f32[8,3072]{1,0:T(8,128)}, u32[]{:S(2)}) copy-start(f32[8,3072]{1,0:T(8,128)} %get-tuple-element.60) | copy-start | bytes 294916
  438.2 2.7 copy-start.14
  438.2 2.8 copy-start.40
  438.2 6.2 copy-start.38
  438.2 6.2 copy-start.45
  440.6 7.4 copy-start.13
  440.6 8.2 copy-start.19
  441.0 7.0 collective-permute-start.1
  448.8 13.3 %copy-start.7 = (bf16[512,1536]{1,0:T(8,128)(2,1)S(1)}, bf16[512,1536]{1,0:T(8,128)(2,1)}, u32[]{:S(2)}) copy-start(bf16[512,1536]{1,0:T(8,128)(2,1)} %param.15) | copy-start | bytes 4718596
  462.0 265.8 %reduce-scatter.8.cloned.1.call-start = ((), (), s32[]{:S(2)}) async-start(), calls=%async_computation.13 | async-start | bytes 9732096 | tf_op jit(solution)/shard_map/reduce_scatter | solution.py:640
  471.7 1.4 copy-start.6
  471.7 397.4 %reduce-scatter.4.cloned.1.call-start = ((), (), s32[]{:S(2)}) async-start(), calls=%async_computation.11 | async-start | bytes 9732096 | tf_op jit(solution)/shard_map/reduce_scatter | solution.py:640
  482.5 533.8 %reduce-scatter.6.cloned.1.call-start = ((), (), s32[]{:S(2)}) async-start(), calls=%async_computation.12 | async-start | bytes 10948608 | tf_op jit(solution)/shard_map/reduce_scatter | solution.py:640
  493.3 10.5 %copy-start.1 = (f32[520,1536]{1,0:T(8,128)S(1)}, f32[520,1536]{1,0:T(8,128)}, u32[]{:S(2)}) copy-start(f32[520,1536]{1,0:T(8,128)} %maximum_convert_fusion) | copy-start | bytes 9584644
  493.3 10.5 %copy-start.3 = (f32[512,1536]{1,0:T(8,128)S(1)}, f32[512,1536]{1,0:T(8,128)}, u32[]{:S(2)}) copy-start(f32[512,1536]{1,0:T(8,128)} %get-tuple-element.117) | copy-start | bytes 9437188
  493.3 10.5 %copy-start.8 = (bf16[512,1536]{1,0:T(8,128)(2,1)S(1)}, bf16[512,1536]{1,0:T(8,128)(2,1)}, u32[]{:S(2)}) copy-start(bf16[512,1536]{1,0:T(8,128)(2,1)} %param.15) | copy-start | bytes 4718596
Sparse Core Ops, SparseCore 0:
  10.8 72.8 all-gather.5
  85.3 64.0 all-gather.7
  151.0 64.2 all-gather.9
  462.1 122.4 all-reduce.4
  590.4 137.4 reduce-scatter.7
  734.6 134.4 reduce-scatter.3
  875.2 141.1 reduce-scatter.5

commit v2 on v1

v2 whole, which is shorter than its diff:
```python
import jax
import jax.numpy as jnp
from jax import lax
from jax.experimental import pallas as pl
from jax.experimental.pallas import tpu as pltpu
from jax.sharding import PartitionSpec as P

HEAD_DIM = 64
CONV = 4
EPS = 1e-05
HALO = 8
GROUP = 4
WIDE = GROUP * HEAD_DIM
TILE = 128
HIGH = lax.Precision.HIGHEST
ALL = ("shard", "seq")
f32 = jnp.float32
bf16 = jnp.bfloat16


def mm(a, b):
    return jnp.dot(a, b, preferred_element_type=f32)


def mm_nt(a, b):
    return lax.dot_general(a, b, (((1,), (1,)), ((), ())), preferred_element_type=f32)


def mm_tn(a, b):
    return lax.dot_general(a, b, (((0,), (0,)), ((), ())), preferred_element_type=f32)


def sigmoid(value):
    return 0.5 * jnp.tanh(0.5 * value) + 0.5


def group_columns(value, group):
    lanes = value.shape[1]
    return pltpu.roll(value, lax.rem(lanes - GROUP * group, lanes), 1)


def spread(columns):
    rows = columns.shape[0]
    lane = lax.broadcasted_iota(jnp.int32, (rows, 2 * HEAD_DIM), 1)
    out = []
    for pair in range(GROUP // 2):
        low = columns[:, 2 * pair : 2 * pair + 1]
        top = columns[:, 2 * pair + 1 : 2 * pair + 2]
        out.append(jnp.where(lane < HEAD_DIM, low, top))
    return jnp.concatenate(out, axis=1)


def conv_rows(wide, taps, masks, start, rows):
    pre = taps[CONV : CONV + 1, :] + taps[CONV - 1 : CONV, :] * wide[pl.ds(HALO + start, rows), :]
    for tap in range(CONV - 1):
        shifted = wide[pl.ds(HALO - CONV + 1 + tap + start, rows), :]
        pre = pre + taps[tap : tap + 1, :] * shifted * masks[pl.ds(start, rows), tap : tap + 1]
    return pre


def prepare_kernel(edge, rates, masks, out, row_out):
    length = out.shape[1]
    shifted = edge[...].astype(f32) + rates[0:1, :]
    step = jax.nn.softplus(shifted)
    here = lax.broadcasted_iota(jnp.int32, (length, length), 0)
    there = lax.broadcasted_iota(jnp.int32, (length, length), 1)
    lower = jnp.where(here >= there, 1.0, 0.0)
    log_decay = -step * jnp.exp(rates[1:2, :])
    cum = lax.dot_general(
        lower, log_decay, (((1,), (0,)), ((), ())), precision=HIGH, preferred_element_type=f32
    )
    out[0] = cum
    out[1] = step
    out[2] = jnp.exp(cum[length - 1 : length, :] - cum) * masks[:, 8:9]
    out[3] = jnp.exp(cum) * masks[:, 7:8]
    out[4] = sigmoid(shifted)
    turned = cum.T
    for group in range(row_out.shape[0]):
        row_out[group] = turned[GROUP * group : GROUP * (group + 1), :]


def state_kernel(raw, raw_bc, taps, masks, heads, x_out, state_out, bc_out, bt_out, ct_out, wide, bt):
    length = x_out.shape[0]
    n_state = bt.shape[0]
    step = pl.program_id(0)

    @pl.when(step == 0)
    def _():
        wide[...] = raw_bc[...].astype(f32)
        for start in range(0, length, TILE):
            rows = pl.ds(start, TILE)
            pre = conv_rows(wide, taps, masks, start, TILE)
            both = pre * sigmoid(pre)
            bc_out[rows, :] = both.astype(bf16)
            turned = both[:, :n_state].T.astype(bf16)
            bt[:, rows] = turned
            bt_out[:, rows] = turned
            ct_out[:, rows] = both[:, n_state:].T.astype(bf16)

    @pl.when(step > 0)
    def _():
        wide[...] = raw[...].astype(f32)
        kept = []
        for start in range(0, length, TILE):
            rows = pl.ds(start, TILE)
            pre = conv_rows(wide, taps, masks, start, TILE)
            x = (pre * sigmoid(pre)).astype(bf16)
            x_out[rows, :] = x
            stepped = spread(group_columns(heads[1, rows, :], step - 1))
            scaled = (x.astype(f32) * stepped).astype(bf16)
            keep = spread(group_columns(heads[2, rows, :], step - 1))
            kept.append((scaled.astype(f32) * keep).astype(bf16))
        state_out[...] = mm(bt[...], jnp.concatenate(kept, 0)).astype(bf16)


def scored(first, second, masks, seg_row, score, later):
    length = score.shape[0]
    for start in range(0, length, TILE):
        rows = pl.ds(start, TILE)
        product = mm(first(rows), second[...])
        here = lax.broadcasted_iota(jnp.int32, (TILE, length), 0) + start
        there = lax.broadcasted_iota(jnp.int32, (TILE, length), 1)
        order = (here >= there) if later else (here <= there)
        seen = (masks[rows, 6:7] == seg_row[0:1, :]) & order
        score[rows, :] = jnp.where(seen, product, 0.0)


def scale_by_step(x_in, heads, xs, group):
    for start in range(0, x_in.shape[0], TILE):
        rows = pl.ds(start, TILE)
        stepped = spread(group_columns(heads[1, rows, :], group))
        xs[rows, :] = (x_in[rows, :].astype(f32) * stepped).astype(bf16)


def forward_kernel(x_in, masks, seg_row, heads, sums_row, bc, bt, y_out, score, xs, weights):
    length = y_out.shape[0]
    n_state = bt.shape[0]
    group = pl.program_id(0)
    big = 2 * TILE

    @pl.when(group == 0)
    def _():
        scored(lambda rows: bc[rows, n_state:], bt, masks, seg_row, score, True)
        weights[...] = jnp.zeros_like(weights)

    scale_by_step(x_in, heads, xs, group)
    columns = [group_columns(heads[0, pl.ds(at, TILE), :], group) for at in range(0, length, TILE)]
    for head in range(GROUP):
        lanes = slice(head * HEAD_DIM, (head + 1) * HEAD_DIM)
        for start in range(0, length, TILE):
            rows = pl.ds(start, TILE)
            seen = start + TILE
            gap = columns[start // TILE][:, head : head + 1] - sums_row[0, head : head + 1, :seen]
            weight = jnp.exp(jnp.minimum(gap, 0.0)) * score[rows, :seen]
            weights[rows, :seen] = weight.astype(bf16)
        for cut in range(0, length, big):
            part = mm(weights[cut:, cut : cut + big], xs[cut : cut + big, lanes])
            if cut == 0:
                y_out[:, lanes] = part
            else:
                y_out[cut:, lanes] += part


def gate_kernel(
    y_in, x_in, z_in, dn_in, bc, ct, enter, state, gain, ssm_out, norm_out, dz_out, dy_out,
    ds_out, dc_out, dg_out, gated_s, sig_s, mo_s, ds_acc
):
    rows = y_in.shape[0]
    width = y_in.shape[1]
    n_state = state.shape[0]
    step = pl.program_id(0)
    lane = lax.broadcasted_iota(jnp.int32, (rows, 2 * HEAD_DIM), 1)
    c_mat = bc[:, n_state:]

    @pl.when(step == 0)
    def _():
        ds_acc[...] = jnp.zeros_like(ds_acc)
        dg_out[...] = jnp.zeros_like(dg_out)

    def entering(block):
        low = enter[:, 2 * block : 2 * block + 1]
        top = enter[:, 2 * block + 1 : 2 * block + 2]
        return jnp.where(lane < HEAD_DIM, low, top)

    square = jnp.zeros((rows, 2 * HEAD_DIM), f32)
    cross = jnp.zeros((rows, 2 * HEAD_DIM), f32)
    for block in range(width // (2 * HEAD_DIM)):
        lanes = slice(block * 2 * HEAD_DIM, (block + 1) * 2 * HEAD_DIM)
        ssm = y_in[:, lanes] + entering(block) * mm(c_mat, state[:, lanes])
        ssm_out[:, lanes] = ssm
        mo = (ssm + gain[1:2, lanes] * x_in[:, lanes].astype(f32)).astype(bf16)
        mo_s[:, lanes] = mo
        z = z_in[:, lanes].astype(f32)
        sig = sigmoid(z)
        gated = mo.astype(f32) * (z * sig)
        gated_s[:, lanes] = gated
        sig_s[:, lanes] = sig
        square = square + gated * gated
        cross = cross + gated * (dn_in[:, lanes] * gain[0:1, lanes])
    scale = lax.rsqrt(jnp.sum(square, axis=1, keepdims=True) * (1.0 / width) + EPS)
    pull = scale * scale * scale * (jnp.sum(cross, axis=1, keepdims=True) * (1.0 / width))
    dc = jnp.zeros((rows, n_state), f32)
    for block in range(width // (2 * HEAD_DIM)):
        lanes = slice(block * 2 * HEAD_DIM, (block + 1) * 2 * HEAD_DIM)
        gated = gated_s[:, lanes]
        sig = sig_s[:, lanes]
        silu = z_in[:, lanes].astype(f32) * sig
        dn = dn_in[:, lanes]
        hat = gated * scale
        norm_out[:, lanes] = (hat * gain[0:1, lanes]).astype(bf16)
        part = dn * hat
        total = part[0:8, :]
        for at in range(8, rows, 8):
            total = total + part[at : at + 8, :]
        dg_out[:, lanes] += total
        d_gated = scale * (dn * gain[0:1, lanes]) - gated * pull
        dy = (d_gated * silu).astype(bf16)
        dy_out[:, lanes] = dy
        mo = mo_s[:, lanes].astype(f32)
        dz_out[:, lanes] = (d_gated * mo * (sig + silu * (1.0 - sig))).astype(bf16)
        weighted = (dy.astype(f32) * entering(block)).astype(bf16)
        ds_acc[:, lanes] += mm(ct[...], weighted)
        dc = dc + mm_nt(weighted, state[:, lanes])
    dc_out[...] = dc

    @pl.when(step == pl.num_programs(0) - 1)
    def _():
        ds_out[...] = ds_acc[...].astype(bf16)


def inside_kernel(
    x_in, masks, seg_row, heads, sums_row, bc, ct, dy, dxs_out, db_out, dc_out, score, pair, xs,
    weights, crossed
):
    length = dxs_out.shape[0]
    n_state = ct.shape[0]
    group = pl.program_id(0)
    big = 2 * TILE

    @pl.when(group == 0)
    def _():
        pair[...] = jnp.zeros_like(pair)
        weights[...] = jnp.zeros_like(weights)
        scored(lambda rows: bc[rows, :n_state], ct, masks, seg_row, score, False)

    scale_by_step(x_in, heads, xs, group)
    columns = [group_columns(heads[0, pl.ds(at, TILE), :], group) for at in range(0, length, TILE)]
    for head in range(GROUP):
        lanes = slice(head * HEAD_DIM, (head + 1) * HEAD_DIM)
        for cut in range(0, length, big):
            stop = cut + big
            crossed[:stop, cut:stop] = mm_nt(xs[:stop, lanes], dy[cut:stop, lanes])
        for start in range(0, length, TILE):
            rows = pl.ds(start, TILE)
            gap = sums_row[0, head : head + 1, start:] - columns[start // TILE][:, head : head + 1]
            decay = jnp.exp(jnp.minimum(gap, 0.0))
            weights[rows, start:] = (decay * score[rows, start:]).astype(bf16)
            pair[rows, start:] += decay * crossed[rows, start:]
        for cut in range(length - big, -1, -big):
            stop = cut + big
            part = mm(weights[:stop, cut:stop], dy[cut:stop, lanes])
            if stop == length:
                dxs_out[:, lanes] = part
            else:
                dxs_out[:stop, lanes] += part

    @pl.when(group == pl.num_programs(0) - 1)
    def _():
        for start in range(0, length, TILE):
            rows = pl.ds(start, TILE)
            here = lax.broadcasted_iota(jnp.int32, (TILE, length), 0) + start
            there = lax.broadcasted_iota(jnp.int32, (TILE, length), 1)
            seen = (masks[rows, 6:7] == seg_row[0:1, :]) & (here <= there)
            part = jnp.where(seen, pair[rows, :], 0.0).astype(bf16)
            db_out[rows, :] = mm(part, bc[:, n_state:])
            if start == 0:
                dc_out[...] = mm_tn(part, bc[rows, :n_state])
            else:
                dc_out[...] += mm_tn(part, bc[rows, :n_state])


def split_mm(value, chosen):
    high = value.astype(bf16)
    low = (value - high.astype(f32)).astype(bf16)
    return mm(high, chosen) + mm(low, chosen)


def outside_kernel(
    raw, raw_bc, taps, masks, heads, rates, bc, dy, ssm, dxs_in, d_state, state, db_in, dc_in,
    dc_more, d_out, first_out, last_out, sums_out, head_out, wide, d_pre, db_acc, found, totals_s
):
    length = d_out.shape[0]
    n_state = bc.shape[1] // 2
    step = pl.program_id(0)
    bc_step = pl.num_programs(0) - 2

    @pl.when(step == 0)
    def _():
        db_acc[...] = jnp.zeros_like(db_acc)
        found[...] = jnp.zeros_like(found)
        totals_s[...] = jnp.zeros_like(totals_s)

    d_pre[pl.ds(length, HALO), :] = jnp.zeros((HALO, d_pre.shape[1]), f32)
    zero = jnp.zeros((1, d_pre.shape[1]), f32)

    @pl.when(step < bc_step)
    def _():
        wide[...] = raw[...].astype(f32)
        skip_sum, keep_sum = (zero, zero)
        ds = d_state[...]
        owner = lax.broadcasted_iota(jnp.int32, (WIDE, TILE), 0) // HEAD_DIM + GROUP * step
        chosen = (owner == lax.broadcasted_iota(jnp.int32, (WIDE, TILE), 1)).astype(f32)
        chosen_b = chosen.astype(bf16)
        for start in range(0, length, TILE):
            rows = pl.ds(start, TILE)
            pre = conv_rows(wide, taps, masks, start, TILE)
            sig = sigmoid(pre)
            x = pre * sig
            stepped = spread(group_columns(heads[1, rows, :], step))
            scaled = (x.astype(bf16).astype(f32) * stepped).astype(bf16)
            keep = spread(group_columns(heads[2, rows, :], step))
            carried = keep * mm(bc[rows, :n_state], ds)
            dxs = dxs_in[rows, :] + carried
            scaled = scaled.astype(f32)
            db_acc[rows, :] += mm_nt((scaled * keep).astype(bf16), ds)
            grad = dy[rows, :].astype(f32)
            keep_sum = keep_sum + jnp.sum(scaled * carried, 0, keepdims=True)
            skip_sum = skip_sum + jnp.sum(grad * x, 0, keepdims=True)
            found[0, rows, :] += split_mm(grad * ssm[rows, :] - scaled * dxs, chosen_b)
            found[1, rows, :] += split_mm(x * dxs, chosen_b)
            d_x = taps[5:6, :] * grad + stepped * dxs
            d_pre[rows, :] = d_x * (sig + x * (1.0 - sig))
        met = jnp.sum(ds.astype(f32) * state[...].astype(f32), 0, keepdims=True)
        rest = jnp.zeros((5, WIDE), f32)
        totals_s[...] += lax.dot_general(
            jnp.concatenate([skip_sum, keep_sum, met, rest], 0),
            chosen,
            (((1,), (0,)), ((), ())),
            precision=HIGH,
            preferred_element_type=f32,
        )

    @pl.when(step == bc_step)
    def _():
        wide[...] = raw_bc[...].astype(f32)
        for start in range(0, length, TILE):
            rows = pl.ds(start, TILE)
            pre = conv_rows(wide, taps, masks, start, TILE)
            sig = sigmoid(pre)
            slope = sig + pre * sig * (1.0 - sig)
            d_b = db_in[rows, :] + db_acc[rows, :]
            d_c = dc_in[rows, :] + dc_more[rows, :]
            d_pre[rows, :] = jnp.concatenate([d_b, d_c], 1) * slope

    @pl.when(step <= bc_step)
    def _():
        totals = [zero] * (CONV + 1)
        for start in range(0, length, TILE):
            rows = pl.ds(start, TILE)
            grad = d_pre[rows, :]
            totals[CONV] = totals[CONV] + jnp.sum(grad, 0, keepdims=True)
            here = wide[pl.ds(HALO + start, TILE), :]
            totals[CONV - 1] = totals[CONV - 1] + jnp.sum(grad * here, 0, keepdims=True)
            back = taps[CONV - 1 : CONV, :] * grad
            for tap in range(CONV - 1):
                shifted = wide[pl.ds(HALO - CONV + 1 + tap + start, TILE), :]
                masked = grad * masks[rows, tap : tap + 1]
                totals[tap] = totals[tap] + jnp.sum(masked * shifted, 0, keepdims=True)
                ahead = d_pre[pl.ds(start + CONV - 1 - tap, TILE), :]
                back = back + taps[tap : tap + 1, :] * ahead * masks[rows, 3 + tap : 4 + tap]
            d_out[rows, :] = back.astype(bf16)
            if start + TILE == length:
                last_out[...] = back[TILE - HALO :, :]
        first_out[...] = d_pre[pl.ds(0, HALO), :]
        for tap in range(CONV + 1):
            sums_out[tap : tap + 1, :] = totals[tap]
        sums_out[CONV + 1 : 8, :] = jnp.zeros((7 - CONV, d_pre.shape[1]), f32)

    @pl.when(step == bc_step + 1)
    def _():
        first_out[...] = jnp.zeros_like(first_out)
        last_out[...] = jnp.zeros_like(last_out)
        sums_out[...] = jnp.zeros_like(sums_out)
        rate = jnp.exp(rates[1:2, :])
        end = totals_s[1:2, :] + heads[3, pl.ds(length - 1, 1), :] * totals_s[2:3, :]
        here = lax.broadcasted_iota(jnp.int32, (length, length), 0)
        there = lax.broadcasted_iota(jnp.int32, (length, length), 1)
        upper = jnp.where(here <= there, 1.0, 0.0)
        d_log = lax.dot_general(
            upper, found[0], (((1,), (0,)), ((), ())), precision=HIGH, preferred_element_type=f32
        )
        d_log = d_log + end
        d_dt = (found[1] - rate * d_log) * heads[4]
        d_out[:, :TILE] = d_dt.astype(bf16)
        d_out[:, TILE:] = jnp.zeros((length, WIDE - TILE), bf16)
        head_out[0:1, :] = jnp.sum(d_dt, 0, keepdims=True)
        head_out[1:2, :] = jnp.sum(d_log * (-heads[1] * rate), 0, keepdims=True)
        head_out[2:3, :] = totals_s[0:1, :]
        head_out[3:8, :] = jnp.zeros((5, TILE), f32)


def pack_kernel(sizes, sums, gain_in, gain_out, head, out):
    devices = out.shape[0]
    wide, channels, inner, heads = sizes
    gains = jnp.sum(gain_out[...], 0, keepdims=True)
    for at in range(devices):
        pieces = [gain_in[:, at * wide : (at + 1) * wide]]
        for tap in range(CONV + 1):
            pieces.append(sums[tap : tap + 1, at * channels : (at + 1) * channels])
        pieces.append(gains[:, at * inner : (at + 1) * inner])
        for row in range(3):
            pieces.append(head[row : row + 1, :heads])
        begin = 0
        for piece in pieces:
            out[at, :, begin : begin + piece.shape[1]] = piece
            begin += piece.shape[1]
        if begin < out.shape[2]:
            out[at, :, begin:] = jnp.zeros((1, out.shape[2] - begin), f32)


def scan_kernel(backward, mine, decay, out):
    count = mine.shape[0]

    def one(index, state):
        at = count - 1 - index if backward else index
        out[at] = state.astype(bf16)
        return decay[pl.ds(at, 1), :] * state + mine[at].astype(f32)

    lax.fori_loop(0, count, one, jnp.zeros(mine.shape[1:], f32))


def to_slices(value, devices):
    n_state, inner = value.shape
    across = max(1, devices // 16)
    rows = n_state * across // devices
    value = value.reshape(n_state // rows, rows, across, inner // across)
    return value.transpose(0, 2, 1, 3).reshape(devices, rows, inner // across)


def from_slices(slices, n_state, inner):
    devices, rows, columns = slices.shape
    value = slices.reshape(n_state // rows, inner // columns, rows, columns)
    return value.transpose(0, 2, 1, 3).reshape(n_state, inner)


def send_slices(local, devices):
    return lax.all_to_all(to_slices(local, devices), ALL, split_axis=0, concat_axis=0, tiled=True)


def return_slices(states, n_state, inner):
    back = lax.all_to_all(states, ALL, split_axis=0, concat_axis=0, tiled=True)
    return from_slices(back, n_state, inner)


def scan_devices(mine, decay, me, backward):
    devices, heads = decay.shape
    across = max(1, devices // 16)
    wide = jnp.repeat(decay, HEAD_DIM, axis=1).reshape(devices, across, heads * HEAD_DIM // across)
    wide = lax.dynamic_index_in_dim(wide, me % across, 1, False)
    return pl.pallas_call(
        lambda *refs: scan_kernel(backward, *refs),
        out_shape=jax.ShapeDtypeStruct(mine.shape, bf16),
        name="scan_backward" if backward else "scan_forward",
    )(mine, wide)


def flip(axis, bit):
    count = lax.axis_size(axis)
    return [(i, i ^ bit) for i in range(count)]


def other_core(value):
    return lax.ppermute(value, "shard", flip("shard", 1))


class Gather:
    def __init__(self, own, other, base, size, chunks):
        self.own, self.other, self.base, self.size = (own, other, base, size)
        self.other_base = base
        self.mine = lax.axis_index("seq") % 2
        self.blocks = []
        for chunk in range(chunks):
            self.blocks += [2 * chunk + self.mine, 2 * chunk + 1 - self.mine]
        self.direct = [None] * chunks
        self.parts = [None] * (2 * chunks)

    def fetch(self, chunk, *wait):
        start = self.base + (2 * chunk + self.mine) * self.size
        send = lax.dynamic_slice_in_dim(self.own, start, self.size, 0)
        if wait:
            send = after(send, *wait)
        self.direct[chunk] = lax.ppermute(send, "shard", flip("shard", 2))

    def share(self, chunk, *wait):
        direct = self.direct[chunk]
        if wait:
            direct = after(direct, *wait)
        passed = lax.ppermute(direct, "seq", flip("seq", 1))
        self.parts[2 * chunk] = (direct, other_core(direct))
        self.parts[2 * chunk + 1] = (passed, other_core(passed))


def project_kernel(table, a0, a1, a2, a3, w0, w1, w2, w3, *rest):
    left = rest[-1]
    out = rest[-2]

    @pl.when(pl.program_id(0) == 0)
    def _():
        left[...] = jnp.concatenate([a0[...], a1[...], a2[...], a3[...]], 1)

    weight = jnp.concatenate([w0[...], w1[...], w2[...], w3[...]], 1)
    out[...] = mm_nt(left[...], weight).astype(bf16)


def project(value, gather, number, shard, result):
    rows = value.shape[0]
    deep = gather.own.shape[1]
    steps = gather.size // WIDE
    first = gather.blocks[number] * steps
    table = jnp.stack([shard, shard ^ 1, shard ^ 2, shard ^ 3, first]).astype(jnp.int32)
    base = gather.base // WIDE
    a_spec = lambda k: pl.BlockSpec((rows, deep), lambda j, t: (0, t[k]))
    other_base = gather.other_base // WIDE
    near = pl.BlockSpec((WIDE, deep), lambda j, t: (base + t[4] + j, 0))
    near_other = pl.BlockSpec((WIDE, deep), lambda j, t: (other_base + t[4] + j, 0))
    far = pl.BlockSpec((WIDE, deep), lambda j, t: (j, 0))
    columns = len(gather.blocks) * gather.size
    direct, crossed = gather.parts[number]
    operands = [table, value, value, value, value, gather.own, gather.other, direct, crossed]
    in_specs = [a_spec(k) for k in range(4)] + [near, near_other, far, far]
    aliases = {}
    if result is not None:
        operands.append(result)
        in_specs.append(pl.BlockSpec(memory_space=pl.ANY))
        aliases = {len(operands) - 1: 0}
    return pl.pallas_call(
        project_kernel,
        grid_spec=pltpu.PrefetchScalarGridSpec(
            num_scalar_prefetch=1,
            grid=(steps,),
            in_specs=in_specs,
            out_specs=pl.BlockSpec((rows, WIDE), lambda j, t: (0, t[4] + j)),
            scratch_shapes=[pltpu.VMEM((rows, 4 * deep), bf16)],
        ),
        out_shape=jax.ShapeDtypeStruct((rows, columns), bf16),
        input_output_aliases=aliases,
        compiler_params=pltpu.CompilerParams(vmem_limit_bytes=40 * 1024 * 1024),
        cost_estimate=pl.CostEstimate(
            flops=8 * rows * deep * gather.size, bytes_accessed=8 * deep * gather.size, transcendentals=0
        ),
        name="project",
    )(*operands)


def back_kernel(count, extra, table, d, own, other, *rest):
    pieces = rest[: 2 * count]
    rest = rest[2 * count :]
    step = pl.program_id(0)
    out, total = rest[-2:]
    deep = own.shape[1]

    @pl.when(step == 0)
    def _():
        for k in range(4):
            if extra:
                total[k] = mm(rest[0][...], rest[1 + k][...])
            else:
                total[k] = jnp.zeros(total.shape[1:], f32)

    value = d[...]
    total[0] += mm(value, own[...])
    total[1] += mm(value, other[...])
    for number in range(count):

        @pl.when(step == number)
        def _(number=number):
            total[2] += mm(value, pieces[2 * number][...])
            total[3] += mm(value, pieces[2 * number + 1][...])

    @pl.when(step == count - 1)
    def _():
        for k in range(4):
            at = pl.multiple_of(table[count + k] * deep, deep)
            out[:, pl.ds(at, deep)] = total[k]


def back(value, gather, shard, extra=()):
    rows = value.shape[0]
    deep = gather.own.shape[1]
    count = len(gather.blocks)
    size = gather.size
    base = gather.base // size
    table = jnp.stack(gather.blocks + [shard, shard ^ 1, shard ^ 2, shard ^ 3]).astype(jnp.int32)
    fixed = lambda shape: pl.BlockSpec(shape, lambda g, t: (0, 0))
    other_base = gather.other_base // size
    near = pl.BlockSpec((size, deep), lambda g, t: (base + t[g], 0))
    near_other = pl.BlockSpec((size, deep), lambda g, t: (other_base + t[g], 0))
    operands = [table, value, gather.own, gather.other]
    in_specs = [pl.BlockSpec((rows, size), lambda g, t: (0, t[g])), near, near_other]
    for part in gather.parts:
        operands += list(part)
        in_specs += [fixed((size, deep))] * 2
    operands += list(extra)
    in_specs += [fixed(e.shape) for e in extra]
    return pl.pallas_call(
        lambda *refs: back_kernel(count, len(extra) > 0, *refs),
        grid_spec=pltpu.PrefetchScalarGridSpec(
            num_scalar_prefetch=1,
            grid=(count,),
            in_specs=in_specs,
            out_specs=fixed((rows, 4 * deep)),
            scratch_shapes=[pltpu.VMEM((4, rows, deep), f32)],
        ),
        out_shape=jax.ShapeDtypeStruct((rows, 4 * deep), f32),
        compiler_params=pltpu.CompilerParams(vmem_limit_bytes=56 * 1024 * 1024),
        cost_estimate=pl.CostEstimate(
            flops=8 * rows * deep * size * count, bytes_accessed=8 * deep * size * count, transcendentals=0
        ),
        name="back",
    )(*operands)


def stacked_project_kernel(value, *rest):
    weight = jnp.concatenate([w[...] for w in rest[:-1]], 1)
    rest[-1][...] = mm_nt(value[...], weight).astype(bf16)


def stacked_project(value, stack, base, count):
    rows = value.shape[0]
    shards, _, deep = stack.shape
    first = base // WIDE
    specs = [
        pl.BlockSpec((None, WIDE, deep), lambda j, k=k: (k, first + j, 0)) for k in range(shards)
    ]
    return pl.pallas_call(
        stacked_project_kernel,
        grid=(count // WIDE,),
        in_specs=[pl.BlockSpec((rows, shards * deep), lambda j: (0, 0))] + specs,
        out_specs=pl.BlockSpec((rows, WIDE), lambda j: (0, j)),
        out_shape=jax.ShapeDtypeStruct((rows, count), bf16),
        compiler_params=pltpu.CompilerParams(vmem_limit_bytes=40 * 1024 * 1024),
        cost_estimate=pl.CostEstimate(
            flops=2 * rows * shards * deep * count,
            bytes_accessed=2 * shards * deep * count,
            transcendentals=0,
        ),
        name="stacked_project",
    )(value, *([stack] * shards))


def stacked_back_kernel(value, *rest):
    out, total = rest[-2:]
    step = pl.program_id(0)

    @pl.when(step == 0)
    def _():
        total[...] = jnp.zeros_like(total)

    weight = jnp.concatenate([w[...] for w in rest[:-2]], 1)
    total[...] += mm(value[...], weight)

    @pl.when(step == pl.num_programs(0) - 1)
    def _():
        out[...] = total[...]


def stacked_back(value, stack, base):
    rows, count = value.shape
    shards, _, deep = stack.shape
    size = 2 * WIDE
    first = base // size
    specs = [
        pl.BlockSpec((None, size, deep), lambda j, k=k: (k, first + j, 0)) for k in range(shards)
    ]
    return pl.pallas_call(
        stacked_back_kernel,
        grid=(count // size,),
        in_specs=[pl.BlockSpec((rows, size), lambda j: (0, j))] + specs,
        out_specs=pl.BlockSpec((rows, shards * deep), lambda j: (0, 0)),
        out_shape=jax.ShapeDtypeStruct((rows, shards * deep), f32),
        scratch_shapes=[pltpu.VMEM((rows, shards * deep), f32)],
        compiler_params=pltpu.CompilerParams(vmem_limit_bytes=40 * 1024 * 1024),
        cost_estimate=pl.CostEstimate(
            flops=2 * rows * shards * deep * count,
            bytes_accessed=2 * shards * deep * count,
            transcendentals=0,
        ),
        name="stacked_back",
    )(value, *([stack] * shards))


def rows_of(gather):
    shard = lax.axis_index("shard")
    direct, passed = gather.parts
    own = 2 * shard
    return [
        (gather.own, own, 2),
        (gather.other, own ^ 2, 2),
        (direct[0], (own ^ 4) + gather.blocks[0], 1),
        (direct[1], (own ^ 6) + gather.blocks[0], 1),
        (passed[0], (own ^ 4) + gather.blocks[1], 1),
        (passed[1], (own ^ 6) + gather.blocks[1], 1),
    ]


def out_specs_of(gather):
    width = gather.own.shape[1]
    size = gather.size
    operands, specs, owners, table = ([], [], [], [])
    for piece, block, count in rows_of(gather):
        begin = len(table)
        for at in range(count):
            owners.append(len(operands))
            table.append(block + at)
        operands.append(piece)
        specs.append(
            pl.BlockSpec(
                (size, width),
                lambda g, t, begin=begin, count=count: (jnp.clip(g - begin, 0, count - 1), 0),
            )
        )
    return operands, specs, owners, jnp.stack(table).astype(jnp.int32)


def out_back_kernel(owners, table, value, *rest):
    step = pl.program_id(0)
    out = rest[-1]
    for at, owner in enumerate(owners):

        @pl.when(step == at)
        def _(owner=owner):
            out[...] = mm_nt(value[...], rest[owner][...])


def out_back(value, gather):
    rows, width = value.shape
    operands, specs, owners, table = out_specs_of(gather)
    size = gather.size
    return pl.pallas_call(
        lambda *refs: out_back_kernel(owners, *refs),
        grid_spec=pltpu.PrefetchScalarGridSpec(
            num_scalar_prefetch=1,
            grid=(len(owners),),
            in_specs=[pl.BlockSpec((rows, width), lambda g, t: (0, 0))] + specs,
            out_specs=pl.BlockSpec((rows, size), lambda g, t: (0, t[g])),
        ),
        out_shape=jax.ShapeDtypeStruct((rows, len(owners) * size), f32),
        compiler_params=pltpu.CompilerParams(vmem_limit_bytes=56 * 1024 * 1024),
        cost_estimate=pl.CostEstimate(
            flops=16 * rows * width * size, bytes_accessed=16 * width * size, transcendentals=0
        ),
        name="out_back",
    )(table, value, *operands)


def out_forward_kernel(owners, table, value, base, *rest):
    step = pl.program_id(0)
    out, total = rest[-2:]

    @pl.when(step == 0)
    def _():
        total[...] = base[...].astype(f32)

    for at, owner in enumerate(owners):

        @pl.when(step == at)
        def _(owner=owner):
            total[...] += mm(value[...], rest[owner][...])

    @pl.when(step == len(owners) - 1)
    def _():
        out[...] = total[...].astype(bf16)


def out_forward(value, base, gather):
    rows = value.shape[0]
    operands, specs, owners, table = out_specs_of(gather)
    size = gather.size
    width = gather.own.shape[1]
    fixed = pl.BlockSpec((rows, width), lambda g, t: (0, 0))
    return pl.pallas_call(
        lambda *refs: out_forward_kernel(owners, *refs),
        grid_spec=pltpu.PrefetchScalarGridSpec(
            num_scalar_prefetch=1,
            grid=(len(owners),),
            in_specs=[pl.BlockSpec((rows, size), lambda g, t: (0, t[g])), fixed] + specs,
            out_specs=fixed,
            scratch_shapes=[pltpu.VMEM((rows, width), f32)],
        ),
        out_shape=jax.ShapeDtypeStruct((rows, width), bf16),
        compiler_params=pltpu.CompilerParams(vmem_limit_bytes=56 * 1024 * 1024),
        cost_estimate=pl.CostEstimate(
            flops=16 * rows * width * size, bytes_accessed=16 * width * size, transcendentals=0
        ),
        name="out_forward",
    )(table, value, base, *operands)


def halve(value, dim, axis, bit, mine):
    shape = value.shape
    value = value.reshape(shape[:dim] + (shape[dim] // 2, 2) + shape[dim + 1 :])
    send = lax.dynamic_index_in_dim(value, 1 - mine, dim + 1, False)
    kept = lax.dynamic_index_in_dim(value, mine, dim + 1, False)
    came = lax.ppermute(send, axis, flip(axis, bit))
    return (kept.astype(f32) + came.astype(f32)).astype(bf16)


class RowSum:
    def __init__(self, partial, far_first):
        shards, places = (lax.axis_size("shard"), lax.axis_size("seq"))
        shard, place = (lax.axis_index("shard"), lax.axis_index("seq"))
        rows, columns = partial.shape
        chips = shards // 2
        self.value = partial.reshape(chips, places, rows // (chips * places), columns)
        far = [(0, "shard", 2 << k, (shard >> (k + 1)) & 1) for k in range(chips.bit_length() - 1)]
        near = [(1, "seq", 1 << k, (place >> k) & 1) for k in range(places.bit_length() - 1)]
        self.order = far + near if far_first else near[:1] + far + near[1:]

    def step(self, *wait):
        if not self.order:
            return
        dim, axis, bit, mine = self.order.pop(0)
        value = after(self.value, *wait) if wait else self.value
        self.value = halve(value, dim, axis, bit, mine)

    def rows(self):
        return self.value.reshape(self.value.shape[2:])


def core_rows(value, core):
    shards = lax.axis_size("shard")
    size = value.shape[1] // shards
    even = [value[:, at * size : (at + 1) * size] for at in range(0, shards, 2)]
    odd = [value[:, at * size : (at + 1) * size] for at in range(1, shards, 2)]
    own = [jnp.where(core == 0, a, b) for a, b in zip(even, odd)]
    rest = [jnp.where(core == 0, b, a) for a, b in zip(even, odd)]
    return jnp.concatenate(own, 1), jnp.concatenate(rest, 1)


def after(value, *others):
    return lax.optimization_barrier((value,) + others)[0]


def turn_blocks(value, shard):
    shards = lax.axis_size("shard")
    size = value.shape[1] // shards
    blocks = [
        lax.dynamic_slice_in_dim(value, (at ^ shard) * size, size, 1) for at in range(shards)
    ]
    return jnp.concatenate(blocks, 1)


def on_device(
    hidden,
    cotangent,
    seg_ids,
    norm_gain,
    in_weight,
    conv_weight,
    conv_bias,
    dt_bias,
    a_log,
    d_skip,
    out_gain,
    out_weight,
):
    shards, places = (lax.axis_size("shard"), lax.axis_size("seq"))
    shard, place = (lax.axis_index("shard"), lax.axis_index("seq"))
    devices = shards * places
    me = shard * places + place
    length, width = hidden.shape
    heads = dt_bias.shape[0]
    inner = out_weight.shape[0] * shards
    channels = conv_bias.shape[0] * shards
    n_state = (channels - inner) // 2
    groups = inner // WIDE
    start = me * length

    small = jnp.concatenate(
        [norm_gain, conv_weight.reshape(-1), conv_bias, out_gain]
    )
    small = jnp.pad(small, (0, -small.shape[0] % 128))[None, None]
    small = jnp.broadcast_to(small, (shards, 1, small.shape[2]))
    small = lax.all_to_all(small, "shard", split_axis=0, concat_axis=0, tiled=True)[:, 0]
    at = 0
    gain_in = small[:, at : at + norm_gain.shape[0]].reshape(-1).astype(f32)
    at += norm_gain.shape[0]
    taps = small[:, at : at + conv_weight.size].reshape(shards, CONV, -1)
    taps = taps.transpose(1, 0, 2).reshape(CONV, channels).astype(f32)
    at += conv_weight.size
    bias = small[:, at : at + conv_bias.shape[0]].reshape(-1).astype(f32)
    at += conv_bias.shape[0]
    gain_out = small[:, at : at + out_gain.shape[0]].reshape(-1).astype(f32)
    core = shard % 2
    w_in = in_weight.T
    spare = -(w_in.shape[0] - 2 * inner) % TILE
    edge_w = jnp.pad(w_in[2 * inner :], ((0, spare), (0, 0)))
    by_hand = shards == 4 and places % 2 == 0
    if by_hand:
        edge_far = lax.ppermute(edge_w, "shard", flip("shard", 2))
        g_x = Gather(w_in, None, inner, inner // 4, 2)
        g_x.fetch(0)
        edge_other = other_core(edge_w)
        g_x.fetch(1)
        x_other = other_core(w_in[inner : 2 * inner])
        g_x.other, g_x.other_base = (x_other, 0)
        g_x.share(0)
        g_out = Gather(out_weight, other_core(out_weight), 0, out_weight.shape[0] // 2, 1)
        g_out.fetch(0, g_x.direct[0])
        g_x.share(1)
        edges = [edge_w, edge_other, edge_far, other_core(edge_far)]
        stack_z = lax.all_gather(after(w_in[:inner], g_x.direct[0]), "shard")
    else:
        stack_z = lax.all_gather(w_in[:inner], "shard")
        stack_x = lax.all_gather(w_in[inner : 2 * inner], "shard")
        w_edge = lax.all_gather(edge_w, "shard").transpose(1, 0, 2).reshape(-1, width)
        w_out = lax.all_gather(out_weight, "shard", axis=0, tiled=True)
    skip_wide = jnp.repeat(d_skip.astype(f32), HEAD_DIM)
    rows = jnp.concatenate([skip_wide, jnp.zeros((channels - inner,), f32)])
    taps8 = jnp.concatenate([taps, bias[None], rows[None], jnp.zeros((2, channels), f32)], 0)

    edge = jnp.full((HALO,), -1, jnp.int32)
    padded = jnp.concatenate([edge, seg_ids, edge - 1])
    near = lax.dynamic_slice_in_dim(padded, start, length + 2 * HALO)
    seg = near[HALO : HALO + length]
    fwd_masks = [near[HALO - CONV + 1 + k : HALO - CONV + 1 + k + length] == seg for k in range(3)]
    spot = jnp.arange(length, dtype=jnp.int32)
    bwd_masks = [
        (near[HALO + CONV - 1 - k : HALO + CONV - 1 - k + length] == seg)
        & (spot + CONV - 1 - k < length)
        for k in range(3)
    ]
    from_before = seg == near[HALO - 1]
    to_last = seg == seg[length - 1]
    masks = jnp.stack(
        [m.astype(f32) for m in fwd_masks + bwd_masks + [seg, from_before, to_last]], 1
    )
    masks = jnp.pad(masks, ((0, 0), (0, 16 - masks.shape[1])))
    seg_row = jnp.broadcast_to(seg.astype(f32)[None, :], (8, length))

    behind = lax.ppermute(
        hidden[length - HALO :], ALL, [(i, i + 1) for i in range(devices - 1)]
    )
    hidden_f = jnp.concatenate([behind, hidden], 0).astype(f32)
    scale_in = lax.rsqrt(jnp.mean(hidden_f * hidden_f, axis=1, keepdims=True) + EPS)
    normed_ext = (hidden_f * scale_in * gain_in[None, :]).astype(bf16)
    normed_in = normed_ext[HALO:]
    if by_hand:
        w_edge = jnp.concatenate(edges, 1)
        proj_edge = mm_nt(turn_blocks(normed_ext, shard), w_edge).astype(bf16)
    else:
        proj_edge = mm_nt(normed_ext, w_edge).astype(bf16)
    proj_bc = proj_edge[:, : 2 * n_state]
    rates = jnp.stack([dt_bias, a_log]).astype(f32)
    rates = jnp.pad(rates, ((0, 6), (0, TILE - heads)))
    big = pltpu.CompilerParams(vmem_limit_bytes=56 * 1024 * 1024)
    by_head, sums_row = pl.pallas_call(
        prepare_kernel,
        out_shape=[
            jax.ShapeDtypeStruct((5, length, TILE), f32),
            jax.ShapeDtypeStruct((groups, GROUP, length), f32),
        ],
        compiler_params=big,
        name="prepare",
    )(proj_edge[HALO:, 2 * n_state :], rates, masks)
    end = by_head[3, length - 1, :heads]
    decays = jnp.broadcast_to(end[None, None, :], (devices, 1, heads))
    decays = lax.all_to_all(decays, ALL, split_axis=0, concat_axis=0, tiled=True)[:, 0, :]
    if by_hand:
        proj = None
        for number in range(4):
            proj = project(after(normed_ext, by_head), g_x, number, shard, proj)
    else:
        proj = stacked_project(normed_ext, stack_x, 0, inner)

    def whole(shape):
        return pl.BlockSpec(shape, lambda g: (0,) * len(shape))

    def group_of(g):
        return jnp.maximum(g - 1, 0)

    order = lambda g: jnp.where(g == 0, groups, g - 1)
    x_conv, state_local, bc, bt, ct = pl.pallas_call(
        state_kernel,
        grid=(groups + 1,),
        in_specs=[
            pl.BlockSpec((length + HALO, WIDE), lambda g: (0, group_of(g))),
            whole((length + HALO, WIDE)),
            pl.BlockSpec((8, WIDE), lambda g: (0, order(g))),
            whole(masks.shape),
            whole(by_head.shape),
        ],
        out_specs=[
            pl.BlockSpec((length, WIDE), lambda g: (0, group_of(g))),
            pl.BlockSpec((n_state, WIDE), lambda g: (0, group_of(g))),
            whole((length, 2 * n_state)),
            whole((n_state, length)),
            whole((n_state, length)),
        ],
        out_shape=[
            jax.ShapeDtypeStruct((length, inner), bf16),
            jax.ShapeDtypeStruct((n_state, inner), bf16),
            jax.ShapeDtypeStruct((length, 2 * n_state), bf16),
            jax.ShapeDtypeStruct((n_state, length), bf16),
            jax.ShapeDtypeStruct((n_state, length), bf16),
        ],
        scratch_shapes=[
            pltpu.VMEM((length + HALO, WIDE), f32),
            pltpu.VMEM((n_state, length), bf16),
        ],
        compiler_params=big,
        cost_estimate=pl.CostEstimate(
            flops=20 * length * inner * n_state, bytes_accessed=10 * length * inner, transcendentals=0
        ),
        name="mixer_state",
    )(proj, proj_bc, taps8, masks, by_head)

    sent = send_slices(state_local, devices)
    if by_hand:
        g_out.share(0, state_local)
    gate_z = stacked_project(after(normed_in, state_local), stack_z, 0, inner)
    states = scan_devices(after(sent, gate_z), decays, me, False)
    state_in = return_slices(states, n_state, inner)
    x_conv = after(x_conv, states)
    y_local = pl.pallas_call(
        forward_kernel,
        grid=(groups,),
        in_specs=[
            pl.BlockSpec((length, WIDE), lambda g: (0, g)),
            whole(masks.shape),
            whole((8, length)),
            whole(by_head.shape),
            pl.BlockSpec((1, GROUP, length), lambda g: (g, 0, 0)),
            whole((length, 2 * n_state)),
            whole((n_state, length)),
        ],
        out_specs=pl.BlockSpec((length, WIDE), lambda g: (0, g)),
        out_shape=jax.ShapeDtypeStruct((length, inner), f32),
        scratch_shapes=[
            pltpu.VMEM((length, length), f32),
            pltpu.VMEM((length, WIDE), bf16),
            pltpu.VMEM((length, length), bf16),
        ],
        compiler_params=big,
        cost_estimate=pl.CostEstimate(
            flops=16 * length * length * inner, bytes_accessed=10 * length * inner, transcendentals=0
        ),
        name="mixer_forward",
    )(x_conv, masks, seg_row, by_head, sums_row, bc, bt)
    if by_hand:
        d_normed = out_back(after(cotangent, y_local), g_out)
    else:
        d_normed = mm_nt(cotangent, w_out)
    block = TILE
    tall = lambda dim: pl.BlockSpec((block, dim), lambda g: (g, 0))
    gains = jnp.stack([gain_out, skip_wide], 0)
    ssm, normed_out, d_z, d_y, d_state_local, dc_more, d_gain = pl.pallas_call(
        gate_kernel,
        grid=(length // block,),
        in_specs=[
            tall(inner),
            tall(inner),
            tall(inner),
            tall(inner),
            tall(2 * n_state),
            pl.BlockSpec((n_state, block), lambda g: (0, g)),
            tall(TILE),
            whole((n_state, inner)),
            whole((2, inner)),
        ],
        out_specs=[
            tall(inner),
            tall(inner),
            tall(inner),
            tall(inner),
            whole((n_state, inner)),
            tall(n_state),
            whole((8, inner)),
        ],
        out_shape=[
            jax.ShapeDtypeStruct((length, inner), f32),
            jax.ShapeDtypeStruct((length, inner), bf16),
            jax.ShapeDtypeStruct((length, inner), bf16),
            jax.ShapeDtypeStruct((length, inner), bf16),
            jax.ShapeDtypeStruct((n_state, inner), bf16),
            jax.ShapeDtypeStruct((length, n_state), f32),
            jax.ShapeDtypeStruct((8, inner), f32),
        ],
        scratch_shapes=[
            pltpu.VMEM((block, inner), f32),
            pltpu.VMEM((block, inner), f32),
            pltpu.VMEM((block, inner), bf16),
            pltpu.VMEM((n_state, inner), f32),
        ],
        compiler_params=big,
        cost_estimate=pl.CostEstimate(
            flops=8 * length * n_state * inner, bytes_accessed=22 * length * inner, transcendentals=0
        ),
        name="mixer_gate",
    )(y_local, x_conv, gate_z, d_normed, bc, ct, by_head[3], state_in, gains)

    sent = send_slices(d_state_local, devices)

    def both(value):
        return jnp.concatenate([value, other_core(value)], 0)

    def both_rows(value):
        own, rest = core_rows(value, core)
        return jnp.concatenate([own, other_core(rest)], 0)

    normed_pair = both_rows(normed_in)
    cot_pair = both(cotangent)
    out_pair = both_rows(normed_out)
    z_pair = both(d_z)
    if by_hand:
        block_out = out_forward(normed_out, hidden, g_out)
    else:
        block_out = (hidden.astype(f32) + mm(normed_out, w_out)).astype(bf16)
    d_normed_z = stacked_back(after(d_z, block_out), stack_z, 0)
    grad_o = mm_tn(after(out_pair, block_out), cot_pair).astype(bf16)
    states = scan_devices(after(sent, grad_o, d_normed_z), decays, me, True)
    d_state = return_slices(states, n_state, inner)
    grad_z = mm_tn(normed_pair, after(z_pair, states)).astype(bf16)
    half_o, half_z = (width // 2, inner // 2)
    sums_o = [RowSum(grad_o[:, :half_o], True), RowSum(grad_o[:, half_o:], False)]
    sums_z = [RowSum(grad_z[:, :half_z], True), RowSum(grad_z[:, half_z:], False)]
    x_conv = after(x_conv, states, grad_z)

    dxs, db_in, dc_in = pl.pallas_call(
        inside_kernel,
        grid=(groups,),
        in_specs=[
            pl.BlockSpec((length, WIDE), lambda g: (0, g)),
            whole(masks.shape),
            whole((8, length)),
            whole(by_head.shape),
            pl.BlockSpec((1, GROUP, length), lambda g: (g, 0, 0)),
            whole((length, 2 * n_state)),
            whole((n_state, length)),
            pl.BlockSpec((length, WIDE), lambda g: (0, g)),
        ],
        out_specs=[
            pl.BlockSpec((length, WIDE), lambda g: (0, g)),
            whole((length, n_state)),
            whole((length, n_state)),
        ],
        out_shape=[
            jax.ShapeDtypeStruct((length, inner), f32),
            jax.ShapeDtypeStruct((length, n_state), f32),
            jax.ShapeDtypeStruct((length, n_state), f32),
        ],
        scratch_shapes=[
            pltpu.VMEM((length, length), f32),
            pltpu.VMEM((length, length), f32),
            pltpu.VMEM((length, WIDE), bf16),
            pltpu.VMEM((length, length), bf16),
            pltpu.VMEM((length, length), f32),
        ],
        compiler_params=big,
        cost_estimate=pl.CostEstimate(
            flops=8 * length * length * inner, bytes_accessed=10 * length * inner, transcendentals=0
        ),
        name="mixer_inside",
    )(x_conv, masks, seg_row, by_head, sums_row, bc, ct, d_y)

    for chain in sums_o + sums_z:
        chain.step()
    d_y = after(d_y, *[chain.value for chain in sums_o + sums_z])
    for chain in sums_o + sums_z:
        chain.step(dxs)

    kept = lambda g: jnp.minimum(g, groups - 1)
    taps8 = jnp.pad(taps8, ((0, 0), (0, WIDE)))
    d_out, first, last, sums, head_sums = pl.pallas_call(
        outside_kernel,
        grid=(groups + 2,),
        in_specs=[
            pl.BlockSpec((length + HALO, WIDE), lambda g: (0, kept(g))),
            whole((length + HALO, WIDE)),
            pl.BlockSpec((8, WIDE), lambda g: (0, g)),
            whole(masks.shape),
            whole(by_head.shape),
            whole(rates.shape),
            whole((length, 2 * n_state)),
            pl.BlockSpec((length, WIDE), lambda g: (0, kept(g))),
            pl.BlockSpec((length, WIDE), lambda g: (0, kept(g))),
            pl.BlockSpec((length, WIDE), lambda g: (0, kept(g))),
            pl.BlockSpec((n_state, WIDE), lambda g: (0, kept(g))),
            pl.BlockSpec((n_state, WIDE), lambda g: (0, kept(g))),
            whole((length, n_state)),
            whole((length, n_state)),
            whole((length, n_state)),
        ],
        out_specs=[
            pl.BlockSpec((length, WIDE), lambda g: (0, g)),
            pl.BlockSpec((HALO, WIDE), lambda g: (0, g)),
            pl.BlockSpec((HALO, WIDE), lambda g: (0, g)),
            pl.BlockSpec((8, WIDE), lambda g: (0, g)),
            whole((8, TILE)),
        ],
        out_shape=[
            jax.ShapeDtypeStruct((length, channels + WIDE), bf16),
            jax.ShapeDtypeStruct((HALO, channels + WIDE), f32),
            jax.ShapeDtypeStruct((HALO, channels + WIDE), f32),
            jax.ShapeDtypeStruct((8, channels + WIDE), f32),
            jax.ShapeDtypeStruct((8, TILE), f32),
        ],
        scratch_shapes=[
            pltpu.VMEM((length + HALO, WIDE), f32),
            pltpu.VMEM((length + HALO, WIDE), f32),
            pltpu.VMEM((length, n_state), f32),
            pltpu.VMEM((2, length, TILE), f32),
            pltpu.VMEM((8, TILE), f32),
        ],
        compiler_params=big,
        cost_estimate=pl.CostEstimate(
            flops=8 * length * n_state * inner, bytes_accessed=16 * length * inner, transcendentals=0
        ),
        name="mixer_outside",
    )(proj, proj_bc, taps8, masks, by_head, rates, bc, d_y, ssm, dxs, d_state, state_in, db_in,
      dc_in, dc_more)

    ahead = lax.ppermute(first, ALL, [(i + 1, i) for i in range(devices - 1)])
    joined = jnp.concatenate([jnp.zeros_like(first), ahead], 0)
    seg_end = near[length : length + 2 * HALO]
    for tap in range(CONV - 1):
        lead = CONV - 1 - tap
        same = (seg_end[lead : lead + HALO] == seg_end[:HALO]).astype(f32)[:, None]
        last = last + taps8[tap][None, :] * joined[lead : lead + HALO] * same
    fixed_rows = last[:, :channels].astype(bf16)
    d_out = lax.dynamic_update_slice(d_out, fixed_rows, (length - HALO, 0))

    x_pair = both(d_out)
    half = d_out.shape[1] // 2
    grad_x = mm_tn(normed_pair, x_pair[:, :half]).astype(bf16)
    grad_y = mm_tn(normed_pair, x_pair[:, half:]).astype(bf16)
    sums_x = [RowSum(grad_x, True), RowSum(grad_y, False)]
    d_edge = d_out[:, inner : inner + w_edge.shape[0]]
    d_edge = after(d_edge, grad_x, grad_y)
    if by_hand:
        d_normed_in = d_normed_z + back(after(d_out, grad_x, grad_y), g_x, shard, (d_edge, *edges))
    else:
        d_normed_in = d_normed_z + stacked_back(d_out[:, :inner], stack_x, 0) + mm(d_edge, w_edge)
    for chain in sums_o + sums_z:
        chain.step(grad_x)
    for chain in sums_x:
        chain.step()
        chain.step(d_normed_in)
    for chain in sums_o + sums_z + sums_x:
        while chain.order:
            chain.step(d_normed_in)
    base = hidden_f[HALO:]
    scale = scale_in[HALO:]
    d_hat = d_normed_in * gain_in[None, :]
    mean = jnp.mean(d_hat * base, axis=1, keepdims=True)
    grad_hidden = cotangent.astype(f32) + scale * d_hat - base * (scale * scale * scale * mean)
    grad_gain_in = jnp.sum(d_normed_in * base * scale, 0)
    counts = [width // devices] + [channels // devices] * (CONV + 1) + [inner // devices]
    counts += [heads] * 3
    total = sum(counts)
    if by_hand:
        sizes = (width // devices, channels // devices, inner // devices, heads)
        packed = pl.pallas_call(
            lambda *refs: pack_kernel(sizes, *refs),
            out_shape=jax.ShapeDtypeStruct((devices, 1, total + -total % TILE), f32),
            name="pack",
        )(sums[:, :channels], grad_gain_in[None], d_gain, head_sums)
    else:
        slots = lambda v: v.reshape(-1, devices, v.shape[-1] // devices).transpose(1, 0, 2)
        same = jnp.broadcast_to(head_sums[:3, :heads].reshape(1, -1), (devices, 3 * heads))
        pieces = [slots(grad_gain_in), slots(sums[: CONV + 1, :channels])]
        pieces += [slots(jnp.sum(d_gain, 0)), same]
        packed = jnp.concatenate([p.reshape(devices, -1) for p in pieces], 1)[:, None]
    packed = lax.all_to_all(packed, ALL, split_axis=0, concat_axis=0, tiled=True).sum((0, 1))
    found, at = ([], 0)
    for size in counts:
        found.append(packed[at : at + size])
        at += size

    grads = jnp.concatenate([c.rows() for c in sums_z + sums_x], 1)
    return (
        block_out,
        grad_hidden,
        found[0],
        grads[:, : 2 * inner + 2 * n_state + heads].astype(f32),
        jnp.stack(found[1 : CONV + 1]),
        found[CONV + 1],
        found[CONV + 3],
        found[CONV + 4],
        found[CONV + 5],
        found[CONV + 2],
        jnp.concatenate([c.rows() for c in sums_o], 1).astype(f32),
    )


def solution(mesh):
    return jax.shard_map(
        on_device,
        mesh=mesh,
        in_specs=(
            P(ALL, None),
            P(ALL, None),
            P(),
            P("shard"),
            P("shard", None),
            P(None, "shard"),
            P("shard"),
            P(),
            P(),
            P(),
            P("shard"),
            P("shard", None),
        ),
        out_specs=(
            P(ALL, None),
            P(ALL, None),
            P(ALL),
            P(ALL, None),
            P(None, ALL),
            P(ALL),
            P(),
            P(),
            P(),
            P(ALL),
            P(ALL, None),
        ),
        check_vma=False,
    )
```

time: 1030 us -> 656 us (0.64)
  waiting for transfers between devices: 567 us -> 143 us
  Pallas kernels: 160 us -> 238 us
  blocking collectives: 99.5 us -> 26.4 us
  matrix products: 94.6 us -> 29.1 us
  starting transfers between devices: 24.2 us -> 78.6 us
  other arithmetic: 26.9 us -> 54.2 us
  local copies, waits for them, and re-layouts: 38.1 us -> 60.7 us
    reduce_scatter x3 -> x0, waiting for transfers between devices: 423 us -> none  [on_device(): lax.psum_scatter(a, ALL, scatter_dimension=0, tiled=True)]
    ppermute x0 -> x46, waiting for transfers between devices: none -> 128 us  [the longest x24 93.9 us: halve(): came = lax.ppermute(send, axis, flip(axis, bit))]
    pallas_call x2 -> x16, Pallas kernels: 100 us -> 188 us  [the longest x1 42 us: on_device(): pl.pallas_call(outside_kernel, grid=(groups + 2,), in_specs=[pl.BlockSpec...]
    all_gather x3 -> x0, blocking collectives: 86.9 us -> none  [the longest x1 74.6 us: on_device(): decays = lax.all_gather(enter[length - 1], ALL)]
    psum x1 -> x0, waiting for transfers between devices: 78.4 us -> none  [on_device(): total = lax.psum(jnp.concatenate(pieces), ALL)]
    ppermute x0 -> x46, starting transfers between devices: none -> 45.5 us  [the longest x24 29.4 us: halve(): came = lax.ppermute(send, axis, flip(axis, bit))]
    all_gather x3 -> x1, waiting for transfers between devices: 42.8 us -> 0.01 us  [on_device(): stack_z = lax.all_gather(after(w_in[:inner], g_x.direct[0]), 'shard')]
    dot_general x5 -> x0, matrix products: 32.3 us -> none  [the longest x3 29.9 us: mm(): return jnp.dot(a, b, preferred_element_type=f32)]
  transfers between devices with their start and end apart: 13 -> 55, of which waited for: 8 -> 18; matrix products, arithmetic and copies ran while one was open for 12% -> 18% of each run, Pallas kernels for 9% -> 27%
where the time goes in v2:
time: 656 us; the launch traced here: 646 us
  Pallas kernels  238 us (36%)
  waiting for transfers between devices  143 us (22%)
  starting transfers between devices  78.6 us (12%)
  local copies, waits for them, and re-layouts  60.7 us (9%)
  other arithmetic  54.2 us (8%)
  matrix products  29.1 us (4%)
  blocking collectives  26.4 us (4%)
  between operations  15.6 us (2%)
    ppermute x24, waiting for transfers between devices, halve(): came = lax.ppermute(send, axis, flip(axis, bit))  93.9 us
    pallas_call x1, Pallas kernels, on_device(): pl.pallas_call(outside_kernel, grid=(groups + 2,), in_specs=[pl.BlockSpec...  42 us
    pallas_call x1, Pallas kernels, on_device(): pl.pallas_call(inside_kernel, grid=(groups,), in_specs=[pl.BlockSpec((len...  30.4 us
    ppermute x24, starting transfers between devices, halve(): came = lax.ppermute(send, axis, flip(axis, bit))  29.4 us
    pallas_call x1, Pallas kernels, on_device(): pl.pallas_call(forward_kernel, grid=(groups,), in_specs=[pl.BlockSpec((le...  29.1 us
    pallas_call x1, Pallas kernels, on_device(): pl.pallas_call(state_kernel, grid=(groups + 1,), in_specs=[pl.BlockSpec((...  29 us
    dot_general x4, matrix products, mm_tn(): lax.dot_general(a, b, (((0,), (0,)), ((), ())), preferred_element_type=f32)  26.7 us
    all_to_all x1, blocking collectives, on_device(): lax.all_to_all(decays, ALL, split_axis=0, concat_axis=0, tiled=True)  26.4 us
  transfers between devices with their start and end apart: 55, of which 18 were waited for; matrix products, arithmetic and copies ran while one was open for 18% of the time, Pallas kernels for 27%

profile of v2, /device:TPU:0, one launch (start us, length us, event | category | flops | bytes accessed | tf_op | source)
XLA Modules:
  0.0 645.5 jit_solution(5756383766697808934)
XLA Ops:
  9.4 2.9 collective-permute-start.9
  12.4 5.0 fusion.80
  17.4 8.3 %collective-permute-done.9.w2.refs_4_ = bf16[768,384]{1,0:T(8,128)(2,1)S(1)} collective-permute-done((bf16[768,384]{1,0:T(8,128)(2,1)S(1)}, bf16[768,384]{1,0:T(8,128)(2,1)S(1)}, u32[]{:S(2)}, u32[]{:S(2)}) %collective-permute-start.9) | collective-permute-done | bytes 589856 | tf_op jit(solution)/shard_map/ppermute | solution.py:492
  31.7 3.3 all-to-all-start
  35.0 3.4 collective-permute-start
  42.8 2.4 constant_dynamic-slice_fusion.9
  51.1 16.5 %collective-permute-done.5.w2.refs_8_ = bf16[768,384]{1,0:T(8,128)(2,1)S(1)} collective-permute-done((bf16[768,384]{1,0:T(8,128)(2,1)}, bf16[768,384]{1,0:T(8,128)(2,1)S(1)}, u32[]{:S(2)}, u32[]{:S(2)}) %collective-permute-start.5) | collective-permute-done | bytes 589856 | tf_op jit(solution)/shard_map/ppermute | solution.py:492
  73.6 9.0 %collective-permute-done.6.w2.refs_10_ = bf16[768,384]{1,0:T(8,128)(2,1)S(1)} collective-permute-done((bf16[768,384]{1,0:T(8,128)(2,1)S(1)}, bf16[768,384]{1,0:T(8,128)(2,1)S(1)}, u32[]{:S(2)}, u32[]{:S(2)}) %collective-permute-start.6) | collective-permute-done | bytes 589856 | tf_op jit(solution)/shard_map/ppermute | solution.py:498
  82.6 2.4 fusion.27
  86.4 3.4 prepare.1
  89.8 2.4 copy-done.1
  92.2 4.1 project.4.rest_0_
  96.3 3.9 project.5.rest_0_
  100.3 4.1 project.6.rest_0_
  104.4 4.1 project.7.raw
  110.1 29.0 %mixer_state.1 = (bf16[512,3072]{1,0:T(8,128)(2,1)}, bf16[128,3072]{1,0:T(8,128)(2,1)}, bf16[512,256]{1,0:T(8,128)(2,1)}, bf16[128,512]{1,0:T(8,128)(2,1)}, bf16[128,512]{1,0:T(8,128)(2,1)}) custom-call(bf16[520,3072]{1,0:T(8,128)(2,1)} %copy-done.2, bf16[520,256]{1,0:T(8,128)(2,1)} %slice.269.raw_bc, f32[8,3328]{1,0:T(8,128)} %maximum_maximum_fusion.taps, ...), custom_call_target="tpu_custom_call" | custom-call | flops 4026531840 | bytes 15728640 | tf_op jit(solution)/shard_map/mixer_state/pallas_call | solution.py:983
  141.5 26.4 %all_to_all.35 = f32[32,1,48]{2,1,0:T(1,128)S(1)} all-to-all(f32[32,1,48]{2,1,0:T(1,128)S(1)} %broadcast_in_dim.23), channel_id=1, replica_groups=mesh['shard'=4,'seq'=8] {'shard','seq'}, dimensions={0} | all-to-all | bytes 12288 | tf_op jit(solution)/shard_map/all_to_all | solution.py:968
  167.9 5.4 all-to-all-start.1
  182.5 3.7 copy-done
  186.2 7.6 %stacked_project.1.z_in = bf16[512,3072]{1,0:T(8,128)(2,1)S(1)} custom-call(bf16[512,1536]{1,0:T(8,128)(2,1)S(1)} %slice.272.value, bf16[4,3072,384]{2,1,0:T(8,128)(2,1)S(1)} %bitcast.209, bf16[4,3072,384]{2,1,0:T(8,128)(2,1)S(1)} %bitcast.210, bf16[4,3072,384]{2,1,0:T(8,128)(2,1)S(1)} %bitcast.211, bf16[4,3072,384]{2,1,0:T(8,128)(2,1)S(1)} %bitcast.212), custom_call_target="tpu_custom_call" | custom-call | flops 4831838208 | bytes 9437184 | tf_op jit(solution)/shard_map/stacked_project/pallas_call | solution.py:635
  195.4 2.4 scan_forward.1
  197.7 5.7 all-to-all-start.3
  204.1 29.1 %mixer_forward.1.y_in = f32[512,3072]{1,0:T(8,128)} custom-call(bf16[512,3072]{1,0:T(8,128)(2,1)} %get-tuple-element.92.x_in, f32[512,16]{1,0:T(8,128)} %pad.28.masks, f32[8,512]{1,0:T(8,128)} %broadcast_in_dim.25.seg_row, f32[5,512,128]{2,1,0:T(8,128)} %get-tuple-element.67.heads, f32[12,4,512]{2,1,0:T(4,128)} %get-tuple-element.75.sums_row, ...), custom_call_target="tpu_custom_call" | custom-call | flops 12884901888 | bytes 15728640 | tf_op jit(solution)/shard_map/mixer_forward/pallas_call | solution.py:1025
  233.2 14.2 %out_back.1.dn_in = f32[512,3072]{1,0:T(8,128)} custom-call(s32[8]{0:T(128)} %stack.193.refs_0_, bf16[512,1536]{1,0:T(8,128)(2,1)} %refs_1_, bf16[768,1536]{1,0:T(8,128)(2,1)} %refs_3_.1, bf16[768,1536]{1,0:T(8,128)(2,1)} %collective-permute-done.13.refs_3_.refs_4_, bf16[384,1536]{1,0:T(8,128)(2,1)} %collective-permute-done.14.refs_4_.refs_5_, ...), custom_call_target="tpu_custom_call" | custom-call | flops 4831838208 | bytes 9437184 | tf_op jit(solution)/shard_map/out_back/pallas_call | solution.py:739
  248.4 19.3 %mixer_gate.1 = (f32[512,3072]{1,0:T(8,128)}, bf16[512,3072]{1,0:T(8,128)(2,1)}, bf16[512,3072]{1,0:T(8,128)(2,1)}, bf16[512,3072]{1,0:T(8,128)(2,1)}, bf16[128,...) custom-call(f32[512,3072]{1,0:T(8,128)} %mixer_forward.1.y_in, bf16[512,3072]{1,0:T(8,128)(2,1)} %get-tuple-element.92.x_in, ...), custom_call_target="tpu_custom_call" | custom-call | flops 1610612736 | bytes 34603008 | tf_op jit(solution)/shard_map/mixer_gate/pallas_call | solution.py:1057
  267.7 3.2 broadcast_select_fusion.3
  275.9 15.0 %out_forward.1 = bf16[512,1536]{1,0:T(8,128)(2,1)} custom-call(s32[8]{0:T(128)} %stack.193.refs_0_, bf16[512,3072]{1,0:T(8,128)(2,1)} %get-tuple-element.82.refs_1_, bf16[512,1536]{1,0:T(8,128)(2,1)} %refs_2_.3, bf16[768,1536]{1,0:T(8,128)(2,1)} %refs_3_.1, bf16[768,1536]{1,0:T(8,128)(2,1)} %collective-permute-done.13.refs_3_.refs_4_, ...), custom_call_target="tpu_custom_call" | custom-call | flops 4831838208 | bytes 9437184 | tf_op jit(solution)/shard_map/out_forward/pallas_call | solution.py:781
  290.9 9.2 %stacked_back.1 = f32[512,1536]{1,0:T(8,128)S(1)} custom-call(bf16[512,3072]{1,0:T(8,128)(2,1)} %get-tuple-element.84.value, bf16[4,3072,384]{2,1,0:T(8,128)(2,1)} %bitcast.205, bf16[4,3072,384]{2,1,0:T(8,128)(2,1)} %bitcast.206, bf16[4,3072,384]{2,1,0:T(8,128)(2,1)} %bitcast.207, bf16[4,3072,384]{2,1,0:T(8,128)(2,1)} %bitcast.208), custom_call_target="tpu_custom_call" | custom-call | flops 4831838208 | bytes 9437184 | tf_op jit(solution)/shard_map/stacked_back/pallas_call | solution.py:675
  300.1 6.0 all-to-all-start.4
  308.2 7.3 %convolution_convert_fusion = bf16[1536,1536]{1,0:T(8,128)(2,1)S(1)} fusion(bf16[1024,1536]{1,0:T(8,128)(2,1)S(1)} %pad_maximum_fusion.5, bf16[512,1536]{1,0:T(8,128)(2,1)} %collective-permute-done.19, bf16[512,1536]{1,0:T(8,128)(2,1)} %refs_1_), kind=kOutput, calls=%fused_computation | convolution fusion | flops 4840488960 | bytes 11010048 | tf_op jit(solution)/shard_map/dot_general | solution.py:30
  315.4 2.5 fusion.82
  317.9 10.2 %all-to-all-done.4.refs_0_ = bf16[32,8,1536]{2,1,0:T(8,128)(2,1)} async-done(((bf16[32,8,1536]{2,1,0:T(8,128)(2,1)}), bf16[32,8,1536]{2,1,0:T(8,128)(2,1)}, u32[]{:S(2)}, u32[]{:S(2)}) %all-to-all-start.4) | async-done | bytes 786464 | tf_op jit(solution)/shard_map/all_to_all | solution.py:447
  328.1 2.5 scan_backward.1
  330.6 2.5 dynamic-slice_bitcast_fusion.5
  335.5 3.5 all-to-all-start.5
  339.1 3.4 pad_maximum_fusion
  342.5 6.5 %convolution_convert_fusion.1 = bf16[768,3072]{1,0:T(8,128)(2,1)S(1)} fusion(bf16[1024,3072]{1,0:T(8,128)(2,1)S(1)} %pad_maximum_fusion, bf16[512,768]{1,0:T(8,128)(2,1)} %collective-permute-done.22, bf16[512,384]{1,0:T(8,128)(2,1)S(1)} %copy-done.33, bf16[512,384]{1,0:T(8,128)(2,1)S(1)} %copy-done.31), kind=kOutput, calls=%fused_computation.4 | convolution fusion | flops 4838916096 | bytes 12582912 | tf_op jit(solution)/shard_map/dot_general | solution.py:30
  352.3 16.1 %collective-permute-done.20 = bf16[1,8,96,768]{3,2,1,0:T(8,128)(2,1)} collective-permute-done((bf16[1,8,96,768]{3,2,1,0:T(8,128)(2,1)}, bf16[1,8,96,768]{3,2,1,0:T(8,128)(2,1)}, u32[]{:S(2)}, u32[]{:S(2)}) %collective-permute-start.20) | collective-permute-done | bytes 1179680 | tf_op jit(solution)/shard_map/ppermute | solution.py:804
  368.3 2.6 fusion.17
  372.8 2.6 fusion.16
  375.4 30.4 %mixer_inside.1 = (f32[512,3072]{1,0:T(8,128)}, f32[512,128]{1,0:T(8,128)}, f32[512,128]{1,0:T(8,128)}) custom-call(bf16[512,3072]{1,0:T(8,128)(2,1)} %get-tuple-element.92.x_in, f32[512,16]{1,0:T(8,128)} %pad.28.masks, f32[8,512]{1,0:T(8,128)} %broadcast_in_dim.25.seg_row, f32[5,512,128]{2,1,0:T(8,128)} %get-tuple-element.67.heads, ...), custom_call_target="tpu_custom_call" | custom-call | flops 6442450944 | bytes 15728640 | tf_op jit(solution)/shard_map/mixer_inside/pallas_call | solution.py:1129
  405.9 2.6 fusion.14
  408.4 2.6 fusion.15
  411.0 42.0 %mixer_outside.1 = (bf16[512,3584]{1,0:T(8,128)(2,1)}, f32[8,3584]{1,0:T(8,128)}, f32[8,3584]{1,0:T(8,128)}, f32[8,3584]{1,0:T(8,128)}, f32[8,128]{1,0:T(8,128)}) custom-call(bf16[520,3072]{1,0:T(8,128)(2,1)} %copy-done.2, bf16[520,256]{1,0:T(8,128)(2,1)} %slice.269.raw_bc, f32[8,3584]{1,0:T(8,128)} %pad.29.taps, f32[512,16]{1,0:T(8,128)} %pad.28.masks, ...), custom_call_target="tpu_custom_call" | custom-call | flops 1610612736 | bytes 25165824 | tf_op jit(solution)/shard_map/mixer_outside/pallas_call | solution.py:1174
  454.7 5.2 collective-permute-done.26
  469.0 10.5 %collective-permute-done.42 = bf16[1,4,96,768]{3,2,1,0:T(8,128)(2,1)S(1)} collective-permute-done((bf16[1,4,96,768]{3,2,1,0:T(8,128)(2,1)S(1)}, bf16[1,4,96,768]{3,2,1,0:T(8,128)(2,1)S(1)}, u32[]{:S(2)}, u32[]{:S(2)}) %collective-permute-start.42) | collective-permute-done | bytes 589856 | tf_op jit(solution)/shard_map/ppermute | solution.py:804
  484.9 6.9 %collective-permute-done.28 = bf16[1,4,48,1536]{3,2,1,0:T(8,128)(2,1)S(1)} collective-permute-done((bf16[1,4,48,1536]{3,2,1,0:T(8,128)(2,1)S(1)}, bf16[1,4,48,1536]{3,2,1,0:T(8,128)(2,1)S(1)}, u32[]{:S(2)}, u32[]{:S(2)}) %collective-permute-start.28) | collective-permute-done | bytes 589856 | tf_op jit(solution)/shard_map/ppermute | solution.py:804
  492.8 2.4 collective-permute-done.31
  496.2 6.5 %fusion.6 = bf16[768,1792]{1,0:T(8,128)(2,1)} fusion(bf16[512,3584]{1,0:T(8,128)(2,1)S(1)} %copy-done.20, bf16[512,3584]{1,0:T(8,128)(2,1)} %collective-permute-done.27, bf16[512,768]{1,0:T(8,128)(2,1)} %collective-permute-done.22, bf16[512,384]{1,0:T(8,128)(2,1)S(1)} %copy-done.34, bf16[512,384]{1,0:T(8,128)(2,1)S(1)} %copy-done.32), kind=kOutput, calls=%fused_computation.11 | convolution fusion | flops 2832007168 | bytes 11665408 | tf_op jit(solution)/shard_map/dot_general | solution.py:30
  503.4 6.4 fusion.5
  512.6 15.4 %back.1 = f32[512,1536]{1,0:T(8,128)} custom-call(s32[8]{0:T(128)} %stack.232.refs_0_, bf16[512,3584]{1,0:T(8,128)(2,1)} %fusion.58.refs_1_, bf16[6448,384]{1,0:T(8,128)(2,1)} %bitcast.215, bf16[3072,384]{1,0:T(8,128)(2,1)} %collective-permute-done.4.w1.refs_3_, bf16[768,384]{1,0:T(8,128)(2,1)} %copy-done.4, ...), custom_call_target="tpu_custom_call" | custom-call | flops 4831838208 | bytes 9437184 | tf_op jit(solution)/shard_map/back/pallas_call | solution.py:605
  528.0 4.4 multiply_reduce_fusion.1
  535.3 4.3 all-to-all-start.6
  545.0 2.5 dynamic-slice_bitcast_fusion.1
  549.3 4.9 multiply_subtract_fusion
  560.4 2.5 collective-permute-start.44
  569.2 7.5 %collective-permute-done.44 = bf16[1,1,96,768]{3,2,1,0:T(8,128)(2,1)S(1)} collective-permute-done((bf16[1,1,96,768]{3,2,1,0:T(8,128)(2,1)S(1)}, bf16[1,1,96,768]{3,2,1,0:T(8,128)(2,1)S(1)}, u32[]{:S(2)}, u32[]{:S(2)}) %collective-permute-start.44) | collective-permute-done | bytes 147488 | tf_op jit(solution)/shard_map/ppermute | solution.py:804
  576.8 3.1 collective-permute-done.47
  579.9 6.3 collective-permute-done.30
  591.7 15.0 %collective-permute-done.35 = bf16[1,4,48,1792]{3,2,1,0:T(8,128)(2,1)S(1)} collective-permute-done((bf16[1,4,48,1792]{3,2,1,0:T(8,128)(2,1)S(1)}, bf16[1,4,48,1792]{3,2,1,0:T(8,128)(2,1)S(1)}, u32[]{:S(2)}, u32[]{:S(2)}) %collective-permute-start.35) | collective-permute-done | bytes 688160 | tf_op jit(solution)/shard_map/ppermute | solution.py:804
  609.3 8.7 %collective-permute-done.36 = bf16[1,2,48,1792]{3,2,1,0:T(8,128)(2,1)S(1)} collective-permute-done((bf16[1,2,48,1792]{3,2,1,0:T(8,128)(2,1)S(1)}, bf16[1,2,48,1792]{3,2,1,0:T(8,128)(2,1)S(1)}, u32[]{:S(2)}, u32[]{:S(2)}) %collective-permute-start.36) | collective-permute-done | bytes 344096 | tf_op jit(solution)/shard_map/ppermute | solution.py:804
  618.1 2.9 collective-permute-start.37
  621.0 5.9 collective-permute-done.40
  628.9 8.2 %collective-permute-done.41 = bf16[1,1,48,1792]{3,2,1,0:T(8,128)(2,1)S(1)} collective-permute-done((bf16[1,1,48,1792]{3,2,1,0:T(8,128)(2,1)S(1)}, bf16[1,1,48,1792]{3,2,1,0:T(8,128)(2,1)S(1)}, u32[]{:S(2)}, u32[]{:S(2)}) %collective-permute-start.41) | collective-permute-done | bytes 172064 | tf_op jit(solution)/shard_map/ppermute | solution.py:804
  (308 shorter events, 112.0 us)
Async XLA Ops:
  7.2 175.4 %all-gather.3.cloned.1.call-start = ((), (), s32[]{:S(2)}) async-start(), calls=%async_computation.7 | async-start | bytes 11796480 | tf_op jit(solution)/shard_map/all_gather | solution.py:912
  9.4 16.3 %collective-permute-start.9 = (bf16[768,384]{1,0:T(8,128)(2,1)S(1)}, bf16[768,384]{1,0:T(8,128)(2,1)S(1)}, u32[]{:S(2)}, u32[]{:S(2)}) collective-permute-start(bf16[768,384]{1,0:T(8,128)(2,1)S(1)} %get-tuple-element.131), channel_id=1, source_target_pairs={{0,16},{8,24},{16,0},{24,8},{1,17},{9,25},{17,1},{25,9},{2,18},{10... | collective-permute-start | bytes 1769480 | tf_op jit(solution)/shard_map/ppermute | solution.py:492
  17.4 23.2 %copy-start.39 = (s32[16384]{0:T(1024)S(1)}, s32[16384]{0:T(1024)}, u32[]{:S(2)}) copy-start(s32[16384]{0:T(1024)} %param.14) | copy-start | bytes 196612
  25.7 64.1 %copy-start.4 = (bf16[768,384]{1,0:T(8,128)(2,1)}, bf16[768,384]{1,0:T(8,128)(2,1)S(1)}, u32[]{:S(2)}) copy-start(bf16[768,384]{1,0:T(8,128)(2,1)S(1)} %collective-permute-done.9.w2.refs_4_) | copy-start | bytes 1769476
  27.7 22.8 %collective-permute-start.2 = (bf16[384,384]{1,0:T(8,128)(2,1)}, bf16[384,384]{1,0:T(8,128)(2,1)}, u32[]{:S(2)}, u32[]{:S(2)}) collective-permute-start(bf16[384,384]{1,0:T(8,128)(2,1)} %pad.25.refs_13_), channel_id=1, source_target_pairs={{0,16},{8,24},{16,0},{24,8},{1,17},{9,25},{17,1},{25,9},{2,18},{10... | collective-permute-start | bytes 884744 | tf_op jit(solution)/shard_map/ppermute | solution.py:900
  29.4 21.1 %collective-permute-start.1 = (bf16[384,384]{1,0:T(8,128)(2,1)}, bf16[384,384]{1,0:T(8,128)(2,1)}, u32[]{:S(2)}, u32[]{:S(2)}) collective-permute-start(bf16[384,384]{1,0:T(8,128)(2,1)} %pad.25.refs_13_), channel_id=1, source_target_pairs={{0,8},{8,0},{16,24},{24,16},{1,9},{9,1},{17,25},{25,17},{2,10},{10... | collective-permute-start | bytes 884744 | tf_op jit(solution)/shard_map/ppermute | solution.py:473
  31.7 16.0 %all-to-all-start = ((bf16[4,2,2688]{2,1,0:T(2,128)(2,1)}), bf16[4,2,2688]{2,1,0:T(2,128)(2,1)S(1)}, u32[]{:S(2)}, u32[]{:S(2)}) async-start(bf16[4,2,2688]{2,1,0:T(2,128)(2,1)} %reshape.473), calls=%async_computation | async-start | bytes 86016 | tf_op jit(solution)/shard_map/all_to_all | solution.py:884
  35.0 12.3 %collective-permute-start = (bf16[8,1536]{1,0:T(8,128)(2,1)S(1)}, bf16[8,1536]{1,0:T(8,128)(2,1)S(1)}, u32[]{:S(2)}, u32[]{:S(2)}) collective-permute-start(bf16[8,1536]{1,0:T(8,128)(2,1)S(1)} %slice.202), channel_id=1, source_target_pairs={{0,1},{1,2},{2,3},{3,4},{4,5},{5,6},{6,7},{7,8},{8,9},{9,10},{10,1... | collective-permute-start | bytes 73736 | tf_op jit(solution)/shard_map/ppermute | solution.py:941
  38.5 51.3 %collective-permute-start.4 = (bf16[3072,384]{1,0:T(8,128)(2,1)}, bf16[3072,384]{1,0:T(8,128)(2,1)}, u32[]{:S(2)}, u32[]{:S(2)}) collective-permute-start(bf16[3072,384]{1,0:T(8,128)(2,1)} %get-tuple-element.130), channel_id=1, source_target_pairs={{0,8},{8,0},{16,24},{24,16},{1,9},{9,1},{17,25},{25,17},{2,10},{10... | collective-permute-start | bytes 7077896 | tf_op jit(solution)/shard_map/ppermute | solution.py:473
  38.8 28.9 %collective-permute-start.5 = (bf16[768,384]{1,0:T(8,128)(2,1)}, bf16[768,384]{1,0:T(8,128)(2,1)S(1)}, u32[]{:S(2)}, u32[]{:S(2)}) collective-permute-start(bf16[768,384]{1,0:T(8,128)(2,1)} %get-tuple-element.132), channel_id=1, source_target_pairs={{0,16},{8,24},{16,0},{24,8},{1,17},{9,25},{17,1},{25,9},{2,18},{10... | collective-permute-start | bytes 1769480 | tf_op jit(solution)/shard_map/ppermute | solution.py:492
  48.2 21.0 %collective-permute-start.10 = (bf16[768,384]{1,0:T(8,128)(2,1)S(1)}, bf16[768,384]{1,0:T(8,128)(2,1)S(1)}, u32[]{:S(2)}, u32[]{:S(2)}) collective-permute-start(bf16[768,384]{1,0:T(8,128)(2,1)S(1)} %collective-permute-done.9.w2.refs_4_), channel_id=1, source_target_pairs={{0,1},{1,0},{2,3},{3,2},{4,5},{5,4},{6,7},{7,6},{8,9},{9,8},{10,11... | collective-permute-start | bytes 1769480 | tf_op jit(solution)/shard_map/ppermute | solution.py:498
  50.5 23.0 %collective-permute-start.12 = (bf16[768,384]{1,0:T(8,128)(2,1)S(1)}, bf16[768,384]{1,0:T(8,128)(2,1)}, u32[]{:S(2)}, u32[]{:S(2)}) collective-permute-start(bf16[768,384]{1,0:T(8,128)(2,1)S(1)} %collective-permute-done.9.w2.refs_4_), channel_id=1, source_target_pairs={{0,8},{8,0},{16,24},{24,16},{1,9},{9,1},{17,25},{25,17},{2,10},{10... | collective-permute-start | bytes 1769480 | tf_op jit(solution)/shard_map/ppermute | solution.py:473
  50.5 23.1 %copy-start.36 = (f32[1536]{0:T(1024)}, f32[1536]{0:T(1024)S(1)}, u32[]{:S(2)}) copy-start(f32[1536]{0:T(1024)S(1)} %reshape.441) | copy-start | bytes 18436
  50.5 20.7 %collective-permute-start.3 = (bf16[384,384]{1,0:T(8,128)(2,1)}, bf16[384,384]{1,0:T(8,128)(2,1)S(1)}, u32[]{:S(2)}, u32[]{:S(2)}) collective-permute-start(bf16[384,384]{1,0:T(8,128)(2,1)} %collective-permute-done.2.refs_15_), channel_id=1, source_target_pairs={{0,8},{8,0},{16,24},{24,16},{1,9},{9,1},{17,25},{25,17},{2,10},{10... | collective-permute-start | bytes 884744 | tf_op jit(solution)/shard_map/ppermute | solution.py:473
  67.6 32.6 %copy-start.5 = (bf16[768,384]{1,0:T(8,128)(2,1)}, bf16[768,384]{1,0:T(8,128)(2,1)S(1)}, u32[]{:S(2)}) copy-start(bf16[768,384]{1,0:T(8,128)(2,1)S(1)} %collective-permute-done.5.w2.refs_8_) | copy-start | bytes 1769476
  67.6 15.0 %collective-permute-start.6 = (bf16[768,384]{1,0:T(8,128)(2,1)S(1)}, bf16[768,384]{1,0:T(8,128)(2,1)S(1)}, u32[]{:S(2)}, u32[]{:S(2)}) collective-permute-start(bf16[768,384]{1,0:T(8,128)(2,1)S(1)} %collective-permute-done.5.w2.refs_8_), channel_id=1, source_target_pairs={{0,1},{1,0},{2,3},{3,2},{4,5},{5,4},{6,7},{7,6},{8,9},{9,8},{10,11... | collective-permute-start | bytes 1769480 | tf_op jit(solution)/shard_map/ppermute | solution.py:498
  69.1 27.2 %copy-start.6 = (bf16[768,384]{1,0:T(8,128)(2,1)}, bf16[768,384]{1,0:T(8,128)(2,1)S(1)}, u32[]{:S(2)}) copy-start(bf16[768,384]{1,0:T(8,128)(2,1)S(1)} %collective-permute-done.10.w2.refs_6_) | copy-start | bytes 1769476
  69.1 27.2 %collective-permute-start.11 = (bf16[768,384]{1,0:T(8,128)(2,1)S(1)}, bf16[768,384]{1,0:T(8,128)(2,1)S(1)}, u32[]{:S(2)}, u32[]{:S(2)}) collective-permute-start(bf16[768,384]{1,0:T(8,128)(2,1)S(1)} %collective-permute-done.10.w2.refs_6_), channel_id=1, source_target_pairs={{0,8},{8,0},{16,24},{24,16},{1,9},{9,1},{17,25},{25,17},{2,10},{10... | collective-permute-start | bytes 1769480 | tf_op jit(solution)/shard_map/ppermute | solution.py:473
  71.2 67.9 %collective-permute-start.14 = (bf16[384,1536]{1,0:T(8,128)(2,1)}, bf16[384,1536]{1,0:T(8,128)(2,1)}, u32[]{:S(2)}, u32[]{:S(2)}) collective-permute-start(bf16[384,1536]{1,0:T(8,128)(2,1)} %constant_dynamic-slice_fusion.9), channel_id=1, source_target_pairs={{0,16},{8,24},{16,0},{24,8},{1,17},{9,25},{17,1},{25,9},{2,18},{10... | collective-permute-start | bytes 3538952 | tf_op jit(solution)/shard_map/ppermute | solution.py:492
  73.5 26.8 %collective-permute-start.8 = (bf16[768,384]{1,0:T(8,128)(2,1)S(1)}, bf16[768,384]{1,0:T(8,128)(2,1)}, u32[]{:S(2)}, u32[]{:S(2)}) collective-permute-start(bf16[768,384]{1,0:T(8,128)(2,1)S(1)} %collective-permute-done.5.w2.refs_8_), channel_id=1, source_target_pairs={{0,8},{8,0},{16,24},{24,16},{1,9},{9,1},{17,25},{25,17},{2,10},{10... | collective-permute-start | bytes 1769480 | tf_op jit(solution)/shard_map/ppermute | solution.py:473
  82.6 21.7 %collective-permute-start.7 = (bf16[768,384]{1,0:T(8,128)(2,1)S(1)}, bf16[768,384]{1,0:T(8,128)(2,1)}, u32[]{:S(2)}, u32[]{:S(2)}) collective-permute-start(bf16[768,384]{1,0:T(8,128)(2,1)S(1)} %collective-permute-done.6.w2.refs_10_), channel_id=1, source_target_pairs={{0,8},{8,0},{16,24},{24,16},{1,9},{9,1},{17,25},{25,17},{2,10},{10... | collective-permute-start | bytes 1769480 | tf_op jit(solution)/shard_map/ppermute | solution.py:473
  139.2 43.2 %collective-permute-start.16 = (bf16[384,1536]{1,0:T(8,128)(2,1)}, bf16[384,1536]{1,0:T(8,128)(2,1)}, u32[]{:S(2)}, u32[]{:S(2)}) collective-permute-start(bf16[384,1536]{1,0:T(8,128)(2,1)} %collective-permute-done.14.refs_4_.refs_5_), channel_id=1, source_target_pairs={{0,1},{1,0},{2,3},{3,2},{4,5},{5,4},{6,7},{7,6},{8,9},{9,8},{10,11... | collective-permute-start | bytes 3538952 | tf_op jit(solution)/shard_map/ppermute | solution.py:498
  167.9 27.5 %all-to-all-start.1 = ((bf16[32,8,1536]{2,1,0:T(8,128)(2,1)}), bf16[32,8,1536]{2,1,0:T(8,128)(2,1)}, u32[]{:S(2)}, u32[]{:S(2)}) async-start(bf16[32,8,1536]{2,1,0:T(8,128)(2,1)} %bitcast.254), calls=%async_computation.1 | async-start | bytes 1572864 | tf_op jit(solution)/shard_map/all_to_all | solution.py:447
  173.3 60.0 %collective-permute-start.13 = (bf16[768,1536]{1,0:T(8,128)(2,1)}, bf16[768,1536]{1,0:T(8,128)(2,1)}, u32[]{:S(2)}, u32[]{:S(2)}) collective-permute-start(bf16[768,1536]{1,0:T(8,128)(2,1)} %refs_3_.1), channel_id=1, source_target_pairs={{0,8},{8,0},{16,24},{24,16},{1,9},{9,1},{17,25},{25,17},{2,10},{10... | collective-permute-start | bytes 7077896 | tf_op jit(solution)/shard_map/ppermute | solution.py:473
  182.0 51.2 %collective-permute-start.15 = (bf16[384,1536]{1,0:T(8,128)(2,1)}, bf16[384,1536]{1,0:T(8,128)(2,1)}, u32[]{:S(2)}, u32[]{:S(2)}) collective-permute-start(bf16[384,1536]{1,0:T(8,128)(2,1)} %collective-permute-done.14.refs_4_.refs_5_), channel_id=1, source_target_pairs={{0,8},{8,0},{16,24},{24,16},{1,9},{9,1},{17,25},{25,17},{2,10},{10... | collective-permute-start | bytes 3538952 | tf_op jit(solution)/shard_map/ppermute | solution.py:473
  182.3 50.9 %collective-permute-start.17 = (bf16[384,1536]{1,0:T(8,128)(2,1)}, bf16[384,1536]{1,0:T(8,128)(2,1)}, u32[]{:S(2)}, u32[]{:S(2)}) collective-permute-start(bf16[384,1536]{1,0:T(8,128)(2,1)} %collective-permute-done.16.refs_6_.refs_7_), channel_id=1, source_target_pairs={{0,8},{8,0},{16,24},{24,16},{1,9},{9,1},{17,25},{25,17},{2,10},{10... | collective-permute-start | bytes 3538952 | tf_op jit(solution)/shard_map/ppermute | solution.py:473
  197.7 49.7 %all-to-all-start.3 = ((bf16[32,8,1536]{2,1,0:T(8,128)(2,1)}), bf16[32,8,1536]{2,1,0:T(8,128)(2,1)S(1)}, u32[]{:S(2)}, u32[]{:S(2)}) async-start(bf16[32,8,1536]{2,1,0:T(8,128)(2,1)} %scan_forward.1), calls=%async_computation.3 | async-start | bytes 1572864 | tf_op jit(solution)/shard_map/all_to_all | solution.py:451
  272.2 33.9 %collective-permute-start.18 = (bf16[512,1536]{1,0:T(8,128)(2,1)}, bf16[512,1536]{1,0:T(8,128)(2,1)}, u32[]{:S(2)}, u32[]{:S(2)}) collective-permute-start(bf16[512,1536]{1,0:T(8,128)(2,1)} %pad_maximum_fusion.6), channel_id=1, source_target_pairs={{0,8},{8,0},{16,24},{24,16},{1,9},{9,1},{17,25},{25,17},{2,10},{10... | collective-permute-start | bytes 4718600 | tf_op jit(solution)/shard_map/ppermute | solution.py:473
  272.4 35.7 %collective-permute-start.19 = (bf16[512,1536]{1,0:T(8,128)(2,1)}, bf16[512,1536]{1,0:T(8,128)(2,1)}, u32[]{:S(2)}, u32[]{:S(2)}) collective-permute-start(bf16[512,1536]{1,0:T(8,128)(2,1)} %refs_1_), channel_id=1, source_target_pairs={{0,8},{8,0},{16,24},{24,16},{1,9},{9,1},{17,25},{25,17},{2,10},{10... | collective-permute-start | bytes 4718600 | tf_op jit(solution)/shard_map/ppermute | solution.py:473
  275.4 67.0 %collective-permute-start.22 = (bf16[512,768]{1,0:T(8,128)(2,1)}, bf16[512,768]{1,0:T(8,128)(2,1)}, u32[]{:S(2)}, u32[]{:S(2)}) collective-permute-start(bf16[512,768]{1,0:T(8,128)(2,1)} %pad_maximum_fusion.8), channel_id=1, source_target_pairs={{0,8},{8,0},{16,24},{24,16},{1,9},{9,1},{17,25},{25,17},{2,10},{10... | collective-permute-start | bytes 2359304 | tf_op jit(solution)/shard_map/ppermute | solution.py:473
  275.7 63.4 %collective-permute-start.23 = (bf16[512,3072]{1,0:T(8,128)(2,1)}, bf16[512,3072]{1,0:T(8,128)(2,1)}, u32[]{:S(2)}, u32[]{:S(2)}) collective-permute-start(bf16[512,3072]{1,0:T(8,128)(2,1)} %get-tuple-element.84.value), channel_id=1, source_target_pairs={{0,8},{8,0},{16,24},{24,16},{1,9},{9,1},{17,25},{25,17},{2,10},{10... | collective-permute-start | bytes 9437192 | tf_op jit(solution)/shard_map/ppermute | solution.py:473
  300.1 27.9 %all-to-all-start.4 = ((bf16[32,8,1536]{2,1,0:T(8,128)(2,1)}), bf16[32,8,1536]{2,1,0:T(8,128)(2,1)}, u32[]{:S(2)}, u32[]{:S(2)}) async-start(bf16[32,8,1536]{2,1,0:T(8,128)(2,1)} %bitcast.255), calls=%async_computation.4 | async-start | bytes 1572864 | tf_op jit(solution)/shard_map/all_to_all | solution.py:447
  333.1 35.2 %collective-permute-start.20 = (bf16[1,8,96,768]{3,2,1,0:T(8,128)(2,1)}, bf16[1,8,96,768]{3,2,1,0:T(8,128)(2,1)}, u32[]{:S(2)}, u32[]{:S(2)}) collective-permute-start(bf16[1,8,96,768]{3,2,1,0:T(8,128)(2,1)} %dynamic-slice_bitcast_fusion.5), channel_id=1, source_target_pairs={{0,16},{8,24},{16,0},{24,8},{1,17},{9,25},{17,1},{25,9},{2,18},{10... | collective-permute-start | bytes 3538952 | tf_op jit(solution)/shard_map/ppermute | solution.py:804
  334.8 38.1 %collective-permute-start.21 = (bf16[2,4,96,768]{3,2,1,0:T(8,128)(2,1)}, bf16[2,4,96,768]{3,2,1,0:T(8,128)(2,1)}, u32[]{:S(2)}, u32[]{:S(2)}) collective-permute-start(bf16[2,4,96,768]{3,2,1,0:T(8,128)(2,1)} %dynamic-slice_bitcast_fusion.4), channel_id=1, source_target_pairs={{0,1},{1,0},{2,3},{3,2},{4,5},{5,4},{6,7},{7,6},{8,9},{9,8},{10,11... | collective-permute-start | bytes 3538952 | tf_op jit(solution)/shard_map/ppermute | solution.py:804
  335.5 75.5 %all-to-all-start.5 = ((bf16[32,8,1536]{2,1,0:T(8,128)(2,1)}), bf16[32,8,1536]{2,1,0:T(8,128)(2,1)}, u32[]{:S(2)}, u32[]{:S(2)}) async-start(bf16[32,8,1536]{2,1,0:T(8,128)(2,1)} %scan_backward.1), calls=%async_computation.5 | async-start | bytes 1572864 | tf_op jit(solution)/shard_map/all_to_all | solution.py:451
  350.5 55.3 %collective-permute-start.25 = (bf16[2,4,48,1536]{3,2,1,0:T(8,128)(2,1)}, bf16[2,4,48,1536]{3,2,1,0:T(8,128)(2,1)}, u32[]{:S(2)}, u32[]{:S(2)}) collective-permute-start(bf16[2,4,48,1536]{3,2,1,0:T(8,128)(2,1)} %dynamic-slice_bitcast_fusion.2), channel_id=1, source_target_pairs={{0,1},{1,0},{2,3},{3,2},{4,5},{5,4},{6,7},{7,6},{8,9},{9,8},{10,11... | collective-permute-start | bytes 3538952 | tf_op jit(solution)/shard_map/ppermute | solution.py:804
  372.1 36.4 %collective-permute-start.24 = (bf16[1,8,48,1536]{3,2,1,0:T(8,128)(2,1)}, bf16[1,8,48,1536]{3,2,1,0:T(8,128)(2,1)}, u32[]{:S(2)}, u32[]{:S(2)}) collective-permute-start(bf16[1,8,48,1536]{3,2,1,0:T(8,128)(2,1)} %dynamic-slice_bitcast_fusion.3), channel_id=1, source_target_pairs={{0,16},{8,24},{16,0},{24,8},{1,17},{9,25},{17,1},{25,9},{2,18},{10... | collective-permute-start | bytes 3538952 | tf_op jit(solution)/shard_map/ppermute | solution.py:804
  453.0 6.9 %collective-permute-start.26 = (f32[8,3584]{1,0:T(8,128)}, f32[8,3584]{1,0:T(8,128)S(1)}, u32[]{:S(2)}, u32[]{:S(2)}) collective-permute-start(f32[8,3584]{1,0:T(8,128)} %get-tuple-element.99), channel_id=1, source_target_pairs={{1,0},{2,1},{3,2},{4,3},{5,4},{6,5},{7,6},{8,7},{9,8},{10,9},{11,1... | collective-permute-start | bytes 344072 | tf_op jit(solution)/shard_map/ppermute | solution.py:1223
  461.6 34.6 %collective-permute-start.27 = (bf16[512,3584]{1,0:T(8,128)(2,1)}, bf16[512,3584]{1,0:T(8,128)(2,1)}, u32[]{:S(2)}, u32[]{:S(2)}) collective-permute-start(bf16[512,3584]{1,0:T(8,128)(2,1)} %fusion.58.refs_1_), channel_id=1, source_target_pairs={{0,8},{8,0},{16,24},{24,16},{1,9},{9,1},{17,25},{25,17},{2,10},{10... | collective-permute-start | bytes 11010056 | tf_op jit(solution)/shard_map/ppermute | solution.py:473
  463.4 16.2 %collective-permute-start.42 = (bf16[1,4,96,768]{3,2,1,0:T(8,128)(2,1)S(1)}, bf16[1,4,96,768]{3,2,1,0:T(8,128)(2,1)S(1)}, u32[]{:S(2)}, u32[]{:S(2)}) collective-permute-start(bf16[1,4,96,768]{3,2,1,0:T(8,128)(2,1)S(1)} %dynamic-slice_bitcast_fusion.7), channel_id=1, source_target_pairs={{0,1},{1,0},{2,3},{3,2},{4,5},{5,4},{6,7},{7,6},{8,9},{9,8},{10,11... | collective-permute-start | bytes 1769480 | tf_op jit(solution)/shard_map/ppermute | solution.py:804
  467.0 61.0 %copy-start.9 = (f32[520,1536]{1,0:T(8,128)}, f32[520,1536]{1,0:T(8,128)S(1)}, u32[]{:S(2)}) copy-start(f32[520,1536]{1,0:T(8,128)S(1)} %maximum_convert_fusion) | copy-start | bytes 9584644
  467.1 16.2 %collective-permute-start.45 = (bf16[1,4,96,768]{3,2,1,0:T(8,128)(2,1)S(1)}, bf16[1,4,96,768]{3,2,1,0:T(8,128)(2,1)S(1)}, u32[]{:S(2)}, u32[]{:S(2)}) collective-permute-start(bf16[1,4,96,768]{3,2,1,0:T(8,128)(2,1)S(1)} %constant_dynamic-slice_fusion.1), channel_id=1, source_target_pairs={{0,16},{8,24},{16,0},{24,8},{1,17},{9,25},{17,1},{25,9},{2,18},{10... | collective-permute-start | bytes 1769480 | tf_op jit(solution)/shard_map/ppermute | solution.py:804
  468.7 23.2 %collective-permute-start.28 = (bf16[1,4,48,1536]{3,2,1,0:T(8,128)(2,1)S(1)}, bf16[1,4,48,1536]{3,2,1,0:T(8,128)(2,1)S(1)}, u32[]{:S(2)}, u32[]{:S(2)}) collective-permute-start(bf16[1,4,48,1536]{3,2,1,0:T(8,128)(2,1)S(1)} %dynamic-slice_bitcast_fusion.8), channel_id=1, source_target_pairs={{0,1},{1,0},{2,3},{3,2},{4,5},{5,4},{6,7},{7,6},{8,9},{9,8},{10,11... | collective-permute-start | bytes 1769480 | tf_op jit(solution)/shard_map/ppermute | solution.py:804
  479.7 22.9 %copy-start.26 = (bf16[1,4,96,768]{3,2,1,0:T(8,128)(2,1)}, bf16[1,4,96,768]{3,2,1,0:T(8,128)(2,1)S(1)}, u32[]{:S(2)}) copy-start(bf16[1,4,96,768]{3,2,1,0:T(8,128)(2,1)S(1)} %fusion.37) | copy-start | bytes 1769476
  479.8 15.4 %collective-permute-start.31 = (bf16[1,4,48,1536]{3,2,1,0:T(8,128)(2,1)S(1)}, bf16[1,4,48,1536]{3,2,1,0:T(8,128)(2,1)S(1)}, u32[]{:S(2)}, u32[]{:S(2)}) collective-permute-start(bf16[1,4,48,1536]{3,2,1,0:T(8,128)(2,1)S(1)} %constant_dynamic-slice_fusion.7), channel_id=1, source_target_pairs={{0,16},{8,24},{16,0},{24,8},{1,17},{9,25},{17,1},{25,9},{2,18},{10... | collective-permute-start | bytes 1769480 | tf_op jit(solution)/shard_map/ppermute | solution.py:804
  483.4 26.4 %copy-start.28 = (bf16[1,4,96,768]{3,2,1,0:T(8,128)(2,1)}, bf16[1,4,96,768]{3,2,1,0:T(8,128)(2,1)S(1)}, u32[]{:S(2)}) copy-start(bf16[1,4,96,768]{3,2,1,0:T(8,128)(2,1)S(1)} %add_convert_fusion.1) | copy-start | bytes 1769476
  503.4 54.5 %collective-permute-start.43 = (bf16[1,2,96,768]{3,2,1,0:T(8,128)(2,1)}, bf16[1,2,96,768]{3,2,1,0:T(8,128)(2,1)}, u32[]{:S(2)}, u32[]{:S(2)}) collective-permute-start(bf16[1,2,96,768]{3,2,1,0:T(8,128)(2,1)} %dynamic-slice_bitcast_fusion.14), channel_id=1, source_target_pairs={{0,2},{1,3},{2,0},{3,1},{4,6},{5,7},{6,4},{7,5},{8,10},{9,11},{10,... | collective-permute-start | bytes 884744 | tf_op jit(solution)/shard_map/ppermute | solution.py:804
  510.6 49.8 %collective-permute-start.46 = (bf16[1,2,96,768]{3,2,1,0:T(8,128)(2,1)}, bf16[1,2,96,768]{3,2,1,0:T(8,128)(2,1)}, u32[]{:S(2)}, u32[]{:S(2)}) collective-permute-start(bf16[1,2,96,768]{3,2,1,0:T(8,128)(2,1)} %dynamic-slice_bitcast_fusion.13), channel_id=1, source_target_pairs={{0,2},{1,3},{2,0},{3,1},{4,6},{5,7},{6,4},{7,5},{8,10},{9,11},{10,... | collective-permute-start | bytes 884744 | tf_op jit(solution)/shard_map/ppermute | solution.py:804
  535.3 20.1 %all-to-all-start.6 = ((f32[32,1,896]{2,1,0:T(1,128)}), f32[32,1,896]{2,1,0:T(1,128)S(1)}, u32[]{:S(2)}, u32[]{:S(2)}) async-start(f32[32,1,896]{2,1,0:T(1,128)} %pack.1), calls=%async_computation.6 | async-start | bytes 229376 | tf_op jit(solution)/shard_map/all_to_all | solution.py:1274
  541.3 22.7 %collective-permute-start.29 = (bf16[1,2,48,1536]{3,2,1,0:T(8,128)(2,1)}, bf16[1,2,48,1536]{3,2,1,0:T(8,128)(2,1)}, u32[]{:S(2)}, u32[]{:S(2)}) collective-permute-start(bf16[1,2,48,1536]{3,2,1,0:T(8,128)(2,1)} %dynamic-slice_bitcast_fusion.16), channel_id=1, source_target_pairs={{0,2},{1,3},{2,0},{3,1},{4,6},{5,7},{6,4},{7,5},{8,10},{9,11},{10,... | collective-permute-start | bytes 884744 | tf_op jit(solution)/shard_map/ppermute | solution.py:804
  544.8 21.1 %collective-permute-start.32 = (bf16[1,2,48,1536]{3,2,1,0:T(8,128)(2,1)}, bf16[1,2,48,1536]{3,2,1,0:T(8,128)(2,1)}, u32[]{:S(2)}, u32[]{:S(2)}) collective-permute-start(bf16[1,2,48,1536]{3,2,1,0:T(8,128)(2,1)} %dynamic-slice_bitcast_fusion.15), channel_id=1, source_target_pairs={{0,2},{1,3},{2,0},{3,1},{4,6},{5,7},{6,4},{7,5},{8,10},{9,11},{10,... | collective-permute-start | bytes 884744 | tf_op jit(solution)/shard_map/ppermute | solution.py:804
  547.5 40.8 %collective-permute-start.34 = (bf16[1,8,48,1792]{3,2,1,0:T(8,128)(2,1)}, bf16[1,8,48,1792]{3,2,1,0:T(8,128)(2,1)}, u32[]{:S(2)}, u32[]{:S(2)}) collective-permute-start(bf16[1,8,48,1792]{3,2,1,0:T(8,128)(2,1)} %dynamic-slice_bitcast_fusion.1), channel_id=1, source_target_pairs={{0,16},{8,24},{16,0},{24,8},{1,17},{9,25},{17,1},{25,9},{2,18},{10... | collective-permute-start | bytes 4128776 | tf_op jit(solution)/shard_map/ppermute | solution.py:804
  557.9 33.0 %collective-permute-start.38 = (bf16[2,4,48,1792]{3,2,1,0:T(8,128)(2,1)}, bf16[2,4,48,1792]{3,2,1,0:T(8,128)(2,1)S(1)}, u32[]{:S(2)}, u32[]{:S(2)}) collective-permute-start(bf16[2,4,48,1792]{3,2,1,0:T(8,128)(2,1)} %dynamic-slice_bitcast_fusion), channel_id=1, source_target_pairs={{0,1},{1,0},{2,3},{3,2},{4,5},{5,4},{6,7},{7,6},{8,9},{9,8},{10,11... | collective-permute-start | bytes 4128776 | tf_op jit(solution)/shard_map/ppermute | solution.py:804
  560.4 16.3 %collective-permute-start.44 = (bf16[1,1,96,768]{3,2,1,0:T(8,128)(2,1)S(1)}, bf16[1,1,96,768]{3,2,1,0:T(8,128)(2,1)S(1)}, u32[]{:S(2)}, u32[]{:S(2)}) collective-permute-start(bf16[1,1,96,768]{3,2,1,0:T(8,128)(2,1)S(1)} %constant_dynamic-slice_fusion.2), channel_id=1, source_target_pairs={{0,4},{1,5},{2,6},{3,7},{4,0},{5,1},{6,2},{7,3},{8,12},{9,13},{10,... | collective-permute-start | bytes 442376 | tf_op jit(solution)/shard_map/ppermute | solution.py:804
  563.9 24.4 %copy-start.23 = (bf16[768,1792]{1,0:T(8,128)(2,1)S(1)}, bf16[768,1792]{1,0:T(8,128)(2,1)}, u32[]{:S(2)}) copy-start(bf16[768,1792]{1,0:T(8,128)(2,1)} %fusion.6) | copy-start | bytes 8257540
  564.0 15.9 %collective-permute-start.47 = (bf16[1,1,96,768]{3,2,1,0:T(8,128)(2,1)S(1)}, bf16[1,1,96,768]{3,2,1,0:T(8,128)(2,1)S(1)}, u32[]{:S(2)}, u32[]{:S(2)}) collective-permute-start(bf16[1,1,96,768]{3,2,1,0:T(8,128)(2,1)S(1)} %constant_dynamic-slice_fusion), channel_id=1, source_target_pairs={{0,4},{1,5},{2,6},{3,7},{4,0},{5,1},{6,2},{7,3},{8,12},{9,13},{10,... | collective-permute-start | bytes 442376 | tf_op jit(solution)/shard_map/ppermute | solution.py:804
  565.8 20.3 %collective-permute-start.30 = (bf16[1,1,48,1536]{3,2,1,0:T(8,128)(2,1)S(1)}, bf16[1,1,48,1536]{3,2,1,0:T(8,128)(2,1)S(1)}, u32[]{:S(2)}, u32[]{:S(2)}) collective-permute-start(bf16[1,1,48,1536]{3,2,1,0:T(8,128)(2,1)S(1)} %constant_dynamic-slice_fusion.8), channel_id=1, source_target_pairs={{0,4},{1,5},{2,6},{3,7},{4,0},{5,1},{6,2},{7,3},{8,12},{9,13},{10,... | collective-permute-start | bytes 442376 | tf_op jit(solution)/shard_map/ppermute | solution.py:804
  576.7 11.6 %collective-permute-start.33 = (bf16[1,1,48,1536]{3,2,1,0:T(8,128)(2,1)S(1)}, bf16[1,1,48,1536]{3,2,1,0:T(8,128)(2,1)S(1)}, u32[]{:S(2)}, u32[]{:S(2)}) collective-permute-start(bf16[1,1,48,1536]{3,2,1,0:T(8,128)(2,1)S(1)} %constant_dynamic-slice_fusion.6), channel_id=1, source_target_pairs={{0,4},{1,5},{2,6},{3,7},{4,0},{5,1},{6,2},{7,3},{8,12},{9,13},{10,... | collective-permute-start | bytes 442376 | tf_op jit(solution)/shard_map/ppermute | solution.py:804
  590.2 16.5 %collective-permute-start.35 = (bf16[1,4,48,1792]{3,2,1,0:T(8,128)(2,1)S(1)}, bf16[1,4,48,1792]{3,2,1,0:T(8,128)(2,1)S(1)}, u32[]{:S(2)}, u32[]{:S(2)}) collective-permute-start(bf16[1,4,48,1792]{3,2,1,0:T(8,128)(2,1)S(1)} %dynamic-slice_bitcast_fusion.6), channel_id=1, source_target_pairs={{0,1},{1,0},{2,3},{3,2},{4,5},{5,4},{6,7},{7,6},{8,9},{9,8},{10,11... | collective-permute-start | bytes 2064392 | tf_op jit(solution)/shard_map/ppermute | solution.py:804
  591.3 17.1 %collective-permute-start.39 = (bf16[1,4,48,1792]{3,2,1,0:T(8,128)(2,1)S(1)}, bf16[1,4,48,1792]{3,2,1,0:T(8,128)(2,1)S(1)}, u32[]{:S(2)}, u32[]{:S(2)}) collective-permute-start(bf16[1,4,48,1792]{3,2,1,0:T(8,128)(2,1)S(1)} %constant_dynamic-slice_fusion.4), channel_id=1, source_target_pairs={{0,16},{8,24},{16,0},{24,8},{1,17},{9,25},{17,1},{25,9},{2,18},{10... | collective-permute-start | bytes 2064392 | tf_op jit(solution)/shard_map/ppermute | solution.py:804
  606.9 11.1 %collective-permute-start.36 = (bf16[1,2,48,1792]{3,2,1,0:T(8,128)(2,1)S(1)}, bf16[1,2,48,1792]{3,2,1,0:T(8,128)(2,1)S(1)}, u32[]{:S(2)}, u32[]{:S(2)}) collective-permute-start(bf16[1,2,48,1792]{3,2,1,0:T(8,128)(2,1)S(1)} %dynamic-slice_bitcast_fusion.12), channel_id=1, source_target_pairs={{0,2},{1,3},{2,0},{3,1},{4,6},{5,7},{6,4},{7,5},{8,10},{9,11},{10,... | collective-permute-start | bytes 1032200 | tf_op jit(solution)/shard_map/ppermute | solution.py:804
  608.6 18.2 %collective-permute-start.40 = (bf16[1,2,48,1792]{3,2,1,0:T(8,128)(2,1)S(1)}, bf16[1,2,48,1792]{3,2,1,0:T(8,128)(2,1)S(1)}, u32[]{:S(2)}, u32[]{:S(2)}) collective-permute-start(bf16[1,2,48,1792]{3,2,1,0:T(8,128)(2,1)S(1)} %dynamic-slice_bitcast_fusion.11), channel_id=1, source_target_pairs={{0,2},{1,3},{2,0},{3,1},{4,6},{5,7},{6,4},{7,5},{8,10},{9,11},{10,... | collective-permute-start | bytes 1032200 | tf_op jit(solution)/shard_map/ppermute | solution.py:804
  618.1 10.7 %collective-permute-start.37 = (bf16[1,1,48,1792]{3,2,1,0:T(8,128)(2,1)S(1)}, bf16[1,1,48,1792]{3,2,1,0:T(8,128)(2,1)S(1)}, u32[]{:S(2)}, u32[]{:S(2)}) collective-permute-start(bf16[1,1,48,1792]{3,2,1,0:T(8,128)(2,1)S(1)} %constant_dynamic-slice_fusion.5), channel_id=1, source_target_pairs={{0,4},{1,5},{2,6},{3,7},{4,0},{5,1},{6,2},{7,3},{8,12},{9,13},{10,... | collective-permute-start | bytes 516104 | tf_op jit(solution)/shard_map/ppermute | solution.py:804
  627.0 10.1 %collective-permute-start.41 = (bf16[1,1,48,1792]{3,2,1,0:T(8,128)(2,1)S(1)}, bf16[1,1,48,1792]{3,2,1,0:T(8,128)(2,1)S(1)}, u32[]{:S(2)}, u32[]{:S(2)}) collective-permute-start(bf16[1,1,48,1792]{3,2,1,0:T(8,128)(2,1)S(1)} %constant_dynamic-slice_fusion.3), channel_id=1, source_target_pairs={{0,4},{1,5},{2,6},{3,7},{4,0},{5,1},{6,2},{7,3},{8,12},{9,13},{10,... | collective-permute-start | bytes 516104 | tf_op jit(solution)/shard_map/ppermute | solution.py:804
  (38 other events, 396.7 us)
Sparse Core Ops, SparseCore 0:
  25.8 103.6 all-gather.2

commit v3 on v2

v3 whole, which is shorter than its diff:
```python
import jax
import jax.numpy as jnp
from jax import lax
from jax.experimental import pallas as pl
from jax.experimental.pallas import tpu as pltpu
from jax.sharding import PartitionSpec as P

HEAD_DIM = 64
CONV = 4
EPS = 1e-05
HALO = 8
GROUP = 4
WIDE = GROUP * HEAD_DIM
TILE = 128
PIECE = 3 * WIDE
HIGH = lax.Precision.HIGHEST
ALL = ("shard", "seq")
f32 = jnp.float32
bf16 = jnp.bfloat16


def mm(a, b):
    return jnp.dot(a, b, preferred_element_type=f32)


def mm_nt(a, b):
    return lax.dot_general(a, b, (((1,), (1,)), ((), ())), preferred_element_type=f32)


def mm_tn(a, b):
    return lax.dot_general(a, b, (((0,), (0,)), ((), ())), preferred_element_type=f32)


def sigmoid(value):
    return 0.5 * jnp.tanh(0.5 * value) + 0.5


def head_lanes(group):
    lane = lax.rem(lax.broadcasted_iota(jnp.int32, (2 * TILE, WIDE), 0), TILE)
    owner = lax.broadcasted_iota(jnp.int32, (2 * TILE, WIDE), 1) // HEAD_DIM + GROUP * group
    return jnp.where(lane == owner, 1.0, 0.0).astype(bf16)


def two_parts(value):
    high = value.astype(bf16)
    low = (value - high.astype(f32)).astype(bf16)
    return high, low


def twice(value):
    return jnp.concatenate([value, value], 1)


def conv_rows(wide, taps, masks, start, rows):
    pre = taps[CONV : CONV + 1, :] + taps[CONV - 1 : CONV, :] * wide[pl.ds(HALO + start, rows), :]
    for tap in range(CONV - 1):
        shifted = wide[pl.ds(HALO - CONV + 1 + tap + start, rows), :]
        pre = pre + taps[tap : tap + 1, :] * shifted * twice(masks[tap, pl.ds(start, rows), :])
    return pre


def prepare_kernel(edge, rates, flags, out, spread_out, cum_out, row_out, masks_out):
    length = out.shape[1]
    shifted = edge[...].astype(f32) + rates[0:1, :]
    step = jax.nn.softplus(shifted)
    here = lax.broadcasted_iota(jnp.int32, (length, length), 0)
    there = lax.broadcasted_iota(jnp.int32, (length, length), 1)
    lower = jnp.where(here >= there, 1.0, 0.0)
    log_decay = -step * jnp.exp(rates[1:2, :])
    cum = lax.dot_general(
        lower, log_decay, (((1,), (0,)), ((), ())), precision=HIGH, preferred_element_type=f32
    )
    keep = jnp.exp(cum[length - 1 : length, :] - cum) * flags[:, 8:9]
    out[0] = cum
    out[1] = step
    out[2] = keep
    out[3] = jnp.exp(cum) * flags[:, 7:8]
    out[4] = sigmoid(shifted)
    for at, value in enumerate((step, keep)):
        high, low = two_parts(value)
        spread_out[at, :, :TILE] = high
        spread_out[at, :, TILE:] = low
    turned = cum.T
    for group in range(row_out.shape[0]):
        heads = slice(GROUP * group, GROUP * (group + 1))
        row_out[group] = turned[heads, :]
        cum_out[group] = cum[:, heads]
    for at in range(2 * (CONV - 1)):
        masks_out[at] = jnp.broadcast_to(flags[:, at : at + 1], (length, TILE))


def state_kernel(raw, raw_bc, taps, masks, spreads, x_out, state_out, bc_out, bt_out, ct_out, wide, bt):
    length = x_out.shape[0]
    n_state = bt.shape[0]
    step = pl.program_id(0)

    @pl.when(step == 0)
    def _():
        wide[...] = raw_bc[...].astype(f32)
        for start in range(0, length, TILE):
            rows = pl.ds(start, TILE)
            pre = conv_rows(wide, taps, masks, start, TILE)
            both = pre * sigmoid(pre)
            bc_out[rows, :] = both.astype(bf16)
            turned = both[:, :n_state].T.astype(bf16)
            bt[:, rows] = turned
            bt_out[:, rows] = turned
            ct_out[:, rows] = both[:, n_state:].T.astype(bf16)

    @pl.when(step > 0)
    def _():
        wide[...] = raw[...].astype(f32)
        lanes = head_lanes(step - 1)
        kept = []
        for start in range(0, length, TILE):
            rows = pl.ds(start, TILE)
            pre = conv_rows(wide, taps, masks, start, TILE)
            x = (pre * sigmoid(pre)).astype(bf16)
            x_out[rows, :] = x
            scaled = (x.astype(f32) * mm(spreads[0, rows, :], lanes)).astype(bf16)
            kept.append((scaled.astype(f32) * mm(spreads[1, rows, :], lanes)).astype(bf16))
        state_out[...] = mm(bt[...], jnp.concatenate(kept, 0)).astype(bf16)


def scored(first, second, flags, seg_row, score, later):
    length = score.shape[0]
    for start in range(0, length, TILE):
        rows = pl.ds(start, TILE)
        product = mm(first(rows), second[...])
        here = lax.broadcasted_iota(jnp.int32, (TILE, length), 0) + start
        there = lax.broadcasted_iota(jnp.int32, (TILE, length), 1)
        order = (here >= there) if later else (here <= there)
        seen = (flags[rows, 6:7] == seg_row[0:1, :]) & order
        score[rows, :] = jnp.where(seen, product, 0.0)


def by_head(value):
    owner = lax.broadcasted_iota(jnp.int32, value.shape, 1) // HEAD_DIM
    zero = jnp.zeros_like(value)
    return [jnp.where(owner == head, value, zero) for head in range(GROUP)]


def forward_kernel(x_in, flags, seg_row, spreads, cum, sums_row, bc, bt, y_out, score, apart, weights):
    length = y_out.shape[0]
    n_state = bt.shape[0]
    group = pl.program_id(0)
    big = weights.shape[2] // GROUP

    @pl.when(group == 0)
    def _():
        scored(lambda rows: bc[rows, n_state:], bt, flags, seg_row, score, True)
        weights[...] = jnp.zeros_like(weights)

    lanes = head_lanes(group)
    for start in range(0, length, TILE):
        rows = pl.ds(start, TILE)
        scaled = x_in[rows, :].astype(f32) * mm(spreads[0, rows, :], lanes)
        for head, value in enumerate(by_head(scaled)):
            apart[start // big, pl.ds(head * big + start % big, TILE), :] = value.astype(bf16)
    for head in range(GROUP):
        for start in range(0, length, TILE):
            rows = pl.ds(start, TILE)
            for at in range(0, start + TILE, big):
                end = min(at + big, start + TILE)
                gap = cum[0, rows, head : head + 1] - sums_row[0, head : head + 1, at:end]
                weight = jnp.exp(jnp.minimum(gap, 0.0)) * score[rows, at:end]
                weights[at // big, rows, head * big : head * big + end - at] = weight.astype(bf16)
    for at in range(0, length, big):
        part = mm(weights[at // big, at:, :], apart[at // big])
        if at == 0:
            y_out[...] = part
        else:
            y_out[at:, :] += part


def gate_kernel(
    y_in, x_in, z_in, dn_in, bc, ct, enter, state, gain, ssm_out, norm_out, dz_out, dy_out,
    ds_out, dc_out, dg_out, gated_s, sig_s, mo_s, ds_acc
):
    rows = y_in.shape[0]
    width = y_in.shape[1]
    n_state = state.shape[0]
    step = pl.program_id(0)
    lane = lax.broadcasted_iota(jnp.int32, (rows, 2 * HEAD_DIM), 1)
    c_mat = bc[:, n_state:]

    @pl.when(step == 0)
    def _():
        ds_acc[...] = jnp.zeros_like(ds_acc)
        dg_out[...] = jnp.zeros_like(dg_out)

    def entering(block):
        low = enter[:, 2 * block : 2 * block + 1]
        top = enter[:, 2 * block + 1 : 2 * block + 2]
        return jnp.where(lane < HEAD_DIM, low, top)

    square = jnp.zeros((rows, 2 * HEAD_DIM), f32)
    cross = jnp.zeros((rows, 2 * HEAD_DIM), f32)
    for block in range(width // (2 * HEAD_DIM)):
        lanes = slice(block * 2 * HEAD_DIM, (block + 1) * 2 * HEAD_DIM)
        ssm = y_in[:, lanes] + entering(block) * mm(c_mat, state[:, lanes])
        ssm_out[:, lanes] = ssm
        mo = (ssm + gain[1:2, lanes] * x_in[:, lanes].astype(f32)).astype(bf16)
        mo_s[:, lanes] = mo
        z = z_in[:, lanes].astype(f32)
        sig = sigmoid(z)
        gated = mo.astype(f32) * (z * sig)
        gated_s[:, lanes] = gated
        sig_s[:, lanes] = sig
        square = square + gated * gated
        cross = cross + gated * (dn_in[:, lanes] * gain[0:1, lanes])
    scale = lax.rsqrt(jnp.sum(square, axis=1, keepdims=True) * (1.0 / width) + EPS)
    pull = scale * scale * scale * (jnp.sum(cross, axis=1, keepdims=True) * (1.0 / width))
    dc = jnp.zeros((rows, n_state), f32)
    for block in range(width // (2 * HEAD_DIM)):
        lanes = slice(block * 2 * HEAD_DIM, (block + 1) * 2 * HEAD_DIM)
        gated = gated_s[:, lanes]
        sig = sig_s[:, lanes]
        silu = z_in[:, lanes].astype(f32) * sig
        dn = dn_in[:, lanes]
        hat = gated * scale
        norm_out[:, lanes] = (hat * gain[0:1, lanes]).astype(bf16)
        part = dn * hat
        total = part[0:8, :]
        for at in range(8, rows, 8):
            total = total + part[at : at + 8, :]
        dg_out[:, lanes] += total
        d_gated = scale * (dn * gain[0:1, lanes]) - gated * pull
        dy = (d_gated * silu).astype(bf16)
        dy_out[:, lanes] = dy
        mo = mo_s[:, lanes].astype(f32)
        dz_out[:, lanes] = (d_gated * mo * (sig + silu * (1.0 - sig))).astype(bf16)
        weighted = (dy.astype(f32) * entering(block)).astype(bf16)
        ds_acc[:, lanes] += mm(ct[...], weighted)
        dc = dc + mm_nt(weighted, state[:, lanes])
    dc_out[...] = dc

    @pl.when(step == pl.num_programs(0) - 1)
    def _():
        ds_out[...] = ds_acc[...].astype(bf16)


def inside_kernel(
    x_in, flags, seg_row, spreads, cum, sums_row, bc, ct, dy, dxs_out, db_out, dc_out, score, pair,
    apart, weights, xs, crossed
):
    length = dxs_out.shape[0]
    n_state = ct.shape[0]
    group = pl.program_id(0)
    big = weights.shape[2] // GROUP

    @pl.when(group == 0)
    def _():
        pair[...] = jnp.zeros_like(pair)
        weights[...] = jnp.zeros_like(weights)
        scored(lambda rows: bc[rows, :n_state], ct, flags, seg_row, score, False)

    lanes = head_lanes(group)
    for start in range(0, length, TILE):
        rows = pl.ds(start, TILE)
        scaled = x_in[rows, :].astype(f32) * mm(spreads[0, rows, :], lanes)
        for head, value in enumerate(by_head(scaled)):
            xs[head, rows, :] = value.astype(bf16)
        for head, value in enumerate(by_head(dy[rows, :].astype(f32))):
            apart[start // big, pl.ds(head * big + start % big, TILE), :] = value.astype(bf16)
    for head in range(GROUP):
        for at in range(0, length, big):
            end = at + big
            crossed[head % 2, :end, at:end] = mm_nt(xs[head, :end, :], dy[at:end, :])
        for start in range(0, length, TILE):
            rows = pl.ds(start, TILE)
            for at in range(start // big * big, length, big):
                first = max(at, start)
                end = at + big
                gap = sums_row[0, head : head + 1, first:end] - cum[0, rows, head : head + 1]
                decay = jnp.exp(jnp.minimum(gap, 0.0))
                weight = (decay * score[rows, first:end]).astype(bf16)
                weights[at // big, rows, head * big + first - at : (head + 1) * big] = weight
                pair[rows, first:end] += decay * crossed[head % 2, rows, first:end]
    for at in range(length - big, -1, -big):
        end = at + big
        part = mm(weights[at // big, :end, :], apart[at // big])
        if end == length:
            dxs_out[...] = part
        else:
            dxs_out[:end, :] += part

    @pl.when(group == pl.num_programs(0) - 1)
    def _():
        for start in range(0, length, TILE):
            rows = pl.ds(start, TILE)
            here = lax.broadcasted_iota(jnp.int32, (TILE, length), 0) + start
            there = lax.broadcasted_iota(jnp.int32, (TILE, length), 1)
            seen = (flags[rows, 6:7] == seg_row[0:1, :]) & (here <= there)
            part = jnp.where(seen, pair[rows, :], 0.0).astype(bf16)
            db_out[rows, :] = mm(part, bc[:, n_state:])
            if start == 0:
                dc_out[...] = mm_tn(part, bc[rows, :n_state])
            else:
                dc_out[...] += mm_tn(part, bc[rows, :n_state])


def split_mm(value, chosen):
    high, low = two_parts(value)
    return mm(high, chosen) + mm(low, chosen)


def outside_kernel(first_group, count, final, *refs):
    (raw, raw_bc, taps, masks, spreads, heads, rates, bc, dy, ssm, dxs_in, d_state, state, db_in,
     dc_in, dc_more, db_start, found_start, totals_start, d_out, first_out, last_out, sums_out,
     head_out, db_acc, found, totals_s, wide, d_pre) = refs
    length = d_out.shape[0]
    n_state = bc.shape[1] // 2
    step = pl.program_id(0)
    bc_step = count

    @pl.when(step == 0)
    def _():
        db_acc[...] = db_start[...]
        found[...] = found_start[...]
        totals_s[...] = totals_start[...]

    d_pre[pl.ds(length, HALO), :] = jnp.zeros((HALO, d_pre.shape[1]), f32)
    zero = jnp.zeros((1, d_pre.shape[1]), f32)

    @pl.when(step < bc_step)
    def _():
        wide[...] = raw[...].astype(f32)
        skip_sum, keep_sum = (zero, zero)
        ds = d_state[...]
        group = step + first_group
        lanes = head_lanes(group)
        owner = lax.broadcasted_iota(jnp.int32, (WIDE, TILE), 0) // HEAD_DIM + GROUP * group
        chosen = (owner == lax.broadcasted_iota(jnp.int32, (WIDE, TILE), 1)).astype(f32)
        chosen_b = chosen.astype(bf16)
        for start in range(0, length, TILE):
            rows = pl.ds(start, TILE)
            pre = conv_rows(wide, taps, masks, start, TILE)
            sig = sigmoid(pre)
            x = pre * sig
            stepped = mm(spreads[0, rows, :], lanes)
            scaled = (x.astype(bf16).astype(f32) * stepped).astype(bf16)
            keep = mm(spreads[1, rows, :], lanes)
            carried = keep * mm(bc[rows, :n_state], ds)
            dxs = dxs_in[rows, :] + carried
            scaled = scaled.astype(f32)
            db_acc[rows, :] += mm_nt((scaled * keep).astype(bf16), ds)
            grad = dy[rows, :].astype(f32)
            keep_sum = keep_sum + jnp.sum(scaled * carried, 0, keepdims=True)
            skip_sum = skip_sum + jnp.sum(grad * x, 0, keepdims=True)
            found[0, rows, :] += split_mm(grad * ssm[rows, :] - scaled * dxs, chosen_b)
            found[1, rows, :] += split_mm(x * dxs, chosen_b)
            d_x = taps[5:6, :] * grad + stepped * dxs
            d_pre[rows, :] = d_x * (sig + x * (1.0 - sig))
        met = jnp.sum(ds.astype(f32) * state[...].astype(f32), 0, keepdims=True)
        rest = jnp.zeros((5, WIDE), f32)
        totals_s[...] += lax.dot_general(
            jnp.concatenate([skip_sum, keep_sum, met, rest], 0),
            chosen,
            (((1,), (0,)), ((), ())),
            precision=HIGH,
            preferred_element_type=f32,
        )

    if final:

        @pl.when(step == bc_step)
        def _():
            wide[...] = raw_bc[...].astype(f32)
            for start in range(0, length, TILE):
                rows = pl.ds(start, TILE)
                pre = conv_rows(wide, taps, masks, start, TILE)
                sig = sigmoid(pre)
                slope = sig + pre * sig * (1.0 - sig)
                d_b = db_in[rows, :] + db_acc[rows, :]
                d_c = dc_in[rows, :] + dc_more[rows, :]
                d_pre[rows, :] = jnp.concatenate([d_b, d_c], 1) * slope

    @pl.when(step <= bc_step)
    def _():
        totals = [zero] * (CONV + 1)
        for start in range(0, length, TILE):
            rows = pl.ds(start, TILE)
            grad = d_pre[rows, :]
            totals[CONV] = totals[CONV] + jnp.sum(grad, 0, keepdims=True)
            here = wide[pl.ds(HALO + start, TILE), :]
            totals[CONV - 1] = totals[CONV - 1] + jnp.sum(grad * here, 0, keepdims=True)
            back = taps[CONV - 1 : CONV, :] * grad
            for tap in range(CONV - 1):
                shifted = wide[pl.ds(HALO - CONV + 1 + tap + start, TILE), :]
                masked = grad * twice(masks[tap, rows, :])
                totals[tap] = totals[tap] + jnp.sum(masked * shifted, 0, keepdims=True)
                ahead = d_pre[pl.ds(start + CONV - 1 - tap, TILE), :]
                back = back + taps[tap : tap + 1, :] * ahead * twice(masks[3 + tap, rows, :])
            d_out[rows, :] = back.astype(bf16)
            if start + TILE == length:
                last_out[...] = back[TILE - HALO :, :]
        first_out[...] = d_pre[pl.ds(0, HALO), :]
        for tap in range(CONV + 1):
            sums_out[tap : tap + 1, :] = totals[tap]
        sums_out[CONV + 1 : 8, :] = jnp.zeros((7 - CONV, d_pre.shape[1]), f32)

    if not final:
        head_out[...] = jnp.zeros_like(head_out)
        return

    @pl.when(step == bc_step + 1)
    def _():
        first_out[...] = jnp.zeros_like(first_out)
        last_out[...] = jnp.zeros_like(last_out)
        sums_out[...] = jnp.zeros_like(sums_out)
        rate = jnp.exp(rates[1:2, :])
        end = totals_s[1:2, :] + heads[3, pl.ds(length - 1, 1), :] * totals_s[2:3, :]
        here = lax.broadcasted_iota(jnp.int32, (length, length), 0)
        there = lax.broadcasted_iota(jnp.int32, (length, length), 1)
        upper = jnp.where(here <= there, 1.0, 0.0)
        d_log = lax.dot_general(
            upper, found[0], (((1,), (0,)), ((), ())), precision=HIGH, preferred_element_type=f32
        )
        d_log = d_log + end
        d_dt = (found[1] - rate * d_log) * heads[4]
        d_out[:, :TILE] = d_dt.astype(bf16)
        d_out[:, TILE:] = jnp.zeros((length, WIDE - TILE), bf16)
        head_out[0:1, :] = jnp.sum(d_dt, 0, keepdims=True)
        head_out[1:2, :] = jnp.sum(d_log * (-heads[1] * rate), 0, keepdims=True)
        head_out[2:3, :] = totals_s[0:1, :]
        head_out[3:8, :] = jnp.zeros((5, TILE), f32)


def pack_kernel(sizes, sums, gain_in, gain_out, head, out):
    devices = out.shape[0]
    wide, channels, inner, heads = sizes
    gains = jnp.sum(gain_out[...], 0, keepdims=True)
    for at in range(devices):
        pieces = [gain_in[:, at * wide : (at + 1) * wide]]
        for tap in range(CONV + 1):
            pieces.append(sums[tap : tap + 1, at * channels : (at + 1) * channels])
        pieces.append(gains[:, at * inner : (at + 1) * inner])
        for row in range(3):
            pieces.append(head[row : row + 1, :heads])
        begin = 0
        for piece in pieces:
            out[at, :, begin : begin + piece.shape[1]] = piece
            begin += piece.shape[1]
        if begin < out.shape[2]:
            out[at, :, begin:] = jnp.zeros((1, out.shape[2] - begin), f32)


def scan_kernel(backward, mine, decay, out):
    count = mine.shape[0]

    def one(index, state):
        at = count - 1 - index if backward else index
        out[at] = state.astype(bf16)
        return decay[pl.ds(at, 1), :] * state + mine[at].astype(f32)

    lax.fori_loop(0, count, one, jnp.zeros(mine.shape[1:], f32))


def to_slices(value, devices):
    n_state, inner = value.shape
    across = max(1, devices // 16)
    rows = n_state * across // devices
    value = value.reshape(n_state // rows, rows, across, inner // across)
    return value.transpose(0, 2, 1, 3).reshape(devices, rows, inner // across)


def from_slices(slices, n_state, inner):
    devices, rows, columns = slices.shape
    value = slices.reshape(n_state // rows, inner // columns, rows, columns)
    return value.transpose(0, 2, 1, 3).reshape(n_state, inner)


def exchange(slices):
    return lax.all_to_all(slices, ALL, split_axis=0, concat_axis=0, tiled=True)


def return_slices(states, n_state, inner):
    return from_slices(exchange(states), n_state, inner)


def scan_devices(mine, decay, me, backward):
    devices, heads = decay.shape
    across = max(1, devices // 16)
    wide = jnp.repeat(decay, HEAD_DIM, axis=1).reshape(devices, across, heads * HEAD_DIM // across)
    wide = lax.dynamic_index_in_dim(wide, me % across, 1, False)
    return pl.pallas_call(
        lambda *refs: scan_kernel(backward, *refs),
        out_shape=jax.ShapeDtypeStruct(mine.shape, bf16),
        name="scan_backward" if backward else "scan_forward",
    )(mine, wide)


def flip(axis, bit):
    count = lax.axis_size(axis)
    return [(i, i ^ bit) for i in range(count)]


def other_core(value):
    return lax.ppermute(value, "shard", flip("shard", 1))


class Gather:
    def __init__(self, own, other, base, half, *wait):
        self.own, self.other, self.base, self.half = (own, other, base, half)
        self.mine = lax.axis_index("seq") % 2
        send = lax.dynamic_slice_in_dim(own, base + self.mine * half, half, 0)
        if wait:
            send = after(send, *wait)
        self.send = send
        self.direct = lax.ppermute(send, "shard", flip("shard", 2))

    def share(self, *wait):
        if wait:
            self.direct = after(self.direct, *wait)
        self.passed = lax.ppermute(self.direct, "seq", flip("seq", 1))

    def cross(self, *wait):
        direct, passed = (self.direct, self.passed)
        if wait:
            direct, passed = lax.optimization_barrier((direct, passed) + wait)[:2]
        self.parts = [direct, other_core(direct), passed, other_core(passed)]

    def turns(self):
        shard = lax.axis_index("shard")
        return [shard, shard ^ 1, shard ^ 2, shard ^ 3]


def project_kernel(table, *refs):
    lefts, (own, other, direct, direct_o, passed, passed_o, out, left) = (refs[:4], refs[4:])
    step = pl.program_id(0)

    @pl.when(step == 0)
    def _():
        left[...] = jnp.concatenate([a[...] for a in lefts], 1)

    def product(far, far_o):
        weight = jnp.concatenate([own[...], other[...], far[...], far_o[...]], 1)
        out[...] = mm_nt(left[...], weight).astype(bf16)

    near = pl.num_programs(0) // 2
    pl.when(step < near)(lambda: product(direct, direct_o))
    pl.when(step >= near)(lambda: product(passed, passed_o))


def project(value, gather):
    rows = value.shape[0]
    deep = gather.own.shape[1]
    near = gather.half // PIECE
    base = gather.base // PIECE
    order = [near * gather.mine + at for at in range(near)]
    order += [near * (1 - gather.mine) + at for at in range(near)]
    table = jnp.stack(gather.turns() + order).astype(jnp.int32)
    block = lambda index: pl.BlockSpec((PIECE, deep), index)
    left = lambda k: pl.BlockSpec((rows, deep), lambda j, t: (0, t[k]))
    own = block(lambda j, t: (base + t[4 + j], 0))
    first = block(lambda j, t: (jnp.minimum(j, near - 1), 0))
    second = block(lambda j, t: (jnp.maximum(j - near, 0), 0))
    return pl.pallas_call(
        project_kernel,
        grid_spec=pltpu.PrefetchScalarGridSpec(
            num_scalar_prefetch=1,
            grid=(2 * near,),
            in_specs=[left(k) for k in range(4)] + [own, own, first, first, second, second],
            out_specs=pl.BlockSpec((rows, PIECE), lambda j, t: (0, t[4 + j])),
            scratch_shapes=[pltpu.VMEM((rows, 4 * deep), bf16)],
        ),
        out_shape=jax.ShapeDtypeStruct((rows, 2 * gather.half), bf16),
        compiler_params=pltpu.CompilerParams(vmem_limit_bytes=58 * 1024 * 1024),
        cost_estimate=pl.CostEstimate(
            flops=16 * rows * deep * gather.half,
            bytes_accessed=16 * deep * gather.half,
            transcendentals=0,
        ),
        name="project",
    )(table, *([value] * 4), gather.own, gather.other, *gather.parts)


def back_kernel(values, table, *refs):
    (own, other, direct, direct_o, passed, passed_o, out, total) = refs[-8:]
    start = refs[values : len(refs) - 8]
    step = pl.program_id(0)
    last = pl.num_programs(0) - 1
    deep = own.shape[1]
    place = lambda k: pl.ds(pl.multiple_of(table[k] * deep, deep), deep)

    @pl.when(step == 0)
    def _():
        if start:
            for k in range(4):
                total[:, k * deep : (k + 1) * deep] = start[0][:, place(k)]
        else:
            total[...] = jnp.zeros_like(total)

    def product(value, far, far_o):
        weight = jnp.concatenate([own[...], other[...], far[...], far_o[...]], 1)
        total[...] += mm(value[...], weight)

    near = table[4 + step] == 1
    for at in range(values):
        mine = (step * values // (last + 1)) == at
        pl.when(mine & near)(lambda at=at: product(refs[at], direct, direct_o))
        pl.when(mine & jnp.logical_not(near))(lambda at=at: product(refs[at], passed, passed_o))

    @pl.when(step == last)
    def _():
        for k in range(4):
            out[:, place(k)] = total[:, k * deep : (k + 1) * deep]


def back(values, gather, start):
    rows = values[0].shape[0]
    deep = gather.own.shape[1]
    count = 2 * gather.half // PIECE
    share = count // len(values)
    near = gather.half // PIECE
    base = gather.base // PIECE
    mine = gather.mine
    flags, direct, passed = ([], [], [])
    for at in range(count):
        half, place = (at // near, at % near)
        is_near = mine == half
        ends = lambda own: jnp.where(own > half, 0, near - 1)
        flags.append(is_near)
        direct.append(jnp.where(is_near, place, ends(mine)))
        passed.append(jnp.where(is_near, ends(1 - mine), place))
    table = jnp.stack([jnp.asarray(v, jnp.int32) for v in gather.turns() + flags + direct + passed])
    block = lambda index: pl.BlockSpec((PIECE, deep), index)
    whole = pl.BlockSpec((rows, 4 * deep), lambda j, t: (0, 0))
    own = block(lambda j, t: (base + j, 0))
    one = block(lambda j, t: (t[4 + count + j], 0))
    two = block(lambda j, t: (t[4 + 2 * count + j], 0))
    in_specs = [
        pl.BlockSpec((rows, PIECE), lambda j, t, k=k: (0, jnp.clip(j - k * share, 0, share - 1)))
        for k in range(len(values))
    ]
    started = [] if start is None else [start]
    in_specs += [whole] * len(started) + [own, own, one, one, two, two]
    return pl.pallas_call(
        lambda *refs: back_kernel(len(values), *refs),
        grid_spec=pltpu.PrefetchScalarGridSpec(
            num_scalar_prefetch=1,
            grid=(count,),
            in_specs=in_specs,
            out_specs=whole,
            scratch_shapes=[pltpu.VMEM((rows, 4 * deep), f32)],
        ),
        out_shape=jax.ShapeDtypeStruct((rows, 4 * deep), f32),
        compiler_params=pltpu.CompilerParams(vmem_limit_bytes=58 * 1024 * 1024),
        cost_estimate=pl.CostEstimate(
            flops=16 * rows * deep * gather.half,
            bytes_accessed=16 * deep * gather.half,
            transcendentals=0,
        ),
        name="back",
    )(table, *values, *started, gather.own, gather.other, *gather.parts)


def by_shard(gather):
    half, width = (gather.half, gather.own.shape[1])
    whole = pl.BlockSpec((2 * half, width), lambda g, t: (0, 0))
    part = pl.BlockSpec((half, width), lambda g, t: (0, 0))
    direct, direct_o, passed, passed_o = gather.parts
    operands = [gather.own, gather.other, direct, passed, direct_o, passed_o]
    table = jnp.stack(gather.turns() + [gather.mine]).astype(jnp.int32)
    return operands, [whole] * 2 + [part] * 4, table


def out_back_kernel(table, value, own, other, direct, passed, direct_o, passed_o, out):
    step = pl.program_id(0)
    half = direct.shape[0]

    def two(near, far):
        out[:, pl.ds(pl.multiple_of(table[4] * half, half), half)] = mm_nt(value[...], near[...])
        far_at = pl.multiple_of((1 - table[4]) * half, half)
        out[:, pl.ds(far_at, half)] = mm_nt(value[...], far[...])

    for at, piece in enumerate((own, other)):

        @pl.when(step == at)
        def _(piece=piece):
            out[...] = mm_nt(value[...], piece[...])

    pl.when(step == 2)(lambda: two(direct, passed))
    pl.when(step == 3)(lambda: two(direct_o, passed_o))


def out_back(value, gather):
    rows, width = value.shape
    operands, specs, table = by_shard(gather)
    size = 2 * gather.half
    return pl.pallas_call(
        out_back_kernel,
        grid_spec=pltpu.PrefetchScalarGridSpec(
            num_scalar_prefetch=1,
            grid=(4,),
            in_specs=[pl.BlockSpec((rows, width), lambda g, t: (0, 0))] + specs,
            out_specs=pl.BlockSpec((rows, size), lambda g, t: (0, t[g])),
        ),
        out_shape=jax.ShapeDtypeStruct((rows, 4 * size), f32),
        compiler_params=pltpu.CompilerParams(vmem_limit_bytes=58 * 1024 * 1024),
        cost_estimate=pl.CostEstimate(
            flops=8 * rows * width * size, bytes_accessed=8 * width * size, transcendentals=0
        ),
        name="out_back",
    )(table, value, *operands)


def out_forward_kernel(table, value, base, own, other, direct, passed, direct_o, passed_o, out, total):
    step = pl.program_id(0)
    half = direct.shape[0]

    def two(near, far):
        near_at = pl.multiple_of(table[4] * half, half)
        far_at = pl.multiple_of((1 - table[4]) * half, half)
        total[...] += mm(value[:, pl.ds(near_at, half)], near[...])
        total[...] += mm(value[:, pl.ds(far_at, half)], far[...])

    @pl.when(step == 0)
    def _():
        total[...] = base[...].astype(f32) + mm(value[...], own[...])

    @pl.when(step == 1)
    def _():
        total[...] += mm(value[...], other[...])

    pl.when(step == 2)(lambda: two(direct, passed))

    @pl.when(step == 3)
    def _():
        two(direct_o, passed_o)
        out[...] = total[...].astype(bf16)


def out_forward(value, base, gather):
    rows = value.shape[0]
    operands, specs, table = by_shard(gather)
    size = 2 * gather.half
    width = gather.own.shape[1]
    fixed = pl.BlockSpec((rows, width), lambda g, t: (0, 0))
    return pl.pallas_call(
        out_forward_kernel,
        grid_spec=pltpu.PrefetchScalarGridSpec(
            num_scalar_prefetch=1,
            grid=(4,),
            in_specs=[pl.BlockSpec((rows, size), lambda g, t: (0, t[g])), fixed] + specs,
            out_specs=fixed,
            scratch_shapes=[pltpu.VMEM((rows, width), f32)],
        ),
        out_shape=jax.ShapeDtypeStruct((rows, width), bf16),
        compiler_params=pltpu.CompilerParams(vmem_limit_bytes=58 * 1024 * 1024),
        cost_estimate=pl.CostEstimate(
            flops=8 * rows * width * size, bytes_accessed=8 * width * size, transcendentals=0
        ),
        name="out_forward",
    )(table, value, base, *operands)


def stacked_project_kernel(value, *rest):
    weight = jnp.concatenate([w[...] for w in rest[:-1]], 1)
    rest[-1][...] = mm_nt(value[...], weight).astype(bf16)


def stacked_project(value, stack, base, count):
    rows = value.shape[0]
    shards, _, deep = stack.shape
    first = base // WIDE
    specs = [
        pl.BlockSpec((None, WIDE, deep), lambda j, k=k: (k, first + j, 0)) for k in range(shards)
    ]
    return pl.pallas_call(
        stacked_project_kernel,
        grid=(count // WIDE,),
        in_specs=[pl.BlockSpec((rows, shards * deep), lambda j: (0, 0))] + specs,
        out_specs=pl.BlockSpec((rows, WIDE), lambda j: (0, j)),
        out_shape=jax.ShapeDtypeStruct((rows, count), bf16),
        compiler_params=pltpu.CompilerParams(vmem_limit_bytes=58 * 1024 * 1024),
        cost_estimate=pl.CostEstimate(
            flops=2 * rows * shards * deep * count,
            bytes_accessed=2 * shards * deep * count,
            transcendentals=0,
        ),
        name="stacked_project",
    )(value, *([stack] * shards))


def stacked_back_kernel(value, *rest):
    out, total = rest[-2:]
    step = pl.program_id(0)

    @pl.when(step == 0)
    def _():
        total[...] = jnp.zeros_like(total)

    weight = jnp.concatenate([w[...] for w in rest[:-2]], 1)
    total[...] += mm(value[...], weight)

    @pl.when(step == pl.num_programs(0) - 1)
    def _():
        out[...] = total[...]


def stacked_back(value, stack, base):
    rows, count = value.shape
    shards, _, deep = stack.shape
    size = WIDE
    first = base // size
    specs = [
        pl.BlockSpec((None, size, deep), lambda j, k=k: (k, first + j, 0)) for k in range(shards)
    ]
    return pl.pallas_call(
        stacked_back_kernel,
        grid=(count // size,),
        in_specs=[pl.BlockSpec((rows, size), lambda j: (0, j))] + specs,
        out_specs=pl.BlockSpec((rows, shards * deep), lambda j: (0, 0)),
        out_shape=jax.ShapeDtypeStruct((rows, shards * deep), f32),
        scratch_shapes=[pltpu.VMEM((rows, shards * deep), f32)],
        compiler_params=pltpu.CompilerParams(vmem_limit_bytes=58 * 1024 * 1024),
        cost_estimate=pl.CostEstimate(
            flops=2 * rows * shards * deep * count,
            bytes_accessed=2 * shards * deep * count,
            transcendentals=0,
        ),
        name="stacked_back",
    )(value, *([stack] * shards))


def halve(value, dim, axis, bit, mine, wait):
    shape = value.shape
    value = value.reshape(shape[:dim] + (shape[dim] // 2, 2) + shape[dim + 1 :])
    send = lax.dynamic_index_in_dim(value, 1 - mine, dim + 1, False)
    kept = lax.dynamic_index_in_dim(value, mine, dim + 1, False)
    came = lax.ppermute(send, axis, flip(axis, bit))
    if wait:
        came = after(came, *wait)
    return (kept.astype(f32) + came.astype(f32)).astype(bf16), send


class RowSum:
    def __init__(self, partial, far_first):
        shards, places = (lax.axis_size("shard"), lax.axis_size("seq"))
        shard, place = (lax.axis_index("shard"), lax.axis_index("seq"))
        rows, columns = partial.shape
        chips = shards // 2
        self.value = partial.reshape(chips, places, rows // (chips * places), columns)
        far = [(0, "shard", 2 << k, (shard >> (k + 1)) & 1) for k in range(chips.bit_length() - 1)]
        near = [(1, "seq", 1 << k, (place >> k) & 1) for k in range(places.bit_length() - 1)]
        self.order = far + near if far_first else near[:1] + far + near[1:]

    def step(self, *wait):
        if not self.order:
            return
        dim, axis, bit, mine = self.order.pop(0)
        self.value, self.send = halve(self.value, dim, axis, bit, mine, wait)

    def rows(self):
        return self.value.reshape(self.value.shape[2:])


def core_rows(value, core):
    shards = lax.axis_size("shard")
    size = value.shape[1] // shards
    even = [value[:, at * size : (at + 1) * size] for at in range(0, shards, 2)]
    odd = [value[:, at * size : (at + 1) * size] for at in range(1, shards, 2)]
    own = [jnp.where(core == 0, a, b) for a, b in zip(even, odd)]
    rest = [jnp.where(core == 0, b, a) for a, b in zip(even, odd)]
    return jnp.concatenate(own, 1), jnp.concatenate(rest, 1)


def after(value, *others):
    return lax.optimization_barrier((value,) + others)[0]


def turn_blocks(value, shard):
    shards = lax.axis_size("shard")
    size = value.shape[1] // shards
    blocks = [
        lax.dynamic_slice_in_dim(value, (at ^ shard) * size, size, 1) for at in range(shards)
    ]
    return jnp.concatenate(blocks, 1)


def on_device(
    hidden,
    cotangent,
    seg_ids,
    norm_gain,
    in_weight,
    conv_weight,
    conv_bias,
    dt_bias,
    a_log,
    d_skip,
    out_gain,
    out_weight,
):
    shards, places = (lax.axis_size("shard"), lax.axis_size("seq"))
    shard, place = (lax.axis_index("shard"), lax.axis_index("seq"))
    devices = shards * places
    me = shard * places + place
    length, width = hidden.shape
    heads = dt_bias.shape[0]
    inner = out_weight.shape[0] * shards
    channels = conv_bias.shape[0] * shards
    n_state = (channels - inner) // 2
    groups = inner // WIDE
    start = me * length

    core = shard % 2
    w_in = in_weight.T
    by_hand = shards == 4 and places % 2 == 0
    edge_rows = w_in.shape[0] - 2 * inner
    small = jnp.concatenate([norm_gain, conv_weight.reshape(-1), conv_bias, out_gain])
    small_rows = pl.cdiv(small.shape[0], w_in.shape[1])
    small_rows += -(small_rows + edge_rows) % 16
    small = jnp.pad(small, (0, small_rows * w_in.shape[1] - small.shape[0]))
    edges = jnp.concatenate([w_in[2 * inner :], small.reshape(small_rows, w_in.shape[1])], 0)
    if by_hand:
        in_other = other_core(w_in)
        g_x = Gather(w_in, in_other, inner, inner // 2)
        edges = after(edges, g_x.send)
    edges = jnp.broadcast_to(edges[None], (shards, *edges.shape))
    edges = lax.all_to_all(edges, "shard", split_axis=0, concat_axis=0, tiled=True)
    w_edge = edges[:, :edge_rows].transpose(1, 0, 2).reshape(edge_rows, width)
    w_edge = jnp.pad(w_edge, ((0, -edge_rows % TILE), (0, 0)))
    small = edges[:, edge_rows:].reshape(shards, -1)
    if by_hand:
        g_x.share()
        g_x.cross()
        g_z = Gather(w_in, in_other, 0, inner // 2, g_x.direct)
        g_z.share()
        out_other = other_core(after(out_weight, g_x.direct))
        g_out = Gather(out_weight, out_other, 0, out_weight.shape[0] // 2, g_z.direct)
    else:
        stack_x = lax.all_gather(w_in[inner : 2 * inner], "shard")
        stack_z = lax.all_gather(w_in[:inner], "shard")
        w_out = lax.all_gather(out_weight, "shard", axis=0, tiled=True)
    at = 0
    gain_in = small[:, at : at + norm_gain.shape[0]].reshape(-1).astype(f32)
    at += norm_gain.shape[0]
    taps = small[:, at : at + conv_weight.size].reshape(shards, CONV, -1)
    taps = taps.transpose(1, 0, 2).reshape(CONV, channels).astype(f32)
    at += conv_weight.size
    bias = small[:, at : at + conv_bias.shape[0]].reshape(-1).astype(f32)
    at += conv_bias.shape[0]
    gain_out = small[:, at : at + out_gain.shape[0]].reshape(-1).astype(f32)
    skip_wide = jnp.repeat(d_skip.astype(f32), HEAD_DIM)
    rows = jnp.concatenate([skip_wide, jnp.zeros((channels - inner,), f32)])
    taps8 = jnp.concatenate([taps, bias[None], rows[None], jnp.zeros((2, channels), f32)], 0)

    edge = jnp.full((HALO,), -1, jnp.int32)
    padded = jnp.concatenate([edge, seg_ids, edge - 1])
    near = lax.dynamic_slice_in_dim(padded, start, length + 2 * HALO)
    seg = near[HALO : HALO + length]
    fwd_masks = [near[HALO - CONV + 1 + k : HALO - CONV + 1 + k + length] == seg for k in range(3)]
    spot = jnp.arange(length, dtype=jnp.int32)
    bwd_masks = [
        (near[HALO + CONV - 1 - k : HALO + CONV - 1 - k + length] == seg)
        & (spot + CONV - 1 - k < length)
        for k in range(3)
    ]
    from_before = seg == near[HALO - 1]
    to_last = seg == seg[length - 1]
    flags = jnp.stack(
        [m.astype(f32) for m in fwd_masks + bwd_masks + [seg, from_before, to_last]], 1
    )
    flags = jnp.pad(flags, ((0, 0), (0, 16 - flags.shape[1])))
    seg_row = jnp.broadcast_to(seg.astype(f32)[None, :], (8, length))

    behind = lax.ppermute(
        hidden[length - HALO :], ALL, [(i, i + 1) for i in range(devices - 1)]
    )
    hidden_f = jnp.concatenate([behind, hidden], 0).astype(f32)
    scale_in = lax.rsqrt(jnp.mean(hidden_f * hidden_f, axis=1, keepdims=True) + EPS)
    normed_ext = (hidden_f * scale_in * gain_in[None, :]).astype(bf16)
    normed_in = normed_ext[HALO:]
    proj_edge = mm_nt(normed_ext, w_edge).astype(bf16)
    proj_bc = proj_edge[:, : 2 * n_state]
    rates = jnp.stack([dt_bias, a_log]).astype(f32)
    rates = jnp.pad(rates, ((0, 6), (0, TILE - heads)))
    big = pltpu.CompilerParams(vmem_limit_bytes=56 * 1024 * 1024)
    per_head, spreads, cum, sums_row, masks = pl.pallas_call(
        prepare_kernel,
        out_shape=[
            jax.ShapeDtypeStruct((5, length, TILE), f32),
            jax.ShapeDtypeStruct((2, length, 2 * TILE), bf16),
            jax.ShapeDtypeStruct((groups, length, GROUP), f32),
            jax.ShapeDtypeStruct((groups, GROUP, length), f32),
            jax.ShapeDtypeStruct((2 * (CONV - 1), length, TILE), f32),
        ],
        compiler_params=big,
        name="prepare",
    )(proj_edge[HALO:, 2 * n_state :], rates, flags)
    end = per_head[3, length - 1, :heads]
    decays = jnp.broadcast_to(end[None, None, :], (devices, 1, heads))
    decays = lax.all_to_all(decays, ALL, split_axis=0, concat_axis=0, tiled=True)[:, 0, :]
    if by_hand:
        proj = project(after(normed_ext, g_z.direct, decays), g_x)
    else:
        proj = stacked_project(normed_ext, stack_x, 0, inner)

    def whole(shape):
        return pl.BlockSpec(shape, lambda g: (0,) * len(shape))

    def group_of(g):
        return jnp.maximum(g - 1, 0)

    order = lambda g: jnp.where(g == 0, groups, g - 1)
    x_conv, state_local, bc, bt, ct = pl.pallas_call(
        state_kernel,
        grid=(groups + 1,),
        in_specs=[
            pl.BlockSpec((length + HALO, WIDE), lambda g: (0, group_of(g))),
            whole((length + HALO, WIDE)),
            pl.BlockSpec((8, WIDE), lambda g: (0, order(g))),
            whole(masks.shape),
            whole(spreads.shape),
        ],
        out_specs=[
            pl.BlockSpec((length, WIDE), lambda g: (0, group_of(g))),
            pl.BlockSpec((n_state, WIDE), lambda g: (0, group_of(g))),
            whole((length, 2 * n_state)),
            whole((n_state, length)),
            whole((n_state, length)),
        ],
        out_shape=[
            jax.ShapeDtypeStruct((length, inner), bf16),
            jax.ShapeDtypeStruct((n_state, inner), bf16),
            jax.ShapeDtypeStruct((length, 2 * n_state), bf16),
            jax.ShapeDtypeStruct((n_state, length), bf16),
            jax.ShapeDtypeStruct((n_state, length), bf16),
        ],
        scratch_shapes=[
            pltpu.VMEM((length + HALO, WIDE), f32),
            pltpu.VMEM((n_state, length), bf16),
        ],
        compiler_params=big,
        cost_estimate=pl.CostEstimate(
            flops=20 * length * inner * n_state, bytes_accessed=10 * length * inner, transcendentals=0
        ),
        name="mixer_state",
    )(proj, proj_bc, taps8, masks, spreads)

    if by_hand:
        slices = after(to_slices(state_local, devices), g_out.direct)
        g_out.share(slices)
        sent = exchange(slices)
        g_z.cross(slices)
        gate_z = project(after(normed_in, slices), g_z)
        states = scan_devices(after(sent, gate_z), decays, me, False)
    else:
        sent = exchange(to_slices(state_local, devices))
        gate_z = stacked_project(normed_in, stack_z, 0, inner)
        states = scan_devices(sent, decays, me, False)
    state_in = return_slices(states, n_state, inner)
    x_conv = after(x_conv, states)
    half_t = 2 * TILE
    y_local = pl.pallas_call(
        forward_kernel,
        grid=(groups,),
        in_specs=[
            pl.BlockSpec((length, WIDE), lambda g: (0, g)),
            whole(flags.shape),
            whole((8, length)),
            whole(spreads.shape),
            pl.BlockSpec((1, length, GROUP), lambda g: (g, 0, 0)),
            pl.BlockSpec((1, GROUP, length), lambda g: (g, 0, 0)),
            whole((length, 2 * n_state)),
            whole((n_state, length)),
        ],
        out_specs=pl.BlockSpec((length, WIDE), lambda g: (0, g)),
        out_shape=jax.ShapeDtypeStruct((length, inner), f32),
        scratch_shapes=[
            pltpu.VMEM((length, length), f32),
            pltpu.VMEM((length // half_t, GROUP * half_t, WIDE), bf16),
            pltpu.VMEM((length // half_t, length, GROUP * half_t), bf16),
        ],
        compiler_params=big,
        cost_estimate=pl.CostEstimate(
            flops=16 * length * length * inner, bytes_accessed=10 * length * inner, transcendentals=0
        ),
        name="mixer_forward",
    )(x_conv, flags, seg_row, spreads, cum, sums_row, bc, bt)
    if by_hand:
        g_out.cross(y_local)
        d_normed = out_back(after(cotangent, y_local), g_out)
    else:
        d_normed = mm_nt(cotangent, w_out)
    block = TILE
    tall = lambda dim: pl.BlockSpec((block, dim), lambda g: (g, 0))
    gains = jnp.stack([gain_out, skip_wide], 0)
    ssm, normed_out, d_z, d_y, d_state_local, dc_more, d_gain = pl.pallas_call(
        gate_kernel,
        grid=(length // block,),
        in_specs=[
            tall(inner),
            tall(inner),
            tall(inner),
            tall(inner),
            tall(2 * n_state),
            pl.BlockSpec((n_state, block), lambda g: (0, g)),
            pl.BlockSpec((None, block, TILE), lambda g: (3, g, 0)),
            whole((n_state, inner)),
            whole((2, inner)),
        ],
        out_specs=[
            tall(inner),
            tall(inner),
            tall(inner),
            tall(inner),
            whole((n_state, inner)),
            tall(n_state),
            whole((8, inner)),
        ],
        out_shape=[
            jax.ShapeDtypeStruct((length, inner), f32),
            jax.ShapeDtypeStruct((length, inner), bf16),
            jax.ShapeDtypeStruct((length, inner), bf16),
            jax.ShapeDtypeStruct((length, inner), bf16),
            jax.ShapeDtypeStruct((n_state, inner), bf16),
            jax.ShapeDtypeStruct((length, n_state), f32),
            jax.ShapeDtypeStruct((8, inner), f32),
        ],
        scratch_shapes=[
            pltpu.VMEM((block, inner), f32),
            pltpu.VMEM((block, inner), f32),
            pltpu.VMEM((block, inner), bf16),
            pltpu.VMEM((n_state, inner), f32),
        ],
        compiler_params=big,
        cost_estimate=pl.CostEstimate(
            flops=8 * length * n_state * inner, bytes_accessed=22 * length * inner, transcendentals=0
        ),
        name="mixer_gate",
    )(y_local, x_conv, gate_z, d_normed, bc, ct, per_head, state_in, gains)

    slices = to_slices(d_state_local, devices)
    sent = exchange(slices)
    normed_out, d_z = (after(normed_out, slices), after(d_z, slices))

    def both(value):
        return jnp.concatenate([value, other_core(value)], 0)

    def both_rows(value):
        own, rest = core_rows(value, core)
        return jnp.concatenate([own, other_core(rest)], 0)

    normed_pair = both_rows(normed_in)
    cot_pair = both(cotangent)
    out_pair = both_rows(normed_out)
    z_pair = both(d_z)
    if by_hand:
        block_out = out_forward(normed_out, hidden, g_out)
    else:
        block_out = (hidden.astype(f32) + mm(normed_out, w_out)).astype(bf16)
    grad_o = mm_tn(after(out_pair, block_out), cot_pair).astype(bf16)
    states = scan_devices(after(sent, grad_o), decays, me, True)
    returned = exchange(states)
    grad_z = mm_tn(normed_pair, after(z_pair, states)).astype(bf16)
    half_o, half_z = (width // 2, inner // 2)
    grad_o = after(grad_o, grad_z)
    sums_o = [RowSum(grad_o[:, :half_o], True), RowSum(grad_o[:, half_o:], False)]
    sums_z = [RowSum(grad_z[:, :half_z], True), RowSum(grad_z[:, half_z:], False)]
    x_conv = after(x_conv, grad_o, grad_z)

    dxs, db_in, dc_in = pl.pallas_call(
        inside_kernel,
        grid=(groups,),
        in_specs=[
            pl.BlockSpec((length, WIDE), lambda g: (0, g)),
            whole(flags.shape),
            whole((8, length)),
            whole(spreads.shape),
            pl.BlockSpec((1, length, GROUP), lambda g: (g, 0, 0)),
            pl.BlockSpec((1, GROUP, length), lambda g: (g, 0, 0)),
            whole((length, 2 * n_state)),
            whole((n_state, length)),
            pl.BlockSpec((length, WIDE), lambda g: (0, g)),
        ],
        out_specs=[
            pl.BlockSpec((length, WIDE), lambda g: (0, g)),
            whole((length, n_state)),
            whole((length, n_state)),
        ],
        out_shape=[
            jax.ShapeDtypeStruct((length, inner), f32),
            jax.ShapeDtypeStruct((length, n_state), f32),
            jax.ShapeDtypeStruct((length, n_state), f32),
        ],
        scratch_shapes=[
            pltpu.VMEM((length, length), f32),
            pltpu.VMEM((length, length), f32),
            pltpu.VMEM((length // half_t, GROUP * half_t, WIDE), bf16),
            pltpu.VMEM((length // half_t, length, GROUP * half_t), bf16),
            pltpu.VMEM((GROUP, length, WIDE), bf16),
            pltpu.VMEM((2, length, length), f32),
        ],
        compiler_params=big,
        cost_estimate=pl.CostEstimate(
            flops=8 * length * length * inner, bytes_accessed=10 * length * inner, transcendentals=0
        ),
        name="mixer_inside",
    )(x_conv, flags, seg_row, spreads, cum, sums_row, bc, ct, d_y)

    for chain in sums_o:
        chain.step(dxs)
    d_state = from_slices(after(returned, dxs), n_state, inner)
    taps8 = jnp.pad(taps8, ((0, 0), (0, WIDE)))

    def outside(first_group, count, final, grad, running):
        kept = lambda g: jnp.minimum(g, count - 1) + first_group
        steps = count + (2 if final else 0)
        columns = steps * WIDE
        tall = lambda: pl.BlockSpec((length, WIDE), lambda g: (0, kept(g)))
        flat = lambda: pl.BlockSpec((n_state, WIDE), lambda g: (0, kept(g)))
        return pl.pallas_call(
            lambda *refs: outside_kernel(first_group, count, final, *refs),
            grid=(steps,),
            in_specs=[
                pl.BlockSpec((length + HALO, WIDE), lambda g: (0, kept(g))),
                whole((length + HALO, WIDE)),
                pl.BlockSpec((8, WIDE), lambda g: (0, first_group + g)),
                whole(masks.shape),
                whole(spreads.shape),
                whole(per_head.shape),
                whole(rates.shape),
                whole((length, 2 * n_state)),
                tall(),
                tall(),
                tall(),
                flat(),
                flat(),
                whole((length, n_state)),
                whole((length, n_state)),
                whole((length, n_state)),
                whole((length, n_state)),
                whole((2, length, TILE)),
                whole((8, TILE)),
            ],
            out_specs=[
                pl.BlockSpec((length, WIDE), lambda g: (0, g)),
                pl.BlockSpec((HALO, WIDE), lambda g: (0, g)),
                pl.BlockSpec((HALO, WIDE), lambda g: (0, g)),
                pl.BlockSpec((8, WIDE), lambda g: (0, g)),
                whole((8, TILE)),
                whole((length, n_state)),
                whole((2, length, TILE)),
                whole((8, TILE)),
            ],
            out_shape=[
                jax.ShapeDtypeStruct((length, columns), bf16),
                jax.ShapeDtypeStruct((HALO, columns), f32),
                jax.ShapeDtypeStruct((HALO, columns), f32),
                jax.ShapeDtypeStruct((8, columns), f32),
                jax.ShapeDtypeStruct((8, TILE), f32),
                jax.ShapeDtypeStruct((length, n_state), f32),
                jax.ShapeDtypeStruct((2, length, TILE), f32),
                jax.ShapeDtypeStruct((8, TILE), f32),
            ],
            scratch_shapes=[
                pltpu.VMEM((length + HALO, WIDE), f32),
                pltpu.VMEM((length + HALO, WIDE), f32),
            ],
            compiler_params=big,
            cost_estimate=pl.CostEstimate(
                flops=8 * length * n_state * columns,
                bytes_accessed=16 * length * columns,
                transcendentals=0,
            ),
            name="mixer_outside",
        )(proj, proj_bc, taps8, masks, spreads, per_head, rates, bc, grad, ssm, dxs, d_state,
          state_in, db_in, dc_in, dc_more, *running)

    seg_end = near[length : length + 2 * HALO]

    def finish(grads, first, last, start):
        ahead = lax.ppermute(first, ALL, [(i + 1, i) for i in range(devices - 1)])
        joined = jnp.concatenate([jnp.zeros_like(first), ahead], 0)
        for tap in range(CONV - 1):
            lead = CONV - 1 - tap
            same = (seg_end[lead : lead + HALO] == seg_end[:HALO]).astype(f32)[:, None]
            here = taps8[tap, start : start + first.shape[1]]
            last = last + here[None, :] * joined[lead : lead + HALO] * same
        count = min(channels - start, first.shape[1])
        return lax.dynamic_update_slice(grads, last[:, :count].astype(bf16), (length - HALO, 0))

    running = (
        jnp.zeros((length, n_state), f32),
        jnp.zeros((2, length, TILE), f32),
        jnp.zeros((8, TILE), f32),
    )
    part = groups // 2
    half_x = part * WIDE

    values = lambda *chains: [chain.value for chain in chains]
    grad = after(d_y, *values(*sums_o))
    d_one, first, last, sums_one, _, *running = outside(0, part, False, grad, running)
    for chain in sums_z + sums_o:
        chain.step(d_one)
    d_one = finish(d_one, first, last, 0)
    one_pair = both(d_one)
    if by_hand:
        d_normed_in = back([after(d_z, d_one)], g_z, None)
    else:
        d_normed_in = stacked_back(d_z, stack_z, 0)
    grad_x = mm_tn(normed_pair, after(one_pair, d_normed_in)).astype(bf16)
    sum_a = RowSum(grad_x, True)
    grad = after(d_y, grad_x, *values(*sums_o, *sums_z))
    d_two, first, last, sums_two, head_sums, *_ = outside(part, groups - part, True, grad, running)
    sums = jnp.concatenate([sums_one, sums_two], 1)
    for chain in sums_z + sums_o + [sum_a]:
        chain.step(d_two)
    d_two = finish(d_two, first, last, half_x)
    two_pair = both(d_two)
    count = inner - half_x
    edge = after(d_two, *values(sum_a))[:, count : count + w_edge.shape[0]]
    d_normed_in = d_normed_in + mm(edge, w_edge)
    grad_y = mm_tn(normed_pair, after(two_pair, d_normed_in)).astype(bf16)
    half = grad_y.shape[1] // 2
    sums_b = [RowSum(grad_y[:, :half], True), RowSum(grad_y[:, half:], False)]
    for chain in sums_z + sums_o + [sum_a]:
        chain.step(grad_y)
    if by_hand:
        d_normed_in = back([d_one, after(d_two, grad_y)], g_x, d_normed_in)
    else:
        d_x = jnp.concatenate([d_one, d_two[:, :count]], 1)
        d_normed_in = d_normed_in + stacked_back(d_x, stack_x, 0)
    for chain in sums_b + [sum_a]:
        chain.step(d_normed_in)
    d_normed_in = after(d_normed_in, *values(sum_a, *sums_b))
    sums_x = [sum_a] + sums_b
    base = hidden_f[HALO:]
    scale = scale_in[HALO:]
    d_hat = d_normed_in * gain_in[None, :]
    mean = jnp.mean(d_hat * base, axis=1, keepdims=True)
    grad_hidden = cotangent.astype(f32) + scale * d_hat - base * (scale * scale * scale * mean)
    grad_gain_in = jnp.sum(d_normed_in * base * scale, 0)
    while any(chain.order for chain in sums_o + sums_z + sums_x):
        for chain in sums_x + sums_o + sums_z:
            chain.step(grad_gain_in)
    counts = [width // devices] + [channels // devices] * (CONV + 1) + [inner // devices]
    counts += [heads] * 3
    total = sum(counts)
    if by_hand:
        sizes = (width // devices, channels // devices, inner // devices, heads)
        packed = pl.pallas_call(
            lambda *refs: pack_kernel(sizes, *refs),
            out_shape=jax.ShapeDtypeStruct((devices, 1, total + -total % TILE), f32),
            name="pack",
        )(sums[:, :channels], grad_gain_in[None], d_gain, head_sums)
    else:
        slots = lambda v: v.reshape(-1, devices, v.shape[-1] // devices).transpose(1, 0, 2)
        same = jnp.broadcast_to(head_sums[:3, :heads].reshape(1, -1), (devices, 3 * heads))
        pieces = [slots(grad_gain_in), slots(sums[: CONV + 1, :channels])]
        pieces += [slots(jnp.sum(d_gain, 0)), same]
        packed = jnp.concatenate([p.reshape(devices, -1) for p in pieces], 1)[:, None]
    packed = lax.all_to_all(packed, ALL, split_axis=0, concat_axis=0, tiled=True).sum((0, 1))
    found, at = ([], 0)
    for size in counts:
        found.append(packed[at : at + size])
        at += size

    grads = [c.rows().astype(f32) for c in sums_z + sums_x]
    excess = sum(g.shape[1] for g in grads) - w_in.shape[0]
    grads[-1] = grads[-1][:, : grads[-1].shape[1] - excess]
    return (
        block_out,
        grad_hidden,
        found[0],
        jnp.concatenate(grads, 1),
        jnp.stack(found[1 : CONV + 1]),
        found[CONV + 1],
        found[CONV + 3],
        found[CONV + 4],
        found[CONV + 5],
        found[CONV + 2],
        jnp.concatenate([c.rows().astype(f32) for c in sums_o], 1),
    )


def solution(mesh):
    return jax.shard_map(
        on_device,
        mesh=mesh,
        in_specs=(
            P(ALL, None),
            P(ALL, None),
            P(),
            P("shard"),
            P("shard", None),
            P(None, "shard"),
            P("shard"),
            P(),
            P(),
            P(),
            P("shard"),
            P("shard", None),
        ),
        out_specs=(
            P(ALL, None),
            P(ALL, None),
            P(ALL),
            P(ALL, None),
            P(None, ALL),
            P(ALL),
            P(),
            P(),
            P(),
            P(ALL),
            P(ALL, None),
        ),
        check_vma=False,
    )
```

time: 656 us -> 528 us (0.80)
  waiting for transfers between devices: 143 us -> 93.7 us
  Pallas kernels: 238 us -> 194 us
  blocking collectives: 26.4 us -> 0 us
  between operations: 15.6 us -> 2.74 us
  starting transfers between devices: 78.6 us -> 91.1 us
  local copies, waits for them, and re-layouts: 60.7 us -> 52 us
    ppermute x24 -> x28, waiting for transfers between devices: 93.9 us -> 46.6 us  [halve(): came = lax.ppermute(send, axis, flip(axis, bit))]
    all_to_all x1 -> x0, blocking collectives: 26.4 us -> none  [on_device(): lax.all_to_all(decays, ALL, split_axis=0, concat_axis=0, tiled=True)]
    ppermute x8, waiting for transfers between devices: 39 us -> 17.5 us  [the longest x3 15.2 us: share(): self.passed = lax.ppermute(self.direct, 'seq', flip('seq', 1))]
    all_to_all x5 -> x6, waiting for transfers between devices: 10.2 us -> 29.5 us  [the longest x1 19.2 us: on_device(): lax.all_to_all(edges, 'shard', split_axis=0, concat_axis=0, tiled=True)]
    pallas_call x1, Pallas kernels: 29 us -> 15 us  [on_device(): pl.pallas_call(state_kernel, grid=(groups + 1,), in_specs=[pl.BlockSpec((...]
    pallas_call x1, Pallas kernels: 29.1 us -> 15.2 us  [on_device(): pl.pallas_call(forward_kernel, grid=(groups,), in_specs=[pl.BlockSpec((le...]
    pallas_call x6, Pallas kernels: 103 us -> 91.3 us  [the longest x2 41 us: outside(): pl.pallas_call(lambda *refs: outside_kernel(first_group, count, final, *r...]
    pallas_call x1, Pallas kernels: 30.4 us -> 20 us  [on_device(): pl.pallas_call(inside_kernel, grid=(groups,), in_specs=[pl.BlockSpec((len...]
  transfers between devices with their start and end apart: 55 -> 58, of which waited for: 18 -> 17; matrix products, arithmetic and copies ran while one was open for 18% -> 24% of each run, Pallas kernels for 27% -> 37%
where the time goes in v3:
time: 528 us; the launch traced here: 518 us
  Pallas kernels  194 us (37%)
  waiting for transfers between devices  93.7 us (18%)
  starting transfers between devices  91.1 us (17%)
  other arithmetic  57.2 us (11%)
  local copies, waits for them, and re-layouts  52 us (10%)
  matrix products  27.4 us (5%)
    ppermute x28, waiting for transfers between devices, halve(): came = lax.ppermute(send, axis, flip(axis, bit))  46.6 us
    pallas_call x2, Pallas kernels, outside(): pl.pallas_call(lambda *refs: outside_kernel(first_group, count, final, *r...  41 us
    ppermute x28, starting transfers between devices, halve(): came = lax.ppermute(send, axis, flip(axis, bit))  39.7 us
    pallas_call x2, Pallas kernels, back(): pl.pallas_call(lambda *refs: back_kernel(len(values), *refs), grid_spec=p...  23.9 us
    dot_general x4, matrix products, mm_tn(): lax.dot_general(a, b, (((0,), (0,)), ((), ())), preferred_element_type=f32)  23.8 us
    pallas_call x2, Pallas kernels, project(): pl.pallas_call(project_kernel, grid_spec=pltpu.PrefetchScalarGridSpec(num...  21.3 us
    pallas_call x1, Pallas kernels, on_device(): pl.pallas_call(inside_kernel, grid=(groups,), in_specs=[pl.BlockSpec((len...  20 us
    pallas_call x1, Pallas kernels, on_device(): pl.pallas_call(gate_kernel, grid=(length // block,), in_specs=[tall(inner...  19.3 us
  transfers between devices with their start and end apart: 58, of which 17 were waited for; matrix products, arithmetic and copies ran while one was open for 24% of the time, Pallas kernels for 37%

profile of v3, /device:TPU:0, one launch (start us, length us, event | category | flops | bytes accessed | tf_op | source)
XLA Modules:
  0.0 518.2 jit_solution(10602491382976466053)
XLA Ops:
  0.7 3.3 dynamic-slice_bitcast_fusion.5
  4.0 2.9 collective-permute-start.1
  9.2 4.4 all-to-all-start
  13.6 3.4 collective-permute-start
  19.3 2.4 constant_dynamic-slice_fusion.11
  24.5 19.2 %all-to-all-done = bf16[4,320,384]{2,1,0:T(8,128)(2,1)} async-done(((bf16[4,320,384]{2,1,0:T(8,128)(2,1)}), bf16[4,320,384]{2,1,0:T(8,128)(2,1)}, u32[]{:S(2)}, u32[]{:S(2)}) %all-to-all-start) | async-done | bytes 983072 | tf_op jit(solution)/shard_map/all_to_all | solution.py:923
  45.1 1.8 collective-permute-start.5
  50.0 5.3 %prepare.1 = (f32[5,512,128]{2,1,0:T(8,128)}, bf16[2,512,256]{2,1,0:T(8,128)(2,1)}, f32[12,512,4]{2,1,0:T(8,128)}, f32[12,4,512]{2,1,0:T(4,128)}, f32[6,512,128]{2,1,0:T(8,128)}) custom-call(bf16[512,128]{1,0:T(8,128)(2,1)} %slice.302.edge, f32[8,128]{1,0:T(8,128)} %fusion.60.rates.refs_6_, f32[512,16]{1,0:T(8,128)} %pad.29.flags), custom_call_target="tpu_custom_call" | custom-call | tf_op jit(solution)/shard_map/prepare/pallas_call | solution.py:982
  55.3 1.8 collective-permute-start.2
  57.2 15.2 %collective-permute-done.5.refs_8_ = bf16[1536,384]{1,0:T(8,128)(2,1)} collective-permute-done((bf16[1536,384]{1,0:T(8,128)(2,1)S(1)}, bf16[1536,384]{1,0:T(8,128)(2,1)}, u32[]{:S(2)}, u32[]{:S(2)}) %collective-permute-start.5) | collective-permute-done | bytes 1179680 | tf_op jit(solution)/shard_map/ppermute | solution.py:516
  73.7 5.9 %all-to-all-start.1 = ((f32[32,1,48]{2,1,0:T(1,128)}), f32[32,1,48]{2,1,0:T(1,128)S(1)}, u32[]{:S(2)}, u32[]{:S(2)}) async-start(f32[32,1,48]{2,1,0:T(1,128)} %broadcast_in_dim.26), calls=%async_computation.1 | async-start | bytes 32768 | tf_op jit(solution)/shard_map/all_to_all | solution.py:996
  80.0 2.2 collective-permute-done.2.refs_6_.refs_4_
  82.2 1.8 collective-permute-start.7
  86.7 10.7 %project.2.raw.refs_0_ = bf16[520,3072]{1,0:T(8,128)(2,1)} custom-call(s32[8]{0:T(128)} %stack.206.table, bf16[520,1536]{1,0:T(8,128)(2,1)} %copy-done, bf16[520,1536]{1,0:T(8,128)(2,1)} %copy-done, bf16[520,1536]{1,0:T(8,128)(2,1)} %copy-done, bf16[520,1536]{1,0:T(8,128)(2,1)} %copy-done, bf16[6448,384]{1,0:T(8,128)(2,1)} %bitcast.247, ...), custom_call_target="tpu_custom_call" | custom-call | flops 4907335680 | bytes 9437184 | tf_op jit(solution)/shard_map/project/pallas_call | solution.py:559
  97.3 15.0 %mixer_state.1 = (bf16[512,3072]{1,0:T(8,128)(2,1)}, bf16[128,3072]{1,0:T(8,128)(2,1)}, bf16[512,256]{1,0:T(8,128)(2,1)}, bf16[128,512]{1,0:T(8,128)(2,1)}, bf16[128,512]{1,0:T(8,128)(2,1)}) custom-call(bf16[520,3072]{1,0:T(8,128)(2,1)} %project.2.raw.refs_0_, bf16[520,256]{1,0:T(8,128)(2,1)} %slice.303.raw_bc.refs_1_, f32[8,3328]{1,0:T(8,128)} %maximum_maximum_fusion.taps, ...), custom_call_target="tpu_custom_call" | custom-call | flops 4026531840 | bytes 15728640 | tf_op jit(solution)/shard_map/mixer_state/pallas_call | solution.py:1009
  112.9 4.4 all-to-all-start.2
  119.8 2.3 reshape_reshape.25
  126.0 10.6 %project.3.z_in = bf16[512,3072]{1,0:T(8,128)(2,1)} custom-call(s32[8]{0:T(128)} %stack.206.table, bf16[512,1536]{1,0:T(8,128)(2,1)} %slice.306.refs_0_.refs_1_.refs_2_.refs_3_, bf16[512,1536]{1,0:T(8,128)(2,1)} %slice.306.refs_0_.refs_1_.refs_2_.refs_3_, bf16[512,1536]{1,0:T(8,128)(2,1)} %slice.306.refs_0_.refs_1_.refs_2_.refs_3_, ...), custom_call_target="tpu_custom_call" | custom-call | flops 4831838208 | bytes 9437184 | tf_op jit(solution)/shard_map/project/pallas_call | solution.py:559
  136.5 2.8 all-to-all-done.2.refs_0_
  139.3 2.4 scan_forward.1
  142.3 15.2 %mixer_forward.1.y_in = f32[512,3072]{1,0:T(8,128)} custom-call(bf16[512,3072]{1,0:T(8,128)(2,1)} %get-tuple-element.137.x_in, f32[512,16]{1,0:T(8,128)} %pad.29.flags, f32[8,512]{1,0:T(8,128)} %broadcast_in_dim.31.seg_row, bf16[2,512,256]{2,1,0:T(8,128)(2,1)} %get-tuple-element.107.spreads.refs_4_, f32[12,512,4]{2,1,0:T(8,128)} %get-tuple-element.117.cum, ...), custom_call_target="tpu_custom_call" | custom-call | flops 12884901888 | bytes 15728640 | tf_op jit(solution)/shard_map/mixer_forward/pallas_call | solution.py:1058
  158.0 3.6 all-to-all-start.3
  163.2 13.0 %out_back.1.dn_in = f32[512,3072]{1,0:T(8,128)} custom-call(s32[5]{0:T(128)} %stack.201.table, bf16[512,1536]{1,0:T(8,128)(2,1)} %value, bf16[768,1536]{1,0:T(8,128)(2,1)} %own.3, bf16[768,1536]{1,0:T(8,128)(2,1)} %collective-permute-done.11.other, bf16[384,1536]{1,0:T(8,128)(2,1)} %collective-permute-done.7.direct, ...), custom_call_target="tpu_custom_call" | custom-call | flops 4831838208 | bytes 9437184 | tf_op jit(solution)/shard_map/out_back/pallas_call | solution.py:692
  176.2 7.3 %all-to-all-done.3 = bf16[32,8,1536]{2,1,0:T(8,128)(2,1)} async-done(((bf16[32,8,1536]{2,1,0:T(8,128)(2,1)}), bf16[32,8,1536]{2,1,0:T(8,128)(2,1)}, u32[]{:S(2)}, u32[]{:S(2)}) %all-to-all-start.3) | async-done | bytes 786464 | tf_op jit(solution)/shard_map/all_to_all | solution.py:475
  183.5 19.3 %mixer_gate.1 = (f32[512,3072]{1,0:T(8,128)}, bf16[512,3072]{1,0:T(8,128)(2,1)}, bf16[512,3072]{1,0:T(8,128)(2,1)}, bf16[512,3072]{1,0:T(8,128)(2,1)}, bf16[128,...) custom-call(f32[512,3072]{1,0:T(8,128)} %mixer_forward.1.y_in, ...), custom_call_target="tpu_custom_call" | custom-call | flops 1610612736 | bytes 34603008 | tf_op jit(solution)/shard_map/mixer_gate/pallas_call | solution.py:1092
  202.8 3.3 broadcast_select_fusion.3
  208.7 2.1 maximum_convert_fusion
  214.5 3.0 all-to-all-start.4
  217.5 13.4 %out_forward.1 = bf16[512,1536]{1,0:T(8,128)(2,1)} custom-call(s32[5]{0:T(128)} %stack.201.table, bf16[512,3072]{1,0:T(8,128)(2,1)} %get-tuple-element.129.value, bf16[512,1536]{1,0:T(8,128)(2,1)} %base.1, bf16[768,1536]{1,0:T(8,128)(2,1)} %own.3, bf16[768,1536]{1,0:T(8,128)(2,1)} %collective-permute-done.11.other, ...), custom_call_target="tpu_custom_call" | custom-call | flops 4831838208 | bytes 9437184 | tf_op jit(solution)/shard_map/out_forward/pallas_call | solution.py:741
  230.9 1.7 pad_maximum_fusion.2
  232.8 8.2 %convolution_convert_fusion = bf16[1536,1536]{1,0:T(8,128)(2,1)} fusion(bf16[1024,1536]{1,0:T(8,128)(2,1)S(1)} %pad_maximum_fusion.2, bf16[512,1536]{1,0:T(8,128)(2,1)} %collective-permute-done.16, bf16[512,1536]{1,0:T(8,128)(2,1)S(1)} %copy-done.34), kind=kOutput, calls=%fused_computation | convolution fusion | flops 4840488960 | bytes 11010048 | tf_op jit(solution)/shard_map/dot_general | solution.py:31
  241.9 2.4 scan_backward.1
  244.3 5.8 %all-to-all-start.5 = ((bf16[32,8,1536]{2,1,0:T(8,128)(2,1)}), bf16[32,8,1536]{2,1,0:T(8,128)(2,1)S(1)}, u32[]{:S(2)}, u32[]{:S(2)}) async-start(bf16[32,8,1536]{2,1,0:T(8,128)(2,1)} %scan_backward.1), calls=%async_computation.5 | async-start | bytes 1572864 | tf_op jit(solution)/shard_map/all_to_all | solution.py:475
  250.2 3.4 pad_maximum_fusion
  253.7 6.6 %convolution_convert_fusion.1 = bf16[768,3072]{1,0:T(8,128)(2,1)S(1)} fusion(bf16[1024,3072]{1,0:T(8,128)(2,1)S(1)} %pad_maximum_fusion, bf16[512,768]{1,0:T(8,128)(2,1)} %collective-permute-done.17, bf16[512,384]{1,0:T(8,128)(2,1)S(1)} %copy-done.44, bf16[512,384]{1,0:T(8,128)(2,1)S(1)} %copy-done.41), kind=kOutput, calls=%fused_computation.2 | convolution fusion | flops 4838916096 | bytes 12582912 | tf_op jit(solution)/shard_map/dot_general | solution.py:31
  262.4 1.9 collective-permute-start.19
  269.1 20.0 %mixer_inside.1 = (f32[512,3072]{1,0:T(8,128)}, f32[512,128]{1,0:T(8,128)}, f32[512,128]{1,0:T(8,128)}) custom-call(bf16[512,3072]{1,0:T(8,128)(2,1)} %get-tuple-element.137.x_in, f32[512,16]{1,0:T(8,128)} %pad.29.flags, f32[8,512]{1,0:T(8,128)} %broadcast_in_dim.31.seg_row, bf16[2,512,256]{2,1,0:T(8,128)(2,1)} %get-tuple-element.107.spreads.refs_4_, ...), custom_call_target="tpu_custom_call" | custom-call | flops 6442450944 | bytes 15728640 | tf_op jit(solution)/shard_map/mixer_inside/pallas_call | solution.py:1166
  290.7 2.2 collective-permute-done.19
  299.4 19.2 %mixer_outside.2 = (bf16[512,1536]{1,0:T(8,128)(2,1)}, f32[8,1536]{1,0:T(8,128)}, f32[8,1536]{1,0:T(8,128)}, f32[8,1536]{1,0:T(8,128)}, f32[8,128]{1,0:T(8,128)}...) custom-call(bf16[520,3072]{1,0:T(8,128)(2,1)} %project.2.raw.refs_0_, ...), custom_call_target="tpu_custom_call" | custom-call | flops 805306368 | bytes 12582912 | tf_op jit(solution)/shard_map/mixer_outside/pallas_call | solution.py:1216
  320.0 2.5 collective-permute-start.23
  325.0 1.8 collective-permute-start.21
  328.3 7.7 %collective-permute-done.23 = bf16[1,4,96,768]{3,2,1,0:T(8,128)(2,1)S(1)} collective-permute-done((bf16[1,4,96,768]{3,2,1,0:T(8,128)(2,1)S(1)}, bf16[1,4,96,768]{3,2,1,0:T(8,128)(2,1)S(1)}, u32[]{:S(2)}, u32[]{:S(2)}) %collective-permute-start.23) | collective-permute-done | bytes 589856 | tf_op jit(solution)/shard_map/ppermute | solution.py:833
  345.8 11.2 %back.2 = f32[512,1536]{1,0:T(8,128)} custom-call(s32[16]{0:T(128)} %stack.241.refs_0_, bf16[512,3072]{1,0:T(8,128)(2,1)} %get-tuple-element.150.refs_1_, bf16[6448,384]{1,0:T(8,128)(2,1)} %bitcast.249, bf16[6448,384]{1,0:T(8,128)(2,1)} %collective-permute-done.3.refs_5_.refs_3_, bf16[1536,384]{1,0:T(8,128)(2,1)} %collective-permute-done.2.refs_6_.refs_4_, ...), custom_call_target="tpu_custom_call" | custom-call | flops 4831838208 | bytes 9437184 | tf_op jit(solution)/shard_map/back/pallas_call | solution.py:639
  358.7 4.1 convolution_convert_fusion.2
  362.8 21.8 %mixer_outside.3 = (bf16[512,2048]{1,0:T(8,128)(2,1)}, f32[8,2048]{1,0:T(8,128)}, f32[8,2048]{1,0:T(8,128)}, f32[8,2048]{1,0:T(8,128)}, f32[8,128]{1,0:T(8,128)}...) custom-call(bf16[520,3072]{1,0:T(8,128)(2,1)} %project.2.raw.refs_0_, ...), custom_call_target="tpu_custom_call" | custom-call | flops 1073741824 | bytes 16777216 | tf_op jit(solution)/shard_map/mixer_outside/pallas_call | solution.py:1216
  390.0 4.9 collective-permute-start.50
  396.6 17.8 %collective-permute-done.29 = bf16[1,8,48,1536]{3,2,1,0:T(8,128)(2,1)S(1)} collective-permute-done((bf16[1,8,48,1536]{3,2,1,0:T(8,128)(2,1)S(1)}, bf16[1,8,48,1536]{3,2,1,0:T(8,128)(2,1)S(1)}, u32[]{:S(2)}, u32[]{:S(2)}) %collective-permute-start.29) | collective-permute-done | bytes 1179680 | tf_op jit(solution)/shard_map/ppermute | solution.py:833
  420.2 2.6 convolution_add_fusion.refs_3_
  424.8 4.8 convolution_convert_fusion.3
  432.7 1.7 collective-permute-start.32
  434.5 4.6 collective-permute-done.30
  444.9 12.8 %back.3 = f32[512,1536]{1,0:T(8,128)} custom-call(s32[16]{0:T(128)} %stack.241.refs_0_, bf16[512,1536]{1,0:T(8,128)(2,1)} %copy-done.17, bf16[512,2048]{1,0:T(8,128)(2,1)} %copy-done.7, f32[512,1536]{1,0:T(8,128)} %convolution_add_fusion.refs_3_, bf16[6448,384]{1,0:T(8,128)(2,1)} %bitcast.250, bf16[6448,384]{1,0:T(8,128)(2,1)} %collective-permute-done.3.refs_5_.refs_3_, ...), custom_call_target="tpu_custom_call" | custom-call | flops 4831838208 | bytes 9437184 | tf_op jit(solution)/shard_map/back/pallas_call | solution.py:639
  463.6 2.6 fusion.9
  468.9 2.0 pack.1
  471.0 4.2 all-to-all-start.6
  475.1 1.8 collective-permute-start.44
  476.9 1.8 dynamic-slice_bitcast_fusion.12
  483.3 4.8 multiply_subtract_fusion
  498.4 4.6 collective-permute-done.45
  503.0 2.5 collective-permute-start.46
  506.9 2.5 collective-permute-start.43
  509.4 1.9 collective-permute-done.46
  511.3 3.0 collective-permute-done.43
  515.6 2.2 concatenate.89
  (378 shorter events, 114.0 us)
Async XLA Ops:
  4.0 41.1 %collective-permute-start.1 = (bf16[1536,384]{1,0:T(8,128)(2,1)}, bf16[1536,384]{1,0:T(8,128)(2,1)S(1)}, u32[]{:S(2)}, u32[]{:S(2)}) collective-permute-start(bf16[1536,384]{1,0:T(8,128)(2,1)} %get-tuple-element.199), channel_id=1, source_target_pairs={{0,16},{8,24},{16,0},{24,8},{1,17},{9,25},{17,1},{25,9},{2,18},{10... | collective-permute-start | bytes 3538952 | tf_op jit(solution)/shard_map/ppermute | solution.py:511
  6.9 79.7 %collective-permute-start.3 = (bf16[6448,384]{1,0:T(8,128)(2,1)}, bf16[6448,384]{1,0:T(8,128)(2,1)}, u32[]{:S(2)}, u32[]{:S(2)}) collective-permute-start(bf16[6448,384]{1,0:T(8,128)(2,1)} %bitcast.245), channel_id=1, source_target_pairs={{0,8},{8,0},{16,24},{24,16},{1,9},{9,1},{17,25},{25,17},{2,10},{10... | collective-permute-start | bytes 14856200 | tf_op jit(solution)/shard_map/ppermute | solution.py:500
  9.2 34.5 %all-to-all-start = ((bf16[4,320,384]{2,1,0:T(8,128)(2,1)}), bf16[4,320,384]{2,1,0:T(8,128)(2,1)}, u32[]{:S(2)}, u32[]{:S(2)}) async-start(bf16[4,320,384]{2,1,0:T(8,128)(2,1)} %broadcast_in_dim.24), calls=%async_computation | async-start | bytes 1966080 | tf_op jit(solution)/shard_map/all_to_all | solution.py:923
  13.6 10.5 %collective-permute-start = (bf16[8,1536]{1,0:T(8,128)(2,1)S(1)}, bf16[8,1536]{1,0:T(8,128)(2,1)S(1)}, u32[]{:S(2)}, u32[]{:S(2)}) collective-permute-start(bf16[8,1536]{1,0:T(8,128)(2,1)S(1)} %slice.230), channel_id=1, source_target_pairs={{0,1},{1,2},{2,3},{3,4},{4,5},{5,6},{6,7},{7,8},{8,9},{9,10},{10,1... | collective-permute-start | bytes 73736 | tf_op jit(solution)/shard_map/ppermute | solution.py:970
  44.6 421.6 %copy-start.47 = (f32[1536]{0:T(1024)}, f32[1536]{0:T(1024)S(1)}, u32[]{:S(2)}) copy-start(f32[1536]{0:T(1024)S(1)} %reshape.505) | copy-start | bytes 18436
  45.1 27.3 %collective-permute-start.5 = (bf16[1536,384]{1,0:T(8,128)(2,1)S(1)}, bf16[1536,384]{1,0:T(8,128)(2,1)}, u32[]{:S(2)}, u32[]{:S(2)}) collective-permute-start(bf16[1536,384]{1,0:T(8,128)(2,1)S(1)} %collective-permute-done.1.refs_6_), channel_id=1, source_target_pairs={{0,1},{1,0},{2,3},{3,2},{4,5},{5,4},{6,7},{7,6},{8,9},{9,8},{10,11... | collective-permute-start | bytes 3538952 | tf_op jit(solution)/shard_map/ppermute | solution.py:516
  55.3 26.9 %collective-permute-start.2 = (bf16[1536,384]{1,0:T(8,128)(2,1)}, bf16[1536,384]{1,0:T(8,128)(2,1)}, u32[]{:S(2)}, u32[]{:S(2)}) collective-permute-start(bf16[1536,384]{1,0:T(8,128)(2,1)} %get-tuple-element.103), channel_id=1, source_target_pairs={{0,16},{8,24},{16,0},{24,8},{1,17},{9,25},{17,1},{25,9},{2,18},{10... | collective-permute-start | bytes 3538952 | tf_op jit(solution)/shard_map/ppermute | solution.py:511
  57.1 29.6 %collective-permute-start.4 = (bf16[1536,384]{1,0:T(8,128)(2,1)S(1)}, bf16[1536,384]{1,0:T(8,128)(2,1)}, u32[]{:S(2)}, u32[]{:S(2)}) collective-permute-start(bf16[1536,384]{1,0:T(8,128)(2,1)S(1)} %collective-permute-done.1.refs_6_), channel_id=1, source_target_pairs={{0,8},{8,0},{16,24},{24,16},{1,9},{9,1},{17,25},{25,17},{2,10},{10... | collective-permute-start | bytes 3538952 | tf_op jit(solution)/shard_map/ppermute | solution.py:500
  72.4 14.3 %collective-permute-start.6 = (bf16[1536,384]{1,0:T(8,128)(2,1)}, bf16[1536,384]{1,0:T(8,128)(2,1)}, u32[]{:S(2)}, u32[]{:S(2)}) collective-permute-start(bf16[1536,384]{1,0:T(8,128)(2,1)} %collective-permute-done.5.refs_8_), channel_id=1, source_target_pairs={{0,8},{8,0},{16,24},{24,16},{1,9},{9,1},{17,25},{25,17},{2,10},{10... | collective-permute-start | bytes 3538952 | tf_op jit(solution)/shard_map/ppermute | solution.py:500
  73.7 12.9 %all-to-all-start.1 = ((f32[32,1,48]{2,1,0:T(1,128)}), f32[32,1,48]{2,1,0:T(1,128)S(1)}, u32[]{:S(2)}, u32[]{:S(2)}) async-start(f32[32,1,48]{2,1,0:T(1,128)} %broadcast_in_dim.26), calls=%async_computation.1 | async-start | bytes 32768 | tf_op jit(solution)/shard_map/all_to_all | solution.py:996
  82.2 30.2 %collective-permute-start.7 = (bf16[384,1536]{1,0:T(8,128)(2,1)}, bf16[384,1536]{1,0:T(8,128)(2,1)}, u32[]{:S(2)}, u32[]{:S(2)}) collective-permute-start(bf16[384,1536]{1,0:T(8,128)(2,1)} %constant_dynamic-slice_fusion.11), channel_id=1, source_target_pairs={{0,16},{8,24},{16,0},{24,8},{1,17},{9,25},{17,1},{25,9},{2,18},{10... | collective-permute-start | bytes 3538952 | tf_op jit(solution)/shard_map/ppermute | solution.py:511
  84.0 28.4 %collective-permute-start.8 = (bf16[1536,384]{1,0:T(8,128)(2,1)}, bf16[1536,384]{1,0:T(8,128)(2,1)}, u32[]{:S(2)}, u32[]{:S(2)}) collective-permute-start(bf16[1536,384]{1,0:T(8,128)(2,1)} %collective-permute-done.2.refs_6_.refs_4_), channel_id=1, source_target_pairs={{0,1},{1,0},{2,3},{3,2},{4,5},{5,4},{6,7},{7,6},{8,9},{9,8},{10,11... | collective-permute-start | bytes 3538952 | tf_op jit(solution)/shard_map/ppermute | solution.py:516
  112.4 13.6 %collective-permute-start.10 = (bf16[1536,384]{1,0:T(8,128)(2,1)}, bf16[1536,384]{1,0:T(8,128)(2,1)}, u32[]{:S(2)}, u32[]{:S(2)}) collective-permute-start(bf16[1536,384]{1,0:T(8,128)(2,1)} %collective-permute-done.8.refs_8_.refs_6_), channel_id=1, source_target_pairs={{0,8},{8,0},{16,24},{24,16},{1,9},{9,1},{17,25},{25,17},{2,10},{10... | collective-permute-start | bytes 3538952 | tf_op jit(solution)/shard_map/ppermute | solution.py:500
  112.4 13.5 %collective-permute-start.9 = (bf16[1536,384]{1,0:T(8,128)(2,1)}, bf16[1536,384]{1,0:T(8,128)(2,1)}, u32[]{:S(2)}, u32[]{:S(2)}) collective-permute-start(bf16[1536,384]{1,0:T(8,128)(2,1)} %collective-permute-done.2.refs_6_.refs_4_), channel_id=1, source_target_pairs={{0,8},{8,0},{16,24},{24,16},{1,9},{9,1},{17,25},{25,17},{2,10},{10... | collective-permute-start | bytes 3538952 | tf_op jit(solution)/shard_map/ppermute | solution.py:500
  112.9 26.4 %all-to-all-start.2 = ((bf16[32,8,1536]{2,1,0:T(8,128)(2,1)}), bf16[32,8,1536]{2,1,0:T(8,128)(2,1)}, u32[]{:S(2)}, u32[]{:S(2)}) async-start(bf16[32,8,1536]{2,1,0:T(8,128)(2,1)} %bitcast.295), calls=%async_computation.2 | async-start | bytes 1572864 | tf_op jit(solution)/shard_map/all_to_all | solution.py:475
  123.9 39.3 %collective-permute-start.11 = (bf16[768,1536]{1,0:T(8,128)(2,1)}, bf16[768,1536]{1,0:T(8,128)(2,1)}, u32[]{:S(2)}, u32[]{:S(2)}) collective-permute-start(bf16[768,1536]{1,0:T(8,128)(2,1)} %own.3), channel_id=1, source_target_pairs={{0,8},{8,0},{16,24},{24,16},{1,9},{9,1},{17,25},{25,17},{2,10},{10... | collective-permute-start | bytes 7077896 | tf_op jit(solution)/shard_map/ppermute | solution.py:500
  124.3 33.2 %collective-permute-start.12 = (bf16[384,1536]{1,0:T(8,128)(2,1)}, bf16[384,1536]{1,0:T(8,128)(2,1)}, u32[]{:S(2)}, u32[]{:S(2)}) collective-permute-start(bf16[384,1536]{1,0:T(8,128)(2,1)} %collective-permute-done.7.direct), channel_id=1, source_target_pairs={{0,1},{1,0},{2,3},{3,2},{4,5},{5,4},{6,7},{7,6},{8,9},{9,8},{10,11... | collective-permute-start | bytes 3538952 | tf_op jit(solution)/shard_map/ppermute | solution.py:516
  157.5 5.8 %collective-permute-start.13 = (bf16[384,1536]{1,0:T(8,128)(2,1)}, bf16[384,1536]{1,0:T(8,128)(2,1)}, u32[]{:S(2)}, u32[]{:S(2)}) collective-permute-start(bf16[384,1536]{1,0:T(8,128)(2,1)} %collective-permute-done.7.direct), channel_id=1, source_target_pairs={{0,8},{8,0},{16,24},{24,16},{1,9},{9,1},{17,25},{25,17},{2,10},{10... | collective-permute-start | bytes 3538952 | tf_op jit(solution)/shard_map/ppermute | solution.py:500
  157.5 5.7 %collective-permute-start.14 = (bf16[384,1536]{1,0:T(8,128)(2,1)}, bf16[384,1536]{1,0:T(8,128)(2,1)}, u32[]{:S(2)}, u32[]{:S(2)}) collective-permute-start(bf16[384,1536]{1,0:T(8,128)(2,1)} %collective-permute-done.12.passed), channel_id=1, source_target_pairs={{0,8},{8,0},{16,24},{24,16},{1,9},{9,1},{17,25},{25,17},{2,10},{10... | collective-permute-start | bytes 3538952 | tf_op jit(solution)/shard_map/ppermute | solution.py:500
  158.0 25.5 %all-to-all-start.3 = ((bf16[32,8,1536]{2,1,0:T(8,128)(2,1)}), bf16[32,8,1536]{2,1,0:T(8,128)(2,1)}, u32[]{:S(2)}, u32[]{:S(2)}) async-start(bf16[32,8,1536]{2,1,0:T(8,128)(2,1)} %scan_forward.1), calls=%async_computation.3 | async-start | bytes 1572864 | tf_op jit(solution)/shard_map/all_to_all | solution.py:475
  161.6 71.1 %collective-permute-start.16 = (bf16[512,1536]{1,0:T(8,128)(2,1)}, bf16[512,1536]{1,0:T(8,128)(2,1)}, u32[]{:S(2)}, u32[]{:S(2)}) collective-permute-start(bf16[512,1536]{1,0:T(8,128)(2,1)} %value), channel_id=1, source_target_pairs={{0,8},{8,0},{16,24},{24,16},{1,9},{9,1},{17,25},{25,17},{2,10},{10... | collective-permute-start | bytes 4718600 | tf_op jit(solution)/shard_map/ppermute | solution.py:500
  207.4 23.5 %collective-permute-start.15 = (bf16[512,1536]{1,0:T(8,128)(2,1)}, bf16[512,1536]{1,0:T(8,128)(2,1)}, u32[]{:S(2)}, u32[]{:S(2)}) collective-permute-start(bf16[512,1536]{1,0:T(8,128)(2,1)} %pad_maximum_fusion.4), channel_id=1, source_target_pairs={{0,8},{8,0},{16,24},{24,16},{1,9},{9,1},{17,25},{25,17},{2,10},{10... | collective-permute-start | bytes 4718600 | tf_op jit(solution)/shard_map/ppermute | solution.py:500
  210.9 255.3 %copy-start.53 = (f32[512]{0:T(512)}, f32[512]{0:T(512)S(1)}, u32[]{:S(2)}) copy-start(f32[512]{0:T(512)S(1)} %slice.251) | copy-start | bytes 6148
  211.5 38.7 %collective-permute-start.18 = (bf16[512,3072]{1,0:T(8,128)(2,1)}, bf16[512,3072]{1,0:T(8,128)(2,1)}, u32[]{:S(2)}, u32[]{:S(2)}) collective-permute-start(bf16[512,3072]{1,0:T(8,128)(2,1)} %get-tuple-element.150.refs_1_), channel_id=1, source_target_pairs={{0,8},{8,0},{16,24},{24,16},{1,9},{9,1},{17,25},{25,17},{2,10},{10... | collective-permute-start | bytes 9437192 | tf_op jit(solution)/shard_map/ppermute | solution.py:500
  213.1 40.5 %collective-permute-start.17 = (bf16[512,768]{1,0:T(8,128)(2,1)S(1)}, bf16[512,768]{1,0:T(8,128)(2,1)}, u32[]{:S(2)}, u32[]{:S(2)}) collective-permute-start(bf16[512,768]{1,0:T(8,128)(2,1)S(1)} %pad_maximum_fusion.6), channel_id=1, source_target_pairs={{0,8},{8,0},{16,24},{24,16},{1,9},{9,1},{17,25},{25,17},{2,10},{10... | collective-permute-start | bytes 2359304 | tf_op jit(solution)/shard_map/ppermute | solution.py:500
  214.5 26.6 %all-to-all-start.4 = ((bf16[32,8,1536]{2,1,0:T(8,128)(2,1)}), bf16[32,8,1536]{2,1,0:T(8,128)(2,1)S(1)}, u32[]{:S(2)}, u32[]{:S(2)}) async-start(bf16[32,8,1536]{2,1,0:T(8,128)(2,1)} %bitcast.37), calls=%async_computation.4 | async-start | bytes 1572864 | tf_op jit(solution)/shard_map/all_to_all | solution.py:475
  244.3 44.8 %all-to-all-start.5 = ((bf16[32,8,1536]{2,1,0:T(8,128)(2,1)}), bf16[32,8,1536]{2,1,0:T(8,128)(2,1)S(1)}, u32[]{:S(2)}, u32[]{:S(2)}) async-start(bf16[32,8,1536]{2,1,0:T(8,128)(2,1)} %scan_backward.1), calls=%async_computation.5 | async-start | bytes 1572864 | tf_op jit(solution)/shard_map/all_to_all | solution.py:475
  262.4 30.5 %collective-permute-start.19 = (bf16[1,8,96,768]{3,2,1,0:T(8,128)(2,1)}, bf16[1,8,96,768]{3,2,1,0:T(8,128)(2,1)}, u32[]{:S(2)}, u32[]{:S(2)}) collective-permute-start(bf16[1,8,96,768]{3,2,1,0:T(8,128)(2,1)} %dynamic-slice_bitcast_fusion.4), channel_id=1, source_target_pairs={{0,16},{8,24},{16,0},{24,8},{1,17},{9,25},{17,1},{25,9},{2,18},{10... | collective-permute-start | bytes 3538952 | tf_op jit(solution)/shard_map/ppermute | solution.py:833
  266.0 29.7 %collective-permute-start.20 = (bf16[2,4,96,768]{3,2,1,0:T(8,128)(2,1)}, bf16[2,4,96,768]{3,2,1,0:T(8,128)(2,1)}, u32[]{:S(2)}, u32[]{:S(2)}) collective-permute-start(bf16[2,4,96,768]{3,2,1,0:T(8,128)(2,1)} %dynamic-slice_bitcast_fusion.3), channel_id=1, source_target_pairs={{0,1},{1,0},{2,3},{3,2},{4,5},{5,4},{6,7},{7,6},{8,9},{9,8},{10,11... | collective-permute-start | bytes 3538952 | tf_op jit(solution)/shard_map/ppermute | solution.py:833
  268.6 51.3 %collective-permute-start.26 = (bf16[2,4,48,1536]{3,2,1,0:T(8,128)(2,1)}, bf16[2,4,48,1536]{3,2,1,0:T(8,128)(2,1)}, u32[]{:S(2)}, u32[]{:S(2)}) collective-permute-start(bf16[2,4,48,1536]{3,2,1,0:T(8,128)(2,1)} %dynamic-slice_bitcast_fusion.1), channel_id=1, source_target_pairs={{0,1},{1,0},{2,3},{3,2},{4,5},{5,4},{6,7},{7,6},{8,9},{9,8},{10,11... | collective-permute-start | bytes 3538952 | tf_op jit(solution)/shard_map/ppermute | solution.py:833
  290.3 34.7 %collective-permute-start.25 = (bf16[1,8,48,1536]{3,2,1,0:T(8,128)(2,1)}, bf16[1,8,48,1536]{3,2,1,0:T(8,128)(2,1)}, u32[]{:S(2)}, u32[]{:S(2)}) collective-permute-start(bf16[1,8,48,1536]{3,2,1,0:T(8,128)(2,1)} %dynamic-slice_bitcast_fusion.2), channel_id=1, source_target_pairs={{0,16},{8,24},{16,0},{24,8},{1,17},{9,25},{17,1},{25,9},{2,18},{10... | collective-permute-start | bytes 3538952 | tf_op jit(solution)/shard_map/ppermute | solution.py:833
  320.0 16.1 %collective-permute-start.23 = (bf16[1,4,96,768]{3,2,1,0:T(8,128)(2,1)S(1)}, bf16[1,4,96,768]{3,2,1,0:T(8,128)(2,1)S(1)}, u32[]{:S(2)}, u32[]{:S(2)}) collective-permute-start(bf16[1,4,96,768]{3,2,1,0:T(8,128)(2,1)S(1)} %dynamic-slice_bitcast_fusion.11), channel_id=1, source_target_pairs={{0,1},{1,0},{2,3},{3,2},{4,5},{5,4},{6,7},{7,6},{8,9},{9,8},{10,11... | collective-permute-start | bytes 1769480 | tf_op jit(solution)/shard_map/ppermute | solution.py:833
  322.5 14.6 %collective-permute-start.24 = (bf16[1,4,96,768]{3,2,1,0:T(8,128)(2,1)S(1)}, bf16[1,4,96,768]{3,2,1,0:T(8,128)(2,1)S(1)}, u32[]{:S(2)}, u32[]{:S(2)}) collective-permute-start(bf16[1,4,96,768]{3,2,1,0:T(8,128)(2,1)S(1)} %constant_dynamic-slice_fusion.9), channel_id=1, source_target_pairs={{0,16},{8,24},{16,0},{24,8},{1,17},{9,25},{17,1},{25,9},{2,18},{10... | collective-permute-start | bytes 1769480 | tf_op jit(solution)/shard_map/ppermute | solution.py:833
  325.0 12.1 %collective-permute-start.21 = (f32[8,1536]{1,0:T(8,128)S(1)}, f32[8,1536]{1,0:T(8,128)S(1)}, u32[]{:S(2)}, u32[]{:S(2)}) collective-permute-start(f32[8,1536]{1,0:T(8,128)S(1)} %copy-done.72), channel_id=1, source_target_pairs={{1,0},{2,1},{3,2},{4,3},{5,4},{6,5},{7,6},{8,7},{9,8},{10,9},{11,1... | collective-permute-start | bytes 147464 | tf_op jit(solution)/shard_map/ppermute | solution.py:1277
  337.3 19.7 %collective-permute-start.22 = (bf16[512,1536]{1,0:T(8,128)(2,1)S(1)}, bf16[512,1536]{1,0:T(8,128)(2,1)}, u32[]{:S(2)}, u32[]{:S(2)}) collective-permute-start(bf16[512,1536]{1,0:T(8,128)(2,1)S(1)} %fusion.52.refs_1_), channel_id=1, source_target_pairs={{0,8},{8,0},{16,24},{24,16},{1,9},{9,1},{17,25},{25,17},{2,10},{10... | collective-permute-start | bytes 4718600 | tf_op jit(solution)/shard_map/ppermute | solution.py:500
  338.3 50.0 %collective-permute-start.34 = (bf16[1,4,48,1536]{3,2,1,0:T(8,128)(2,1)}, bf16[1,4,48,1536]{3,2,1,0:T(8,128)(2,1)}, u32[]{:S(2)}, u32[]{:S(2)}) collective-permute-start(bf16[1,4,48,1536]{3,2,1,0:T(8,128)(2,1)} %dynamic-slice_bitcast_fusion.9), channel_id=1, source_target_pairs={{0,1},{1,0},{2,3},{3,2},{4,5},{5,4},{6,7},{7,6},{8,9},{9,8},{10,11... | collective-permute-start | bytes 1769480 | tf_op jit(solution)/shard_map/ppermute | solution.py:833
  340.4 47.9 %collective-permute-start.37 = (bf16[1,4,48,1536]{3,2,1,0:T(8,128)(2,1)}, bf16[1,4,48,1536]{3,2,1,0:T(8,128)(2,1)}, u32[]{:S(2)}, u32[]{:S(2)}) collective-permute-start(bf16[1,4,48,1536]{3,2,1,0:T(8,128)(2,1)} %constant_dynamic-slice_fusion.7), channel_id=1, source_target_pairs={{0,16},{8,24},{16,0},{24,8},{1,17},{9,25},{17,1},{25,9},{2,18},{10... | collective-permute-start | bytes 1769480 | tf_op jit(solution)/shard_map/ppermute | solution.py:833
  342.0 42.6 %collective-permute-start.47 = (bf16[1,2,96,768]{3,2,1,0:T(8,128)(2,1)}, bf16[1,2,96,768]{3,2,1,0:T(8,128)(2,1)}, u32[]{:S(2)}, u32[]{:S(2)}) collective-permute-start(bf16[1,2,96,768]{3,2,1,0:T(8,128)(2,1)} %dynamic-slice_bitcast_fusion.14), channel_id=1, source_target_pairs={{0,2},{1,3},{2,0},{3,1},{4,6},{5,7},{6,4},{7,5},{8,10},{9,11},{10,... | collective-permute-start | bytes 884744 | tf_op jit(solution)/shard_map/ppermute | solution.py:833
  344.6 45.3 %collective-permute-start.49 = (bf16[1,2,96,768]{3,2,1,0:T(8,128)(2,1)}, bf16[1,2,96,768]{3,2,1,0:T(8,128)(2,1)S(1)}, u32[]{:S(2)}, u32[]{:S(2)}) collective-permute-start(bf16[1,2,96,768]{3,2,1,0:T(8,128)(2,1)} %dynamic-slice_bitcast_fusion.13), channel_id=1, source_target_pairs={{0,2},{1,3},{2,0},{3,1},{4,6},{5,7},{6,4},{7,5},{8,10},{9,11},{10,... | collective-permute-start | bytes 884744 | tf_op jit(solution)/shard_map/ppermute | solution.py:833
  385.9 43.8 %collective-permute-start.48 = (bf16[1,1,96,768]{3,2,1,0:T(8,128)(2,1)S(1)}, bf16[1,1,96,768]{3,2,1,0:T(8,128)(2,1)S(1)}, u32[]{:S(2)}, u32[]{:S(2)}) collective-permute-start(bf16[1,1,96,768]{3,2,1,0:T(8,128)(2,1)S(1)} %constant_dynamic-slice_fusion.1), channel_id=1, source_target_pairs={{0,4},{1,5},{2,6},{3,7},{4,0},{5,1},{6,2},{7,3},{8,12},{9,13},{10,... | collective-permute-start | bytes 442376 | tf_op jit(solution)/shard_map/ppermute | solution.py:833
  387.4 27.0 %copy-start.6 = (bf16[512,2048]{1,0:T(8,128)(2,1)S(1)}, bf16[512,2048]{1,0:T(8,128)(2,1)}, u32[]{:S(2)}) copy-start(bf16[512,2048]{1,0:T(8,128)(2,1)} %get-tuple-element.160) | copy-start | bytes 6291460
  387.5 27.0 %copy-start.50 = (f32[8,2048]{1,0:T(8,128)S(1)}, f32[8,2048]{1,0:T(8,128)}, u32[]{:S(2)}) copy-start(f32[8,2048]{1,0:T(8,128)} %get-tuple-element.161) | copy-start | bytes 196612
  387.5 26.9 %collective-permute-start.29 = (bf16[1,8,48,1536]{3,2,1,0:T(8,128)(2,1)S(1)}, bf16[1,8,48,1536]{3,2,1,0:T(8,128)(2,1)S(1)}, u32[]{:S(2)}, u32[]{:S(2)}) collective-permute-start(bf16[1,8,48,1536]{3,2,1,0:T(8,128)(2,1)S(1)} %dynamic-slice_bitcast_fusion), channel_id=1, source_target_pairs={{0,16},{8,24},{16,0},{24,8},{1,17},{9,25},{17,1},{25,9},{2,18},{10... | collective-permute-start | bytes 3538952 | tf_op jit(solution)/shard_map/ppermute | solution.py:833
  388.3 8.3 %collective-permute-start.27 = (f32[8,2048]{1,0:T(8,128)S(1)}, f32[8,2048]{1,0:T(8,128)S(1)}, u32[]{:S(2)}, u32[]{:S(2)}) collective-permute-start(f32[8,2048]{1,0:T(8,128)S(1)} %copy-done.71), channel_id=1, source_target_pairs={{1,0},{2,1},{3,2},{4,3},{5,4},{6,5},{7,6},{8,7},{9,8},{10,9},{11,1... | collective-permute-start | bytes 196616 | tf_op jit(solution)/shard_map/ppermute | solution.py:1277
  390.0 27.4 %copy-start.48 = (f32[8,2048]{1,0:T(8,128)S(1)}, f32[8,2048]{1,0:T(8,128)}, u32[]{:S(2)}) copy-start(f32[8,2048]{1,0:T(8,128)} %get-tuple-element.173) | copy-start | bytes 196612
  390.0 27.4 %copy-start.51 = (f32[8,1536]{1,0:T(8,128)S(1)}, f32[8,1536]{1,0:T(8,128)}, u32[]{:S(2)}) copy-start(f32[8,1536]{1,0:T(8,128)} %get-tuple-element.172) | copy-start | bytes 147460
  390.0 39.6 %collective-permute-start.50 = (bf16[1,1,96,768]{3,2,1,0:T(8,128)(2,1)S(1)}, bf16[1,1,96,768]{3,2,1,0:T(8,128)(2,1)}, u32[]{:S(2)}, u32[]{:S(2)}) collective-permute-start(bf16[1,1,96,768]{3,2,1,0:T(8,128)(2,1)S(1)} %constant_dynamic-slice_fusion), channel_id=1, source_target_pairs={{0,4},{1,5},{2,6},{3,7},{4,0},{5,1},{6,2},{7,3},{8,12},{9,13},{10,... | collective-permute-start | bytes 442376 | tf_op jit(solution)/shard_map/ppermute | solution.py:833
  396.2 44.2 %collective-permute-start.38 = (bf16[1,2,48,1536]{3,2,1,0:T(8,128)(2,1)S(1)}, bf16[1,2,48,1536]{3,2,1,0:T(8,128)(2,1)S(1)}, u32[]{:S(2)}, u32[]{:S(2)}) collective-permute-start(bf16[1,2,48,1536]{3,2,1,0:T(8,128)(2,1)S(1)} %dynamic-slice_bitcast_fusion.15), channel_id=1, source_target_pairs={{0,2},{1,3},{2,0},{3,1},{4,6},{5,7},{6,4},{7,5},{8,10},{9,11},{10,... | collective-permute-start | bytes 884744 | tf_op jit(solution)/shard_map/ppermute | solution.py:833
  414.6 8.3 %collective-permute-start.28 = (bf16[512,2048]{1,0:T(8,128)(2,1)S(1)}, bf16[512,2048]{1,0:T(8,128)(2,1)S(1)}, u32[]{:S(2)}, u32[]{:S(2)}) collective-permute-start(bf16[512,2048]{1,0:T(8,128)(2,1)S(1)} %fusion.51.refs_2_), channel_id=1, source_target_pairs={{0,8},{8,0},{16,24},{24,16},{1,9},{9,1},{17,25},{25,17},{2,10},{10... | collective-permute-start | bytes 6291464 | tf_op jit(solution)/shard_map/ppermute | solution.py:500
  416.3 26.3 %collective-permute-start.35 = (bf16[1,2,48,1536]{3,2,1,0:T(8,128)(2,1)S(1)}, bf16[1,2,48,1536]{3,2,1,0:T(8,128)(2,1)S(1)}, u32[]{:S(2)}, u32[]{:S(2)}) collective-permute-start(bf16[1,2,48,1536]{3,2,1,0:T(8,128)(2,1)S(1)} %dynamic-slice_bitcast_fusion.16), channel_id=1, source_target_pairs={{0,2},{1,3},{2,0},{3,1},{4,6},{5,7},{6,4},{7,5},{8,10},{9,11},{10,... | collective-permute-start | bytes 884744 | tf_op jit(solution)/shard_map/ppermute | solution.py:833
  422.9 16.2 %collective-permute-start.30 = (bf16[1,4,48,1536]{3,2,1,0:T(8,128)(2,1)S(1)}, bf16[1,4,48,1536]{3,2,1,0:T(8,128)(2,1)S(1)}, u32[]{:S(2)}, u32[]{:S(2)}) collective-permute-start(bf16[1,4,48,1536]{3,2,1,0:T(8,128)(2,1)S(1)} %dynamic-slice_bitcast_fusion.10), channel_id=1, source_target_pairs={{0,1},{1,0},{2,3},{3,2},{4,5},{5,4},{6,7},{7,6},{8,9},{9,8},{10,11... | collective-permute-start | bytes 1769480 | tf_op jit(solution)/shard_map/ppermute | solution.py:833
  431.1 30.8 %collective-permute-start.33 = (bf16[2,4,48,1024]{3,2,1,0:T(8,128)(2,1)}, bf16[2,4,48,1024]{3,2,1,0:T(8,128)(2,1)}, u32[]{:S(2)}, u32[]{:S(2)}) collective-permute-start(bf16[2,4,48,1024]{3,2,1,0:T(8,128)(2,1)} %dynamic-slice_bitcast_fusion.7), channel_id=1, source_target_pairs={{0,1},{1,0},{2,3},{3,2},{4,5},{5,4},{6,7},{7,6},{8,9},{9,8},{10,11... | collective-permute-start | bytes 2359304 | tf_op jit(solution)/shard_map/ppermute | solution.py:833
  432.7 30.8 %collective-permute-start.32 = (bf16[1,8,48,1024]{3,2,1,0:T(8,128)(2,1)}, bf16[1,8,48,1024]{3,2,1,0:T(8,128)(2,1)}, u32[]{:S(2)}, u32[]{:S(2)}) collective-permute-start(bf16[1,8,48,1024]{3,2,1,0:T(8,128)(2,1)} %dynamic-slice_bitcast_fusion.8), channel_id=1, source_target_pairs={{0,16},{8,24},{16,0},{24,8},{1,17},{9,25},{17,1},{25,9},{2,18},{10... | collective-permute-start | bytes 2359304 | tf_op jit(solution)/shard_map/ppermute | solution.py:833
  439.3 20.2 %collective-permute-start.31 = (bf16[1,2,48,1536]{3,2,1,0:T(8,128)(2,1)S(1)}, bf16[1,2,48,1536]{3,2,1,0:T(8,128)(2,1)S(1)}, u32[]{:S(2)}, u32[]{:S(2)}) collective-permute-start(bf16[1,2,48,1536]{3,2,1,0:T(8,128)(2,1)S(1)} %dynamic-slice_bitcast_fusion.17), channel_id=1, source_target_pairs={{0,2},{1,3},{2,0},{3,1},{4,6},{5,7},{6,4},{7,5},{8,10},{9,11},{10,... | collective-permute-start | bytes 884744 | tf_op jit(solution)/shard_map/ppermute | solution.py:833
  441.1 39.1 %collective-permute-start.39 = (bf16[1,1,48,1536]{3,2,1,0:T(8,128)(2,1)}, bf16[1,1,48,1536]{3,2,1,0:T(8,128)(2,1)}, u32[]{:S(2)}, u32[]{:S(2)}) collective-permute-start(bf16[1,1,48,1536]{3,2,1,0:T(8,128)(2,1)} %constant_dynamic-slice_fusion.6), channel_id=1, source_target_pairs={{0,4},{1,5},{2,6},{3,7},{4,0},{5,1},{6,2},{7,3},{8,12},{9,13},{10,... | collective-permute-start | bytes 442376 | tf_op jit(solution)/shard_map/ppermute | solution.py:833
  443.5 36.7 %collective-permute-start.36 = (bf16[1,1,48,1536]{3,2,1,0:T(8,128)(2,1)}, bf16[1,1,48,1536]{3,2,1,0:T(8,128)(2,1)}, u32[]{:S(2)}, u32[]{:S(2)}) collective-permute-start(bf16[1,1,48,1536]{3,2,1,0:T(8,128)(2,1)} %constant_dynamic-slice_fusion.8), channel_id=1, source_target_pairs={{0,4},{1,5},{2,6},{3,7},{4,0},{5,1},{6,2},{7,3},{8,12},{9,13},{10,... | collective-permute-start | bytes 442376 | tf_op jit(solution)/shard_map/ppermute | solution.py:833
  460.3 19.9 %collective-permute-start.40 = (bf16[1,1,48,1536]{3,2,1,0:T(8,128)(2,1)}, bf16[1,1,48,1536]{3,2,1,0:T(8,128)(2,1)}, u32[]{:S(2)}, u32[]{:S(2)}) collective-permute-start(bf16[1,1,48,1536]{3,2,1,0:T(8,128)(2,1)} %constant_dynamic-slice_fusion.5), channel_id=1, source_target_pairs={{0,4},{1,5},{2,6},{3,7},{4,0},{5,1},{6,2},{7,3},{8,12},{9,13},{10,... | collective-permute-start | bytes 442376 | tf_op jit(solution)/shard_map/ppermute | solution.py:833
  471.0 20.4 %all-to-all-start.6 = ((f32[32,1,896]{2,1,0:T(1,128)}), f32[32,1,896]{2,1,0:T(1,128)S(1)}, u32[]{:S(2)}, u32[]{:S(2)}) async-start(f32[32,1,896]{2,1,0:T(1,128)} %pack.1), calls=%async_computation.6 | async-start | bytes 229376 | tf_op jit(solution)/shard_map/all_to_all | solution.py:1357
  475.1 18.7 %collective-permute-start.44 = (bf16[1,4,48,1024]{3,2,1,0:T(8,128)(2,1)}, bf16[1,4,48,1024]{3,2,1,0:T(8,128)(2,1)}, u32[]{:S(2)}, u32[]{:S(2)}) collective-permute-start(bf16[1,4,48,1024]{3,2,1,0:T(8,128)(2,1)} %constant_dynamic-slice_fusion.3), channel_id=1, source_target_pairs={{0,16},{8,24},{16,0},{24,8},{1,17},{9,25},{17,1},{25,9},{2,18},{10... | collective-permute-start | bytes 1179656 | tf_op jit(solution)/shard_map/ppermute | solution.py:833
  478.7 17.9 %collective-permute-start.41 = (bf16[1,4,48,1024]{3,2,1,0:T(8,128)(2,1)}, bf16[1,4,48,1024]{3,2,1,0:T(8,128)(2,1)}, u32[]{:S(2)}, u32[]{:S(2)}) collective-permute-start(bf16[1,4,48,1024]{3,2,1,0:T(8,128)(2,1)} %dynamic-slice_bitcast_fusion.12), channel_id=1, source_target_pairs={{0,1},{1,0},{2,3},{3,2},{4,5},{5,4},{6,7},{7,6},{8,9},{9,8},{10,11... | collective-permute-start | bytes 1179656 | tf_op jit(solution)/shard_map/ppermute | solution.py:833
  495.1 7.9 %collective-permute-start.45 = (bf16[1,2,48,1024]{3,2,1,0:T(8,128)(2,1)S(1)}, bf16[1,2,48,1024]{3,2,1,0:T(8,128)(2,1)S(1)}, u32[]{:S(2)}, u32[]{:S(2)}) collective-permute-start(bf16[1,2,48,1024]{3,2,1,0:T(8,128)(2,1)S(1)} %dynamic-slice_bitcast_fusion.18), channel_id=1, source_target_pairs={{0,2},{1,3},{2,0},{3,1},{4,6},{5,7},{6,4},{7,5},{8,10},{9,11},{10,... | collective-permute-start | bytes 589832 | tf_op jit(solution)/shard_map/ppermute | solution.py:833
  497.8 9.0 %collective-permute-start.42 = (bf16[1,2,48,1024]{3,2,1,0:T(8,128)(2,1)S(1)}, bf16[1,2,48,1024]{3,2,1,0:T(8,128)(2,1)S(1)}, u32[]{:S(2)}, u32[]{:S(2)}) collective-permute-start(bf16[1,2,48,1024]{3,2,1,0:T(8,128)(2,1)S(1)} %dynamic-slice_bitcast_fusion.19), channel_id=1, source_target_pairs={{0,2},{1,3},{2,0},{3,1},{4,6},{5,7},{6,4},{7,5},{8,10},{9,11},{10,... | collective-permute-start | bytes 589832 | tf_op jit(solution)/shard_map/ppermute | solution.py:833
  503.0 8.2 %collective-permute-start.46 = (bf16[1,1,48,1024]{3,2,1,0:T(8,128)(2,1)S(1)}, bf16[1,1,48,1024]{3,2,1,0:T(8,128)(2,1)S(1)}, u32[]{:S(2)}, u32[]{:S(2)}) collective-permute-start(bf16[1,1,48,1024]{3,2,1,0:T(8,128)(2,1)S(1)} %constant_dynamic-slice_fusion.2), channel_id=1, source_target_pairs={{0,4},{1,5},{2,6},{3,7},{4,0},{5,1},{6,2},{7,3},{8,12},{9,13},{10,... | collective-permute-start | bytes 294920 | tf_op jit(solution)/shard_map/ppermute | solution.py:833
  506.9 7.4 %collective-permute-start.43 = (bf16[1,1,48,1024]{3,2,1,0:T(8,128)(2,1)S(1)}, bf16[1,1,48,1024]{3,2,1,0:T(8,128)(2,1)S(1)}, u32[]{:S(2)}, u32[]{:S(2)}) collective-permute-start(bf16[1,1,48,1024]{3,2,1,0:T(8,128)(2,1)S(1)} %constant_dynamic-slice_fusion.4), channel_id=1, source_target_pairs={{0,4},{1,5},{2,6},{3,7},{4,0},{5,1},{6,2},{7,3},{8,12},{9,13},{10,... | collective-permute-start | bytes 294920 | tf_op jit(solution)/shard_map/ppermute | solution.py:833
  (69 other events, 646.9 us)
